TPU v7x, 512 devices: a whole 4x4x16 slice. The times are simulated.
512 devices in a mesh: shard: 128 (over z, x, core), tensor: 4 (over y).
Axes of the slice: x: 4, y: 4, z: 16, core: 2. Of those that a mesh axis runs over, the one named last changes fastest.
Arguments:
- grads: bfloat16 [128, 4, 1536, 1024], P('shard', None, None, 'tensor'), may hold values from -240 to 240
- master: float32 [1536, 1024], P('shard', 'tensor'), may hold values from -3 to 3
- moment1: float32 [1536, 1024], P('shard', 'tensor'), may hold values from -3 to 3
- moment2: float32 [1536, 1024], P('shard', 'tensor'), may hold values from 0.25 to 1
- ema: float32 [1536, 1024], P('shard', 'tensor'), may hold values from -3 to 3
Outputs:
- new_master: float32 [1536, 1024], P('shard', 'tensor')
- new_moment1: float32 [1536, 1024], P('shard', 'tensor')
- new_moment2: float32 [1536, 1024], P('shard', 'tensor')
- new_ema: float32 [1536, 1024], P('shard', 'tensor')
- weights: bfloat16 [1536, 1024], P(None, 'tensor')
All inputs are finite; a program needn't handle non-finite values.
Results may differ from a plain program's by a relative error of at most 0.0004.
Values may be sent and summed in bfloat16 or wider, within the bound.
No kernel may reach another device: no remote copies, remote signals or barrier semaphores. Data moves between devices by JAX's collectives and lax.ppermute only.
A program may use at most 64 MiB of HBM per device.

v0:
```python
import jax
import jax.numpy as jnp
from jax import lax
from jax.sharding import PartitionSpec as P

STEP = 10


beta_one = 0.9
beta_two = 0.95
learn_rate = 0.02
decay_weight = 0.1
ema_keep = 0.99


def shards(grads, master, moment1, moment2, ema):
    local = grads[0]
    elements = local.shape[1] * local.shape[2] * lax.axis_size("tensor")
    summed = jnp.sum(local.astype(jnp.float32), axis=0)
    grad_part = lax.psum_scatter(summed, "shard", scatter_dimension=0, tiled=True)
    sq = lax.psum(jnp.sum(grad_part * grad_part), ("shard", "tensor"))
    scale = jnp.minimum(1.0, 1.0 / jnp.sqrt(sq / elements + 1e-06))
    clipped = scale * grad_part
    new_moment1 = beta_one * moment1 + (1.0 - beta_one) * clipped
    new_moment2 = beta_two * moment2 + (1.0 - beta_two) * clipped * clipped
    first_hat = new_moment1 / (1.0 - beta_one**STEP)
    second_hat = new_moment2 / (1.0 - beta_two**STEP)
    new_master = master - learn_rate * (
        first_hat / (jnp.sqrt(second_hat) + 1e-08) + decay_weight * master
    )
    new_ema = ema_keep * ema + (1.0 - ema_keep) * new_master
    weights = lax.all_gather(new_master.astype(jnp.bfloat16), "shard", axis=0, tiled=True)
    return (new_master, new_moment1, new_moment2, new_ema, weights)


def solution(mesh):
    return jax.shard_map(
        shards,
        mesh=mesh,
        in_specs=(
            P("shard", None, None, "tensor"),
            P("shard", "tensor"),
            P("shard", "tensor"),
            P("shard", "tensor"),
            P("shard", "tensor"),
        ),
        out_specs=(
            P("shard", "tensor"),
            P("shard", "tensor"),
            P("shard", "tensor"),
            P("shard", "tensor"),
            P(None, "tensor"),
        ),
        check_vma=False,
    )
```

profile of v0, /device:TPU:1, one launch (start us, length us, event | category | flops | bytes accessed | tf_op | source)
XLA Modules:
  0.0 570.4 jit_solution(2033311778829565577)
XLA Ops:
  0.6 2.5 convert_reduce_fusion
  3.1 0.0 copy-start.2
  3.1 0.0 copy-start.3
  3.1 0.0 copy-start.4
  3.2 262.6 %fusion = f32[16,256]{1,0:T(8,128)S(1)} fusion(f32[1536,256]{1,0:T(8,128)S(1)} %convert_reduce_fusion), kind=kCustom, calls=%all-reduce-scatter | all-reduce-scatter fusion | flops 524289 | bytes 1591296
  265.8 0.0 copy-start.1
  265.8 3.0 collective-permute-start
  268.9 2.6 collective-permute-start.31
  271.5 1.3 collective-permute-start.1
  272.8 1.3 collective-permute-start.10
  274.1 2.4 collective-permute-start.11
  276.5 0.0 collective-permute-done.31
  276.5 7.0 %collective-permute-start.12 = (f32[16,256]{1,0:T(8,128)S(1)}, f32[16,256]{1,0:T(8,128)S(1)}, u32[]{:S(2)}, u32[]{:S(2)}) collective-permute-start(f32[16,256]{1,0:T(8,128)S(1)} %fusion), channel_id=1, source_target_pairs={{0,52},{4,56},{8,60},{12,64},{16,68},{20,72},{24,76},{28,80},{32,8... | collective-permute-start | bytes 49160
  283.6 0.0 collective-permute-done
  283.6 5.3 collective-permute-start.13
  288.9 0.0 collective-permute-done.1
  288.9 8.9 %collective-permute-start.14 = (f32[16,256]{1,0:T(8,128)S(1)}, f32[16,256]{1,0:T(8,128)S(1)}, u32[]{:S(2)}, u32[]{:S(2)}) collective-permute-start(f32[16,256]{1,0:T(8,128)S(1)} %fusion), channel_id=1, source_target_pairs={{0,60},{4,64},{8,68},{12,72},{16,76},{20,80},{24,84},{28,88},{32,9... | collective-permute-start | bytes 49160
  297.8 0.0 collective-permute-done.10
  297.8 1.3 collective-permute-start.15
  299.1 0.0 collective-permute-done.11
  299.1 6.5 %collective-permute-start.16 = (f32[16,256]{1,0:T(8,128)S(1)}, f32[16,256]{1,0:T(8,128)S(1)}, u32[]{:S(2)}, u32[]{:S(2)}) collective-permute-start(f32[16,256]{1,0:T(8,128)S(1)} %fusion), channel_id=1, source_target_pairs={{0,68},{4,72},{8,76},{12,80},{16,84},{20,88},{24,92},{28,96},{32,1... | collective-permute-start | bytes 49160
  305.6 0.0 collective-permute-done.12
  305.6 2.8 collective-permute-start.17
  308.4 0.0 collective-permute-done.13
  308.4 4.0 collective-permute-start.18
  312.4 0.0 collective-permute-done.14
  312.4 2.9 collective-permute-start.19
  315.3 0.0 collective-permute-done.15
  315.3 3.0 collective-permute-start.2
  318.3 0.0 collective-permute-done.16
  318.3 1.4 collective-permute-start.20
  319.7 2.7 collective-permute-start.21
  322.4 1.3 collective-permute-start.22
  323.7 1.3 collective-permute-start.23
  325.0 0.0 collective-permute-done.2
  325.0 1.8 collective-permute-start.24
  326.9 0.0 collective-permute-done.20
  326.9 1.6 collective-permute-start.25
  328.5 3.2 collective-permute-start.26
  331.8 2.8 collective-permute-start.27
  334.7 0.0 collective-permute-done.23
  334.7 1.9 collective-permute-start.28
  336.6 0.0 collective-permute-done.24
  336.6 1.6 collective-permute-start.29
  338.2 2.6 collective-permute-start.3
  340.9 0.0 collective-permute-done.26
  340.9 1.8 collective-permute-start.30
  342.7 4.5 collective-permute-start.4
  347.2 1.3 collective-permute-start.5
  348.5 2.2 collective-permute-start.6
  350.8 3.0 collective-permute-start.7
  353.8 3.7 collective-permute-start.8
  357.4 0.0 collective-permute-done.4
  357.5 1.3 collective-permute-start.9
  358.8 1.3 dynamic-slice.4
  360.7 0.0 collective-permute-done.7
  360.7 0.0 collective-permute-done.8
  360.7 3.7 concatenate
  364.4 0.6 multiply_reduce_fusion
  365.0 102.4 %psum.7 = f32[]{:T(128)} all-reduce(f32[]{:T(128)} %multiply_reduce_fusion), channel_id=1, replica_groups=mesh['shard'=128,'tensor'=4] {'shard','tensor'}, use_global_device_ids=true, to_apply=%region_3.0 | all-reduce | flops 1 | bytes 8 | tf_op jit(solution)/shard_map/psum | solution.py:21
  468.1 0.6 convert_bitcast_fusion
  468.7 100.0 %all-gather = bf16[128,12,256]{2,1,0:T(8,128)(2,1)S(1)} all-gather(bf16[1,12,256]{2,1,0:T(8,128)(2,1)S(1)} %get-tuple-element.5), channel_id=1, replica_groups=mesh['shard'=128,'tensor'=4] {'shard'}, dimensions={0}, use_global_device_ids=true | all-gather | bytes 792576 | tf_op jit(solution)/shard_map/all_gather | solution.py:32
  568.7 1.1 reshape.12
  569.7 0.6 multiply_add_fusion
  (21 shorter events, 0.1 us)
Async XLA Ops:
  3.1 465.0 %copy-start.2 = (f32[12,256]{1,0:T(8,128)S(1)}, f32[12,256]{1,0:T(8,128)}, u32[]{:S(2)}) copy-start(f32[12,256]{1,0:T(8,128)} %param.6) | copy-start | bytes 36868
  3.1 464.9 %copy-start.3 = (f32[12,256]{1,0:T(8,128)S(1)}, f32[12,256]{1,0:T(8,128)}, u32[]{:S(2)}) copy-start(f32[12,256]{1,0:T(8,128)} %param.7) | copy-start | bytes 36868
  3.1 464.9 %copy-start.4 = (f32[12,256]{1,0:T(8,128)S(1)}, f32[12,256]{1,0:T(8,128)}, u32[]{:S(2)}) copy-start(f32[12,256]{1,0:T(8,128)} %param.8) | copy-start | bytes 36868
  265.8 303.9 %copy-start.1 = (f32[12,256]{1,0:T(8,128)S(1)}, f32[12,256]{1,0:T(8,128)}, u32[]{:S(2)}) copy-start(f32[12,256]{1,0:T(8,128)} %param.9) | copy-start | bytes 36868
  265.8 17.7 %collective-permute-start = (f32[16,256]{1,0:T(8,128)S(1)}, f32[16,256]{1,0:T(8,128)S(1)}, u32[]{:S(2)}, u32[]{:S(2)}) collective-permute-start(f32[16,256]{1,0:T(8,128)S(1)} %fusion), channel_id=1, source_target_pairs={{0,4},{4,8},{8,12},{12,16},{16,20},{20,24},{24,28},{28,32},{32,36}... | collective-permute-start | bytes 49160
  268.9 7.7 %collective-permute-start.31 = (f32[12,256]{1,0:T(8,128)S(1)}, f32[12,256]{1,0:T(8,128)S(1)}, u32[]{:S(2)}, u32[]{:S(2)}) collective-permute-start(f32[12,256]{1,0:T(8,128)S(1)} %slice), channel_id=1, source_target_pairs={{0,128},{4,132},{8,136},{12,140},{16,144},{20,148},{24,152},{28,15... | collective-permute-start | bytes 36872
  271.5 17.4 %collective-permute-start.1 = (f32[16,256]{1,0:T(8,128)S(1)}, f32[16,256]{1,0:T(8,128)S(1)}, u32[]{:S(2)}, u32[]{:S(2)}) collective-permute-start(f32[16,256]{1,0:T(8,128)S(1)} %fusion), channel_id=1, source_target_pairs={{0,8},{4,12},{8,16},{12,20},{16,24},{20,28},{24,32},{28,36},{32,40... | collective-permute-start | bytes 49160
  272.8 25.0 %collective-permute-start.10 = (f32[16,256]{1,0:T(8,128)S(1)}, f32[16,256]{1,0:T(8,128)S(1)}, u32[]{:S(2)}, u32[]{:S(2)}) collective-permute-start(f32[16,256]{1,0:T(8,128)S(1)} %fusion), channel_id=1, source_target_pairs={{0,44},{4,48},{8,52},{12,56},{16,60},{20,64},{24,68},{28,72},{32,7... | collective-permute-start | bytes 49160
  274.1 25.0 %collective-permute-start.11 = (f32[16,256]{1,0:T(8,128)S(1)}, f32[16,256]{1,0:T(8,128)S(1)}, u32[]{:S(2)}, u32[]{:S(2)}) collective-permute-start(f32[16,256]{1,0:T(8,128)S(1)} %fusion), channel_id=1, source_target_pairs={{0,48},{4,52},{8,56},{12,60},{16,64},{20,68},{24,72},{28,76},{32,8... | collective-permute-start | bytes 49160
  276.5 29.1 %collective-permute-start.12 = (f32[16,256]{1,0:T(8,128)S(1)}, f32[16,256]{1,0:T(8,128)S(1)}, u32[]{:S(2)}, u32[]{:S(2)}) collective-permute-start(f32[16,256]{1,0:T(8,128)S(1)} %fusion), channel_id=1, source_target_pairs={{0,52},{4,56},{8,60},{12,64},{16,68},{20,72},{24,76},{28,80},{32,8... | collective-permute-start | bytes 49160
  283.6 24.8 %collective-permute-start.13 = (f32[16,256]{1,0:T(8,128)S(1)}, f32[16,256]{1,0:T(8,128)S(1)}, u32[]{:S(2)}, u32[]{:S(2)}) collective-permute-start(f32[16,256]{1,0:T(8,128)S(1)} %fusion), channel_id=1, source_target_pairs={{0,56},{4,60},{8,64},{12,68},{16,72},{20,76},{24,80},{28,84},{32,8... | collective-permute-start | bytes 49160
  288.9 23.5 %collective-permute-start.14 = (f32[16,256]{1,0:T(8,128)S(1)}, f32[16,256]{1,0:T(8,128)S(1)}, u32[]{:S(2)}, u32[]{:S(2)}) collective-permute-start(f32[16,256]{1,0:T(8,128)S(1)} %fusion), channel_id=1, source_target_pairs={{0,60},{4,64},{8,68},{12,72},{16,76},{20,80},{24,84},{28,88},{32,9... | collective-permute-start | bytes 49160
  297.8 17.5 %collective-permute-start.15 = (f32[16,256]{1,0:T(8,128)S(1)}, f32[16,256]{1,0:T(8,128)S(1)}, u32[]{:S(2)}, u32[]{:S(2)}) collective-permute-start(f32[16,256]{1,0:T(8,128)S(1)} %fusion), channel_id=1, source_target_pairs={{0,64},{4,68},{8,72},{12,76},{16,80},{20,84},{24,88},{28,92},{32,9... | collective-permute-start | bytes 49160
  299.1 19.2 %collective-permute-start.16 = (f32[16,256]{1,0:T(8,128)S(1)}, f32[16,256]{1,0:T(8,128)S(1)}, u32[]{:S(2)}, u32[]{:S(2)}) collective-permute-start(f32[16,256]{1,0:T(8,128)S(1)} %fusion), channel_id=1, source_target_pairs={{0,68},{4,72},{8,76},{12,80},{16,84},{20,88},{24,92},{28,96},{32,1... | collective-permute-start | bytes 49160
  305.6 14.1 %collective-permute-start.17 = (f32[16,256]{1,0:T(8,128)S(1)}, f32[16,256]{1,0:T(8,128)S(1)}, u32[]{:S(2)}, u32[]{:S(2)}) collective-permute-start(f32[16,256]{1,0:T(8,128)S(1)} %fusion), channel_id=1, source_target_pairs={{0,72},{4,76},{8,80},{12,84},{16,88},{20,92},{24,96},{28,100},{32,... | collective-permute-start | bytes 49160
  308.4 14.0 %collective-permute-start.18 = (f32[16,256]{1,0:T(8,128)S(1)}, f32[16,256]{1,0:T(8,128)S(1)}, u32[]{:S(2)}, u32[]{:S(2)}) collective-permute-start(f32[16,256]{1,0:T(8,128)S(1)} %fusion), channel_id=1, source_target_pairs={{0,76},{4,80},{8,84},{12,88},{16,92},{20,96},{24,100},{28,104},{32... | collective-permute-start | bytes 49160
  312.4 11.3 %collective-permute-start.19 = (f32[16,256]{1,0:T(8,128)S(1)}, f32[16,256]{1,0:T(8,128)S(1)}, u32[]{:S(2)}, u32[]{:S(2)}) collective-permute-start(f32[16,256]{1,0:T(8,128)S(1)} %fusion), channel_id=1, source_target_pairs={{0,80},{4,84},{8,88},{12,92},{16,96},{20,100},{24,104},{28,108},{3... | collective-permute-start | bytes 49160
  315.3 9.8 %collective-permute-start.2 = (f32[16,256]{1,0:T(8,128)S(1)}, f32[16,256]{1,0:T(8,128)S(1)}, u32[]{:S(2)}, u32[]{:S(2)}) collective-permute-start(f32[16,256]{1,0:T(8,128)S(1)} %fusion), channel_id=1, source_target_pairs={{0,12},{4,16},{8,20},{12,24},{16,28},{20,32},{24,36},{28,40},{32,4... | collective-permute-start | bytes 49160
  318.3 8.5 %collective-permute-start.20 = (f32[16,256]{1,0:T(8,128)S(1)}, f32[16,256]{1,0:T(8,128)S(1)}, u32[]{:S(2)}, u32[]{:S(2)}) collective-permute-start(f32[16,256]{1,0:T(8,128)S(1)} %fusion), channel_id=1, source_target_pairs={{0,84},{4,88},{8,92},{12,96},{16,100},{20,104},{24,108},{28,112},{... | collective-permute-start | bytes 49160
  319.7 8.8 %collective-permute-start.21 = (f32[16,256]{1,0:T(8,128)S(1)}, f32[16,256]{1,0:T(8,128)S(1)}, u32[]{:S(2)}, u32[]{:S(2)}) collective-permute-start(f32[16,256]{1,0:T(8,128)S(1)} %fusion), channel_id=1, source_target_pairs={{0,88},{4,92},{8,96},{12,100},{16,104},{20,108},{24,112},{28,116},... | collective-permute-start | bytes 49160
  322.4 9.4 %collective-permute-start.22 = (f32[16,256]{1,0:T(8,128)S(1)}, f32[16,256]{1,0:T(8,128)S(1)}, u32[]{:S(2)}, u32[]{:S(2)}) collective-permute-start(f32[16,256]{1,0:T(8,128)S(1)} %fusion), channel_id=1, source_target_pairs={{0,92},{4,96},{8,100},{12,104},{16,108},{20,112},{24,116},{28,120}... | collective-permute-start | bytes 49160
  323.7 10.9 %collective-permute-start.23 = (f32[16,256]{1,0:T(8,128)S(1)}, f32[16,256]{1,0:T(8,128)S(1)}, u32[]{:S(2)}, u32[]{:S(2)}) collective-permute-start(f32[16,256]{1,0:T(8,128)S(1)} %fusion), channel_id=1, source_target_pairs={{0,96},{4,100},{8,104},{12,108},{16,112},{20,116},{24,120},{28,124... | collective-permute-start | bytes 49160
  325.0 11.5 %collective-permute-start.24 = (f32[16,256]{1,0:T(8,128)S(1)}, f32[16,256]{1,0:T(8,128)S(1)}, u32[]{:S(2)}, u32[]{:S(2)}) collective-permute-start(f32[16,256]{1,0:T(8,128)S(1)} %fusion), channel_id=1, source_target_pairs={{0,100},{4,104},{8,108},{12,112},{16,116},{20,120},{24,124},{28,12... | collective-permute-start | bytes 49160
  326.9 11.4 %collective-permute-start.25 = (f32[16,256]{1,0:T(8,128)S(1)}, f32[16,256]{1,0:T(8,128)S(1)}, u32[]{:S(2)}, u32[]{:S(2)}) collective-permute-start(f32[16,256]{1,0:T(8,128)S(1)} %fusion), channel_id=1, source_target_pairs={{0,104},{4,108},{8,112},{12,116},{16,120},{20,124},{24,128},{28,13... | collective-permute-start | bytes 49160
  328.5 12.3 %collective-permute-start.26 = (f32[16,256]{1,0:T(8,128)S(1)}, f32[16,256]{1,0:T(8,128)S(1)}, u32[]{:S(2)}, u32[]{:S(2)}) collective-permute-start(f32[16,256]{1,0:T(8,128)S(1)} %fusion), channel_id=1, source_target_pairs={{0,108},{4,112},{8,116},{12,120},{16,124},{20,128},{24,132},{28,13... | collective-permute-start | bytes 49160
  331.8 10.9 %collective-permute-start.27 = (f32[16,256]{1,0:T(8,128)S(1)}, f32[16,256]{1,0:T(8,128)S(1)}, u32[]{:S(2)}, u32[]{:S(2)}) collective-permute-start(f32[16,256]{1,0:T(8,128)S(1)} %fusion), channel_id=1, source_target_pairs={{0,112},{4,116},{8,120},{12,124},{16,128},{20,132},{24,136},{28,14... | collective-permute-start | bytes 49160
  334.7 12.6 %collective-permute-start.28 = (f32[16,256]{1,0:T(8,128)S(1)}, f32[16,256]{1,0:T(8,128)S(1)}, u32[]{:S(2)}, u32[]{:S(2)}) collective-permute-start(f32[16,256]{1,0:T(8,128)S(1)} %fusion), channel_id=1, source_target_pairs={{0,116},{4,120},{8,124},{12,128},{16,132},{20,136},{24,140},{28,14... | collective-permute-start | bytes 49160
  336.6 11.9 %collective-permute-start.29 = (f32[16,256]{1,0:T(8,128)S(1)}, f32[16,256]{1,0:T(8,128)S(1)}, u32[]{:S(2)}, u32[]{:S(2)}) collective-permute-start(f32[16,256]{1,0:T(8,128)S(1)} %fusion), channel_id=1, source_target_pairs={{0,120},{4,124},{8,128},{12,132},{16,136},{20,140},{24,144},{28,14... | collective-permute-start | bytes 49160
  338.2 12.5 %collective-permute-start.3 = (f32[16,256]{1,0:T(8,128)S(1)}, f32[16,256]{1,0:T(8,128)S(1)}, u32[]{:S(2)}, u32[]{:S(2)}) collective-permute-start(f32[16,256]{1,0:T(8,128)S(1)} %fusion), channel_id=1, source_target_pairs={{0,16},{4,20},{8,24},{12,28},{16,32},{20,36},{24,40},{28,44},{32,4... | collective-permute-start | bytes 49160
  340.9 12.9 %collective-permute-start.30 = (f32[16,256]{1,0:T(8,128)S(1)}, f32[16,256]{1,0:T(8,128)S(1)}, u32[]{:S(2)}, u32[]{:S(2)}) collective-permute-start(f32[16,256]{1,0:T(8,128)S(1)} %fusion), channel_id=1, source_target_pairs={{0,124},{4,128},{8,132},{12,136},{16,140},{20,144},{24,148},{28,15... | collective-permute-start | bytes 49160
  342.7 14.7 %collective-permute-start.4 = (f32[16,256]{1,0:T(8,128)S(1)}, f32[16,256]{1,0:T(8,128)S(1)}, u32[]{:S(2)}, u32[]{:S(2)}) collective-permute-start(f32[16,256]{1,0:T(8,128)S(1)} %fusion), channel_id=1, source_target_pairs={{0,20},{4,24},{8,28},{12,32},{16,36},{20,40},{24,44},{28,48},{32,5... | collective-permute-start | bytes 49160
  347.2 13.5 %collective-permute-start.5 = (f32[16,256]{1,0:T(8,128)S(1)}, f32[16,256]{1,0:T(8,128)S(1)}, u32[]{:S(2)}, u32[]{:S(2)}) collective-permute-start(f32[16,256]{1,0:T(8,128)S(1)} %fusion), channel_id=1, source_target_pairs={{0,24},{4,28},{8,32},{12,36},{16,40},{20,44},{24,48},{28,52},{32,5... | collective-permute-start | bytes 49160
  348.5 12.2 %collective-permute-start.6 = (f32[16,256]{1,0:T(8,128)S(1)}, f32[16,256]{1,0:T(8,128)S(1)}, u32[]{:S(2)}, u32[]{:S(2)}) collective-permute-start(f32[16,256]{1,0:T(8,128)S(1)} %fusion), channel_id=1, source_target_pairs={{0,28},{4,32},{8,36},{12,40},{16,44},{20,48},{24,52},{28,56},{32,6... | collective-permute-start | bytes 49160
  350.8 9.9 %collective-permute-start.7 = (f32[16,256]{1,0:T(8,128)S(1)}, f32[16,256]{1,0:T(8,128)S(1)}, u32[]{:S(2)}, u32[]{:S(2)}) collective-permute-start(f32[16,256]{1,0:T(8,128)S(1)} %fusion), channel_id=1, source_target_pairs={{0,32},{4,36},{8,40},{12,44},{16,48},{20,52},{24,56},{28,60},{32,6... | collective-permute-start | bytes 49160
  353.8 6.9 %collective-permute-start.8 = (f32[16,256]{1,0:T(8,128)S(1)}, f32[16,256]{1,0:T(8,128)S(1)}, u32[]{:S(2)}, u32[]{:S(2)}) collective-permute-start(f32[16,256]{1,0:T(8,128)S(1)} %fusion), channel_id=1, source_target_pairs={{0,36},{4,40},{8,44},{12,48},{16,52},{20,56},{24,60},{28,64},{32,6... | collective-permute-start | bytes 49160
  357.5 3.3 collective-permute-start.9
  468.7 101.6 %copy-start = (f32[12,256]{1,0:T(8,128)}, f32[12,256]{1,0:T(8,128)S(1)}, u32[]{:S(2)}) copy-start(f32[12,256]{1,0:T(8,128)S(1)} %get-tuple-element.6) | copy-start | bytes 36868
where the time goes:
time: 572 us; the launch traced here: 570 us
  blocking collectives  465 us (81%)
  starting transfers between devices  92.4 us (16%)
  local copies, waits for them, and re-layouts  6.01 us (1%)
    unnamed x1, blocking collectives  263 us
    psum x1, blocking collectives, shards(): sq = lax.psum(jnp.sum(grad_part * grad_part), ('shard', 'tensor'))  102 us
    all_gather x1, blocking collectives, shards(): lax.all_gather(new_master.astype(jnp.bfloat16), 'shard', axis=0, tiled=True)  100 us
    unnamed x32, starting transfers between devices  92.4 us
  transfers between devices with their start and end apart: 32, of which 0 were waited for; matrix products, arithmetic and copies ran while one was open for 0% of the time, Pallas kernels for 0%

commit v1 on v0

v1 whole, which is shorter than its diff:
```python
import jax
import jax.numpy as jnp
from jax import lax
from jax.experimental import pallas as pl
from jax.experimental.pallas import tpu as pltpu
from jax.sharding import Mesh, PartitionSpec as P

STEP = 10
BETA_ONE = 0.9
BETA_TWO = 0.95
LEARN_RATE = 0.02
DECAY_WEIGHT = 0.1
EMA_KEEP = 0.99

Z, X, C, T = 16, 4, 2, 4
ROWS, COLS = 12, 256
PR, PC = 24, 128

F32 = jnp.float32
BF16 = jnp.bfloat16


def to_piece(v):
    return jnp.concatenate([v[0:8, :PC], v[0:8, PC:], v[8:12, :PC], v[8:12, PC:]], axis=0)


def from_piece(p):
    top = jnp.concatenate([p[0:8], p[8:16]], axis=1)
    low = jnp.concatenate([p[16:20], p[20:24]], axis=1)
    return jnp.concatenate([top, low], axis=0)


def sum_kernel(g_ref, o_ref):
    for zz in range(g_ref.shape[1] // (X * C * ROWS)):
        for pair in range(X // 2):
            at = zz * X * C * ROWS + pair * 48
            v = g_ref[0, at : at + 48, :].astype(F32)
            for m in range(1, g_ref.shape[0]):
                v = v + g_ref[m, at : at + 48, :].astype(F32)
            for k in range(4):
                o_ref[k % 2, pair * 2 + k // 2, zz] = to_piece(v[k * ROWS : (k + 1) * ROWS])


def micro_sum(local):
    steps = 4
    zs = Z // steps
    return pl.pallas_call(
        sum_kernel,
        out_shape=jax.ShapeDtypeStruct((C, X, Z, PR, PC), F32),
        grid=(steps,),
        in_specs=[pl.BlockSpec((local.shape[0], zs * X * C * ROWS, COLS), lambda i: (0, i, 0))],
        out_specs=pl.BlockSpec((C, X, zs, PR, PC), lambda i: (0, 0, i, 0, 0)),
        name="micro_sum",
    )(local)


def total_kernel(p_ref, t_ref, s_ref):
    t = jnp.sum(p_ref[...], axis=0)
    t_ref[...] = from_piece(t)
    sq = t * t
    part = sq[0:8] + sq[8:16] + sq[16:24]
    s_ref[...] = jnp.broadcast_to(part[None], s_ref.shape)


def spread_kernel(p_ref, s_ref):
    s_ref[...] = jnp.broadcast_to(jnp.sum(p_ref[...], axis=0)[None], s_ref.shape)


def update_kernel(elements, sq_ref, t_ref, ma_ref, m1_ref, m2_ref, em_ref, oma, om1, om2, oem, ow):
    sq = jnp.sum(jnp.sum(sq_ref[...], axis=0))
    sq = jnp.full((1, COLS), sq, F32)
    scale = jnp.minimum(1.0, 1.0 / jnp.sqrt(sq / elements + 1e-06))
    clipped = scale * t_ref[...]
    master = ma_ref[...]
    m1 = BETA_ONE * m1_ref[...] + (1.0 - BETA_ONE) * clipped
    m2 = BETA_TWO * m2_ref[...] + (1.0 - BETA_TWO) * clipped * clipped
    first_hat = m1 / (1.0 - BETA_ONE**STEP)
    second_hat = m2 / (1.0 - BETA_TWO**STEP)
    new = master - LEARN_RATE * (
        first_hat / (jnp.sqrt(second_hat) + 1e-08) + DECAY_WEIGHT * master
    )
    oma[...] = new
    om1[...] = m1
    om2[...] = m2
    oem[...] = EMA_KEEP * em_ref[...] + (1.0 - EMA_KEEP) * new
    ow[...] = jnp.broadcast_to(to_piece(new).astype(BF16)[None], ow.shape)


def place_kernel(w_ref, o_ref):
    for zz in range(w_ref.shape[2]):
        for pair in range(X // 2):
            parts = [
                from_piece(w_ref[k % 2, pair * 2 + k // 2, zz].astype(F32)) for k in range(4)
            ]
            at = zz * X * C * ROWS + pair * 48
            o_ref[at : at + 48, :] = jnp.concatenate(parts, axis=0).astype(BF16)


def place(w):
    steps = 4
    zs = Z // steps
    return pl.pallas_call(
        place_kernel,
        out_shape=jax.ShapeDtypeStruct((C * X * Z * ROWS, COLS), BF16),
        grid=(steps,),
        in_specs=[pl.BlockSpec((C, X, zs, PR, PC), lambda i: (0, 0, i, 0, 0))],
        out_specs=pl.BlockSpec((zs * X * C * ROWS, COLS), lambda i: (i, 0)),
        name="place",
    )(w)


def exchange(v, axes):
    return lax.all_to_all(v, axes, split_axis=0, concat_axis=0, tiled=True)


def shards(grads, master, moment1, moment2, ema):
    local = grads[0]
    elements = local.shape[1] * local.shape[2] * T

    part = micro_sum(local)
    part = jnp.sum(exchange(part, "c"), axis=0)
    part = jnp.sum(exchange(part, "x"), axis=0)
    part = exchange(part, "z")
    total, sq = pl.pallas_call(
        total_kernel,
        out_shape=(
            jax.ShapeDtypeStruct((ROWS, COLS), F32),
            jax.ShapeDtypeStruct((X * C * T, 8, 128), F32),
        ),
        name="total",
    )(part)
    sq = exchange(sq, ("x", "c", "t"))
    sq = pl.pallas_call(
        spread_kernel, out_shape=jax.ShapeDtypeStruct((Z, 8, 128), F32), name="spread"
    )(sq)
    sq = exchange(sq, "z")

    state = jax.ShapeDtypeStruct((ROWS, COLS), F32)
    new_master, new_moment1, new_moment2, new_ema, w = pl.pallas_call(
        lambda *refs: update_kernel(elements, *refs),
        out_shape=(state, state, state, state, jax.ShapeDtypeStruct((Z, PR, PC), BF16)),
        name="update",
    )(sq, total, master, moment1, moment2, ema)

    w = exchange(w, "z")
    w = exchange(jnp.broadcast_to(w[None], (X,) + w.shape), "x")
    w = lax.all_gather(w, "c", axis=0, tiled=False)
    weights = place(w)
    return (new_master, new_moment1, new_moment2, new_ema, weights)


def solution(mesh):
    fine = Mesh(mesh.devices.reshape(Z, X, C, T), ("z", "x", "c", "t"))
    rows = ("z", "x", "c")
    return jax.shard_map(
        shards,
        mesh=fine,
        in_specs=(P(rows, None, None, "t"),) + (P(rows, "t"),) * 4,
        out_specs=(P(rows, "t"),) * 4 + (P(None, "t"),),
        check_vma=False,
    )
```

time: 572 us -> 129 us (0.23)
  blocking collectives: 465 us -> 115 us
  starting transfers between devices: 92.4 us -> 0 us
  Pallas kernels: 0 us -> 12.3 us
  local copies, waits for them, and re-layouts: 6.01 us -> 0.05 us
    unnamed x1 -> x0, blocking collectives: 263 us -> none
    all_to_all x0 -> x7, blocking collectives: none -> 108 us  [exchange(): return lax.all_to_all(v, axes, split_axis=0, concat_axis=0, tiled=True)]
    psum x1 -> x0, blocking collectives: 102 us -> none  [shards(): sq = lax.psum(jnp.sum(grad_part * grad_part), ('shard', 'tensor'))]
    all_gather x1, blocking collectives: 100 us -> 6.28 us  [shards(): w = lax.all_gather(w, 'c', axis=0, tiled=False)]
    unnamed x32 -> x0, starting transfers between devices: 92.4 us -> none
    pallas_call x0 -> x5, Pallas kernels: none -> 12.3 us  [the longest x1 4.1 us: micro_sum(): pl.pallas_call(sum_kernel, out_shape=jax.ShapeDtypeStruct((C, X, Z, PR, P...]
    unnamed x14 -> x0, local copies, waits for them, and re-layouts: 6.01 us -> none
  transfers between devices with their start and end apart: 32 -> 0, of which waited for: 0 -> 0; matrix products, arithmetic and copies ran while one was open for 0% -> 0% of each run, Pallas kernels for 0% -> 0%
where the time goes in v1:
time: 129 us; the launch traced here: 128 us
  blocking collectives  115 us (89%)
  Pallas kernels  12.3 us (10%)
    all_to_all x7, blocking collectives, exchange(): return lax.all_to_all(v, axes, split_axis=0, concat_axis=0, tiled=True)  108 us
    all_gather x1, blocking collectives, shards(): w = lax.all_gather(w, 'c', axis=0, tiled=False)  6.28 us
    pallas_call x1, Pallas kernels, micro_sum(): pl.pallas_call(sum_kernel, out_shape=jax.ShapeDtypeStruct((C, X, Z, PR, P...  4.1 us
    pallas_call x1, Pallas kernels, place(): pl.pallas_call(place_kernel, out_shape=jax.ShapeDtypeStruct((C * X * Z *...  3.3 us

profile of v1, /device:TPU:1, one launch (start us, length us, event | category | flops | bytes accessed | tf_op | source)
XLA Modules:
  0.0 127.9 jit_solution(5592636883719267662)
XLA Ops:
  0.6 4.1 %micro_sum.1 = f32[2,4,16,24,128]{4,3,2,1,0:T(8,128)} custom-call(bf16[4,1536,256]{2,1,0:T(8,128)(2,1)} %bitcast.2), custom_call_target="tpu_custom_call" | custom-call | tf_op jit(solution)/shard_map/micro_sum/pallas_call | solution.py:47
  4.7 12.7 %all_to_all.35 = f32[2,4,16,24,128]{4,3,2,1,0:T(8,128)S(1)} all-to-all(f32[2,4,16,24,128]{4,3,2,1,0:T(8,128)} %micro_sum.1), channel_id=1, replica_groups=mesh['z'=16,'x'=4,'c'=2,'t'=4] {'c'}, dimensions={0} | all-to-all | bytes 3145728 | tf_op jit(solution)/shard_map/all_to_all | solution.py:113
  17.4 0.2 reduce_sum.18
  17.5 14.4 %all_to_all.36 = f32[4,16,24,128]{3,2,1,0:T(8,128)S(1)} all-to-all(f32[4,16,24,128]{3,2,1,0:T(8,128)S(1)} %reduce_sum.18), channel_id=1, replica_groups=mesh['z'=16,'x'=4,'c'=2,'t'=4] {'x'}, dimensions={0} | all-to-all | bytes 1572864 | tf_op jit(solution)/shard_map/all_to_all | solution.py:113
  32.0 22.6 %all_to_all.37.p_ref = f32[16,24,128]{2,1,0:T(8,128)} all-to-all(f32[16,24,128]{2,1,0:T(8,128)S(1)} %reduce_sum.19), channel_id=1, replica_groups=mesh['z'=16,'x'=4,'c'=2,'t'=4] {'z'}, dimensions={0} | all-to-all | bytes 393216 | tf_op jit(solution)/shard_map/all_to_all | solution.py:113
  54.6 1.6 %total.1 = (f32[12,256]{1,0:T(8,128)}, f32[32,8,128]{2,1,0:T(8,128)}) custom-call(f32[16,24,128]{2,1,0:T(8,128)} %all_to_all.37.p_ref), custom_call_target="tpu_custom_call" | custom-call | tf_op jit(solution)/shard_map/total/pallas_call | solution.py:124
  56.2 18.2 %all_to_all.38.p_ref = f32[32,8,128]{2,1,0:T(8,128)} all-to-all(f32[32,8,128]{2,1,0:T(8,128)} %get-tuple-element.12), channel_id=1, replica_groups=mesh['z'=16,'x'=4,'c'=2,'t'=4] {'x','c','t'}, dimensions={0} | all-to-all | bytes 262144 | tf_op jit(solution)/shard_map/all_to_all | solution.py:113
  74.5 1.6 %spread.1 = f32[16,8,128]{2,1,0:T(8,128)} custom-call(f32[32,8,128]{2,1,0:T(8,128)} %all_to_all.38.p_ref), custom_call_target="tpu_custom_call" | custom-call | tf_op jit(solution)/shard_map/spread/pallas_call | solution.py:133
  76.0 16.0 %all_to_all.39.refs_0_ = f32[16,8,128]{2,1,0:T(8,128)} all-to-all(f32[16,8,128]{2,1,0:T(8,128)} %spread.1), channel_id=1, replica_groups=mesh['z'=16,'x'=4,'c'=2,'t'=4] {'z'}, dimensions={0} | all-to-all | bytes 131072 | tf_op jit(solution)/shard_map/all_to_all | solution.py:113
  92.1 1.7 %update.1 = (f32[12,256]{1,0:T(8,128)}, f32[12,256]{1,0:T(8,128)}, f32[12,256]{1,0:T(8,128)}, f32[12,256]{1,0:T(8,128)}, bf16[16,24,128]{2,1,0:T(8,128)(2,1)}) custom-call(f32[16,8,128]{2,1,0:T(8,128)} %all_to_all.39.refs_0_, f32[12,256]{1,0:T(8,128)} %get-tuple-element.13.refs_1_, f32[12,256]{1,0:T(8,128)} %refs_2_.1, f32[12,256]{1,0:T(8,128)} %refs_3_.1, ...), custom_call_target="tpu_custom_call" | custom-call | tf_op jit(solution)/shard_map/update/pallas_call | solution.py:139
  93.8 15.9 %all_to_all.40 = bf16[16,24,128]{2,1,0:T(8,128)(2,1)S(1)} all-to-all(bf16[16,24,128]{2,1,0:T(8,128)(2,1)} %get-tuple-element.18), channel_id=1, replica_groups=mesh['z'=16,'x'=4,'c'=2,'t'=4] {'z'}, dimensions={0} | all-to-all | bytes 196608 | tf_op jit(solution)/shard_map/all_to_all | solution.py:113
  109.6 0.1 broadcast_in_dim.2
  109.7 8.6 %all_to_all.41 = bf16[4,16,24,128]{3,2,1,0:T(8,128)(2,1)S(1)} all-to-all(bf16[4,16,24,128]{3,2,1,0:T(8,128)(2,1)S(1)} %broadcast_in_dim.2), channel_id=1, replica_groups=mesh['z'=16,'x'=4,'c'=2,'t'=4] {'x'}, dimensions={0} | all-to-all | bytes 786432 | tf_op jit(solution)/shard_map/all_to_all | solution.py:113
  118.3 6.3 %all-gather = bf16[8,16,24,128]{3,2,1,0:T(8,128)(2,1)} all-gather(bf16[4,16,24,128]{3,2,1,0:T(8,128)(2,1)S(1)} %all_to_all.41), channel_id=2, replica_groups=mesh['z'=16,'x'=4,'c'=2,'t'=4] {'c'}, dimensions={0}, use_global_device_ids=true | all-gather | bytes 1179648 | tf_op jit(solution)/shard_map/all_gather | solution.py:147
  124.6 3.3 %place.1 = bf16[1536,256]{1,0:T(8,128)(2,1)} custom-call(bf16[2,4,16,24,128]{4,3,2,1,0:T(8,128)(2,1)} %bitcast.3), custom_call_target="tpu_custom_call" | custom-call | tf_op jit(solution)/shard_map/place/pallas_call | solution.py:102
  (1 shorter events, 0.0 us)

commit v2 on v1

v2 whole, which is shorter than its diff:
```python
import jax
import jax.numpy as jnp
from jax import lax
from jax.experimental import pallas as pl
from jax.experimental.pallas import tpu as pltpu
from jax.sharding import Mesh, PartitionSpec as P

STEP = 10
BETA_ONE = 0.9
BETA_TWO = 0.95
LEARN_RATE = 0.02
DECAY_WEIGHT = 0.1
EMA_KEEP = 0.99

ZH, ZL, X, C, T = 4, 4, 4, 2, 4
ROWS, COLS = 12, 256
PR, PC = 24, 128
SET = ZH * PR

F32 = jnp.float32
BF16 = jnp.bfloat16


def to_piece(v):
    return jnp.concatenate([v[0:8, :PC], v[0:8, PC:], v[8:12, :PC], v[8:12, PC:]], axis=0)


def from_piece(p):
    top = jnp.concatenate([p[0:8], p[8:16]], axis=1)
    low = jnp.concatenate([p[16:20], p[20:24]], axis=1)
    return jnp.concatenate([top, low], axis=0)


def sum_kernel(g_ref, o_ref):
    for zl in range(ZL):
        for pair in range(X // 2):
            at = zl * X * C * ROWS + pair * 48
            v = g_ref[0, at : at + 48, :].astype(F32)
            for m in range(1, g_ref.shape[0]):
                v = v + g_ref[m, at : at + 48, :].astype(F32)
            for k in range(4):
                o_ref[k % 2, pair * 2 + k // 2, zl, 0] = to_piece(v[k * ROWS : (k + 1) * ROWS])


def micro_sum(local):
    rows = ZL * X * C * ROWS
    return pl.pallas_call(
        sum_kernel,
        out_shape=jax.ShapeDtypeStruct((C, X, ZL, ZH, PR, PC), F32),
        grid=(ZH,),
        in_specs=[pl.BlockSpec((local.shape[0], rows, COLS), lambda i: (0, i, 0))],
        out_specs=pl.BlockSpec((C, X, ZL, 1, PR, PC), lambda i: (0, 0, 0, i, 0, 0)),
        name="micro_sum",
    )(local)


def pack_kernel(p_ref, ma_ref, m1_ref, m2_ref, o_ref):
    part = jnp.sum(p_ref[...], axis=0)
    state = [to_piece(r[...]) for r in (ma_ref, m1_ref, m2_ref)]
    o_ref[...] = jnp.broadcast_to(jnp.concatenate([part] + state, axis=0)[None], o_ref.shape)


def total_kernel(p_ref, t_ref, s_ref):
    t = jnp.sum(p_ref[:, :SET, :], axis=0)
    t_ref[...] = t
    sq = t * t
    s_ref[...] = jnp.broadcast_to(jnp.sum(sq.reshape(-1, 8, PC), axis=0)[None], s_ref.shape)


def adam(scale, total, master, moment1, moment2):
    clipped = scale * total
    m1 = BETA_ONE * moment1 + (1.0 - BETA_ONE) * clipped
    m2 = BETA_TWO * moment2 + (1.0 - BETA_TWO) * clipped * clipped
    first_hat = m1 / (1.0 - BETA_ONE**STEP)
    second_hat = m2 / (1.0 - BETA_TWO**STEP)
    new = master - LEARN_RATE * (
        first_hat / (jnp.sqrt(second_hat) + 1e-08) + DECAY_WEIGHT * master
    )
    return new, m1, m2


def update_kernel(elements, sq_ref, t_ref, p_ref, ma_ref, m1_ref, m2_ref, em_ref, oma, om1, om2, oem, ow):
    sq = jnp.sum(jnp.sum(sq_ref[...], axis=0))
    sq = jnp.full((1, PC), sq, F32)
    scale = jnp.minimum(1.0, 1.0 / jnp.sqrt(sq / elements + 1e-06))
    for k in range(ZH):
        state = [p_ref[k, SET + j * PR : SET + (j + 1) * PR, :] for j in range(3)]
        new, _, _ = adam(scale, t_ref[k * PR : (k + 1) * PR, :], *state)
        ow[:, k] = jnp.broadcast_to(new.astype(BF16)[None], (ow.shape[0], PR, PC))
    at = pl.multiple_of(lax.axis_index("zh") * PR, 8)
    total = from_piece(t_ref[pl.ds(at, PR), :])
    wide = jnp.concatenate([scale, scale], axis=1)
    new, m1, m2 = adam(wide, total, ma_ref[...], m1_ref[...], m2_ref[...])
    oma[...] = new
    om1[...] = m1
    om2[...] = m2
    oem[...] = EMA_KEEP * em_ref[...] + (1.0 - EMA_KEEP) * new


def place_kernel(w_ref, o_ref):
    for zl in range(ZL):
        for pair in range(X // 2):
            parts = [
                from_piece(w_ref[k % 2, pair * 2 + k // 2, zl, 0].astype(F32)) for k in range(4)
            ]
            at = zl * X * C * ROWS + pair * 48
            o_ref[at : at + 48, :] = jnp.concatenate(parts, axis=0).astype(BF16)


def place(w):
    rows = ZL * X * C * ROWS
    return pl.pallas_call(
        place_kernel,
        out_shape=jax.ShapeDtypeStruct((ZH * rows, COLS), BF16),
        grid=(ZH,),
        in_specs=[pl.BlockSpec((C, X, ZL, 1, PR, PC), lambda i: (0, 0, 0, i, 0, 0))],
        out_specs=pl.BlockSpec((rows, COLS), lambda i: (i, 0)),
        name="place",
    )(w)


def exchange(v, axes):
    return lax.all_to_all(v, axes, split_axis=0, concat_axis=0, tiled=True)


def copies(v, n):
    return jnp.broadcast_to(v[None], (n,) + v.shape)


def shards(grads, master, moment1, moment2, ema):
    local = grads[0]
    elements = local.shape[1] * local.shape[2] * T

    part = micro_sum(local)
    part = jnp.sum(exchange(part, "c"), axis=0)
    part = jnp.sum(exchange(part, "x"), axis=0)
    part = exchange(part.reshape(ZL, SET, PC), "zl")
    both = pl.pallas_call(
        pack_kernel,
        out_shape=jax.ShapeDtypeStruct((ZH, SET + 3 * PR, PC), F32),
        name="pack",
    )(part, master, moment1, moment2)
    both = exchange(both, "zh")
    total, sq = pl.pallas_call(
        total_kernel,
        out_shape=(
            jax.ShapeDtypeStruct((SET, PC), F32),
            jax.ShapeDtypeStruct((X * C * T, 8, PC), F32),
        ),
        name="total",
    )(both)
    sq = jnp.sum(exchange(sq, ("x", "c", "t")), axis=0)
    sq = exchange(copies(sq, ZL), "zl")

    state = jax.ShapeDtypeStruct((ROWS, COLS), F32)
    new_master, new_moment1, new_moment2, new_ema, w = pl.pallas_call(
        lambda *refs: update_kernel(elements, *refs),
        out_shape=(state, state, state, state, jax.ShapeDtypeStruct((ZL, ZH, PR, PC), BF16)),
        name="update",
    )(sq, total, both, master, moment1, moment2, ema)

    w = exchange(w, "zl")
    w = exchange(copies(w, X), "x")
    w = lax.all_gather(w, "c", axis=0, tiled=False)
    weights = place(w)
    return (new_master, new_moment1, new_moment2, new_ema, weights)


def solution(mesh):
    fine = Mesh(mesh.devices.reshape(ZH, ZL, X, C, T), ("zh", "zl", "x", "c", "t"))
    rows = ("zh", "zl", "x", "c")
    return jax.shard_map(
        shards,
        mesh=fine,
        in_specs=(P(rows, None, None, "t"),) + (P(rows, "t"),) * 4,
        out_specs=(P(rows, "t"),) * 4 + (P(None, "t"),),
        check_vma=False,
    )
```

time: 129 us -> 129 us (level)
    all_to_all x7 -> x8, blocking collectives: 108 us -> 108 us  [exchange(): return lax.all_to_all(v, axes, split_axis=0, concat_axis=0, tiled=True)]
where the time goes in v2:
time: 129 us; the launch traced here: 128 us
  blocking collectives  114 us (88%)
  Pallas kernels  12.7 us (10%)
    all_to_all x8, blocking collectives, exchange(): return lax.all_to_all(v, axes, split_axis=0, concat_axis=0, tiled=True)  108 us
    all_gather x1, blocking collectives, shards(): w = lax.all_gather(w, 'c', axis=0, tiled=False)  6.33 us
    pallas_call x1, Pallas kernels, micro_sum(): pl.pallas_call(sum_kernel, out_shape=jax.ShapeDtypeStruct((C, X, ZL, ZH,...  4.1 us
    pallas_call x1, Pallas kernels, place(): pl.pallas_call(place_kernel, out_shape=jax.ShapeDtypeStruct((ZH * rows, C...  3.31 us

profile of v2, /device:TPU:1, one launch (start us, length us, event | category | flops | bytes accessed | tf_op | source)
XLA Modules:
  0.0 128.0 jit_solution(12854905320363880948)
XLA Ops:
  0.6 4.1 %micro_sum.1 = f32[2,4,4,4,24,128]{5,4,3,2,1,0:T(8,128)} custom-call(bf16[4,1536,256]{2,1,0:T(8,128)(2,1)} %bitcast.3), custom_call_target="tpu_custom_call" | custom-call | tf_op jit(solution)/shard_map/micro_sum/pallas_call | solution.py:47
  4.7 12.7 %all_to_all.40 = f32[2,4,4,4,24,128]{5,4,3,2,1,0:T(8,128)S(1)} all-to-all(f32[2,4,4,4,24,128]{5,4,3,2,1,0:T(8,128)} %micro_sum.1), channel_id=1, replica_groups=mesh['zh'=4,'zl'=4,'x'=4,'c'=2,'t'=4] {'c'}, dimensions={0} | all-to-all | bytes 3145728 | tf_op jit(solution)/shard_map/all_to_all | solution.py:123
  17.4 0.2 reduce_sum.27
  17.6 14.4 %all_to_all.41 = f32[4,4,4,24,128]{4,3,2,1,0:T(8,128)S(1)} all-to-all(f32[4,4,4,24,128]{4,3,2,1,0:T(8,128)S(1)} %reduce_sum.27), channel_id=1, replica_groups=mesh['zh'=4,'zl'=4,'x'=4,'c'=2,'t'=4] {'x'}, dimensions={0} | all-to-all | bytes 1572864 | tf_op jit(solution)/shard_map/all_to_all | solution.py:123
  32.1 8.8 %all_to_all.42.p_ref = f32[4,96,128]{2,1,0:T(8,128)} all-to-all(f32[4,96,128]{2,1,0:T(8,128)S(1)} %bitcast.5), channel_id=1, replica_groups=mesh['zh'=4,'zl'=4,'x'=4,'c'=2,'t'=4] {'zl'}, dimensions={0} | all-to-all | bytes 393216 | tf_op jit(solution)/shard_map/all_to_all | solution.py:123
  40.8 1.7 %pack.1 = f32[4,168,128]{2,1,0:T(8,128)} custom-call(f32[4,96,128]{2,1,0:T(8,128)} %all_to_all.42.p_ref, f32[12,256]{1,0:T(8,128)} %refs_3_.1, f32[12,256]{1,0:T(8,128)} %refs_4_.1, f32[12,256]{1,0:T(8,128)} %refs_5_.1), custom_call_target="tpu_custom_call" | custom-call | tf_op jit(solution)/shard_map/pack/pallas_call | solution.py:138
  42.5 29.6 %all_to_all.43.p_ref.refs_2_ = f32[4,168,128]{2,1,0:T(8,128)} all-to-all(f32[4,168,128]{2,1,0:T(8,128)} %pack.1), channel_id=1, replica_groups=mesh['zh'=4,'zl'=4,'x'=4,'c'=2,'t'=4] {'zh'}, dimensions={0} | all-to-all | bytes 688128 | tf_op jit(solution)/shard_map/all_to_all | solution.py:123
  72.1 1.7 %total.1 = (f32[96,128]{1,0:T(8,128)}, f32[32,8,128]{2,1,0:T(8,128)}) custom-call(f32[4,168,128]{2,1,0:T(8,128)} %all_to_all.43.p_ref.refs_2_), custom_call_target="tpu_custom_call" | custom-call | tf_op jit(solution)/shard_map/total/pallas_call | solution.py:144
  73.8 18.0 %all_to_all.44 = f32[32,8,128]{2,1,0:T(8,128)S(1)} all-to-all(f32[32,8,128]{2,1,0:T(8,128)} %get-tuple-element.12), channel_id=1, replica_groups=mesh['zh'=4,'zl'=4,'x'=4,'c'=2,'t'=4] {'x','c','t'}, dimensions={0} | all-to-all | bytes 262144 | tf_op jit(solution)/shard_map/all_to_all | solution.py:123
  91.8 7.9 %all_to_all.45.refs_0_ = f32[4,8,128]{2,1,0:T(8,128)} all-to-all(f32[4,8,128]{2,1,0:T(8,128)S(1)} %broadcast_in_dim.4), channel_id=1, replica_groups=mesh['zh'=4,'zl'=4,'x'=4,'c'=2,'t'=4] {'zl'}, dimensions={0} | all-to-all | bytes 32768 | tf_op jit(solution)/shard_map/all_to_all | solution.py:123
  99.8 1.9 %update.1 = (f32[12,256]{1,0:T(8,128)}, f32[12,256]{1,0:T(8,128)}, f32[12,256]{1,0:T(8,128)}, f32[12,256]{1,0:T(8,128)}, bf16[4,4,24,128]{3,2,1,0:T(8,128)(2,1)}) custom-call(f32[4,8,128]{2,1,0:T(8,128)} %all_to_all.45.refs_0_, f32[96,128]{1,0:T(8,128)} %get-tuple-element.13.refs_1_, f32[4,168,128]{2,1,0:T(8,128)} %all_to_all.43.p_ref.refs_2_, ...), custom_call_target="tpu_custom_call" | custom-call | tf_op jit(solution)/shard_map/update/pallas_call | solution.py:156
  101.7 8.0 %all_to_all.46 = bf16[4,4,24,128]{3,2,1,0:T(8,128)(2,1)S(1)} all-to-all(bf16[4,4,24,128]{3,2,1,0:T(8,128)(2,1)} %get-tuple-element.18), channel_id=1, replica_groups=mesh['zh'=4,'zl'=4,'x'=4,'c'=2,'t'=4] {'zl'}, dimensions={0} | all-to-all | bytes 196608 | tf_op jit(solution)/shard_map/all_to_all | solution.py:123
  109.6 0.1 broadcast_in_dim.5
  109.7 8.6 %all_to_all.47 = bf16[4,4,4,24,128]{4,3,2,1,0:T(8,128)(2,1)S(1)} all-to-all(bf16[4,4,4,24,128]{4,3,2,1,0:T(8,128)(2,1)S(1)} %broadcast_in_dim.5), channel_id=1, replica_groups=mesh['zh'=4,'zl'=4,'x'=4,'c'=2,'t'=4] {'x'}, dimensions={0} | all-to-all | bytes 786432 | tf_op jit(solution)/shard_map/all_to_all | solution.py:123
  118.3 6.3 %all-gather = bf16[8,4,4,24,128]{4,3,2,1,0:T(8,128)(2,1)} all-gather(bf16[4,4,4,24,128]{4,3,2,1,0:T(8,128)(2,1)S(1)} %all_to_all.47), channel_id=2, replica_groups=mesh['zh'=4,'zl'=4,'x'=4,'c'=2,'t'=4] {'c'}, dimensions={0}, use_global_device_ids=true | all-gather | bytes 1179648 | tf_op jit(solution)/shard_map/all_gather | solution.py:164
  124.6 3.3 %place.1 = bf16[1536,256]{1,0:T(8,128)(2,1)} custom-call(bf16[2,4,4,4,24,128]{5,4,3,2,1,0:T(8,128)(2,1)} %bitcast.4), custom_call_target="tpu_custom_call" | custom-call | tf_op jit(solution)/shard_map/place/pallas_call | solution.py:112
  (3 shorter events, 0.1 us)

commit v3 on v2

--- a/solution.py
+++ b/solution.py
@@ -15,7 +15,6 @@
 ZH, ZL, X, C, T = 4, 4, 4, 2, 4
 ROWS, COLS = 12, 256
 PR, PC = 24, 128
-SET = ZH * PR
 
 F32 = jnp.float32
 BF16 = jnp.bfloat16
@@ -31,7 +30,7 @@
     return jnp.concatenate([top, low], axis=0)
 
 
-def sum_kernel(g_ref, o_ref):
+def sum_kernel(g_ref, ma_ref, m1_ref, m2_ref, o_ref, st_ref):
     for zl in range(ZL):
         for pair in range(X // 2):
             at = zl * X * C * ROWS + pair * 48
@@ -41,30 +40,29 @@
             for k in range(4):
                 o_ref[k % 2, pair * 2 + k // 2, zl, 0] = to_piece(v[k * ROWS : (k + 1) * ROWS])
 
+    @pl.when(pl.program_id(0) == 0)
+    def _():
+        for j, r in enumerate((ma_ref, m1_ref, m2_ref)):
+            st_ref[:, j] = jnp.broadcast_to(to_piece(r[...])[None], (ZH, PR, PC))
 
-def micro_sum(local):
+
+def micro_sum(local, *state):
     rows = ZL * X * C * ROWS
     return pl.pallas_call(
         sum_kernel,
-        out_shape=jax.ShapeDtypeStruct((C, X, ZL, ZH, PR, PC), F32),
+        out_shape=(
+            jax.ShapeDtypeStruct((C, X, ZL, ZH, PR, PC), F32),
+            jax.ShapeDtypeStruct((ZH, 3, PR, PC), F32),
+        ),
         grid=(ZH,),
-        in_specs=[pl.BlockSpec((local.shape[0], rows, COLS), lambda i: (0, i, 0))],
-        out_specs=pl.BlockSpec((C, X, ZL, 1, PR, PC), lambda i: (0, 0, 0, i, 0, 0)),
+        in_specs=[pl.BlockSpec((local.shape[0], rows, COLS), lambda i: (0, i, 0))]
+        + [pl.BlockSpec((ROWS, COLS), lambda i: (0, 0))] * 3,
+        out_specs=(
+            pl.BlockSpec((C, X, ZL, 1, PR, PC), lambda i: (0, 0, 0, i, 0, 0)),
+            pl.BlockSpec((ZH, 3, PR, PC), lambda i: (0, 0, 0, 0)),
+        ),
         name="micro_sum",
-    )(local)
-
-
-def pack_kernel(p_ref, ma_ref, m1_ref, m2_ref, o_ref):
-    part = jnp.sum(p_ref[...], axis=0)
-    state = [to_piece(r[...]) for r in (ma_ref, m1_ref, m2_ref)]
-    o_ref[...] = jnp.broadcast_to(jnp.concatenate([part] + state, axis=0)[None], o_ref.shape)
-
-
-def total_kernel(p_ref, t_ref, s_ref):
-    t = jnp.sum(p_ref[:, :SET, :], axis=0)
-    t_ref[...] = t
-    sq = t * t
-    s_ref[...] = jnp.broadcast_to(jnp.sum(sq.reshape(-1, 8, PC), axis=0)[None], s_ref.shape)
+    )(local, *state)
 
 
 def adam(scale, total, master, moment1, moment2):
@@ -79,16 +77,14 @@
     return new, m1, m2
 
 
-def update_kernel(elements, sq_ref, t_ref, p_ref, ma_ref, m1_ref, m2_ref, em_ref, oma, om1, om2, oem, ow):
+def update_kernel(elements, sq_ref, t_ref, st_ref, ma_ref, m1_ref, m2_ref, em_ref, oma, om1, om2, oem, ow):
     sq = jnp.sum(jnp.sum(sq_ref[...], axis=0))
     sq = jnp.full((1, PC), sq, F32)
     scale = jnp.minimum(1.0, 1.0 / jnp.sqrt(sq / elements + 1e-06))
-    for k in range(ZH):
-        state = [p_ref[k, SET + j * PR : SET + (j + 1) * PR, :] for j in range(3)]
-        new, _, _ = adam(scale, t_ref[k * PR : (k + 1) * PR, :], *state)
-        ow[:, k] = jnp.broadcast_to(new.astype(BF16)[None], (ow.shape[0], PR, PC))
-    at = pl.multiple_of(lax.axis_index("zh") * PR, 8)
-    total = from_piece(t_ref[pl.ds(at, PR), :])
+    for zh in range(ZH):
+        new, _, _ = adam(scale, t_ref[zh], st_ref[zh, 0], st_ref[zh, 1], st_ref[zh, 2])
+        ow[:, zh] = jnp.broadcast_to(new.astype(BF16)[None], (ow.shape[0], PR, PC))
+    total = from_piece(t_ref[lax.axis_index("zh")])
     wide = jnp.concatenate([scale, scale], axis=1)
     new, m1, m2 = adam(wide, total, ma_ref[...], m1_ref[...], m2_ref[...])
     oma[...] = new
@@ -131,25 +127,15 @@
     local = grads[0]
     elements = local.shape[1] * local.shape[2] * T
 
-    part = micro_sum(local)
+    part, held = micro_sum(local, master, moment1, moment2)
+    held = exchange(held, "zh")
     part = jnp.sum(exchange(part, "c"), axis=0)
     part = jnp.sum(exchange(part, "x"), axis=0)
-    part = exchange(part.reshape(ZL, SET, PC), "zl")
-    both = pl.pallas_call(
-        pack_kernel,
-        out_shape=jax.ShapeDtypeStruct((ZH, SET + 3 * PR, PC), F32),
-        name="pack",
-    )(part, master, moment1, moment2)
-    both = exchange(both, "zh")
-    total, sq = pl.pallas_call(
-        total_kernel,
-        out_shape=(
-            jax.ShapeDtypeStruct((SET, PC), F32),
-            jax.ShapeDtypeStruct((X * C * T, 8, PC), F32),
-        ),
-        name="total",
-    )(both)
-    sq = jnp.sum(exchange(sq, ("x", "c", "t")), axis=0)
+    part, held = lax.optimization_barrier((part, held))
+    part = jnp.sum(exchange(part, "zl"), axis=0)
+    total = jnp.sum(exchange(copies(part, ZH), "zh"), axis=0)
+    sq = jnp.sum((total * total).reshape(-1, 8, PC), axis=0)
+    sq = jnp.sum(exchange(copies(sq, X * C * T), ("x", "c", "t")), axis=0)
     sq = exchange(copies(sq, ZL), "zl")
 
     state = jax.ShapeDtypeStruct((ROWS, COLS), F32)
@@ -157,7 +143,7 @@
         lambda *refs: update_kernel(elements, *refs),
         out_shape=(state, state, state, state, jax.ShapeDtypeStruct((ZL, ZH, PR, PC), BF16)),
         name="update",
-    )(sq, total, both, master, moment1, moment2, ema)
+    )(sq, total, held, master, moment1, moment2, ema)
 
     w = exchange(w, "zl")
     w = exchange(copies(w, X), "x")

time: 129 us -> 136 us (1.054)
  waiting for transfers between devices: 0 us -> 12.3 us
  blocking collectives: 114 us -> 103 us
  starting transfers between devices: 0 us -> 10.2 us
  Pallas kernels: 12.7 us -> 9.29 us
    all_to_all x0 -> x1, waiting for transfers between devices: none -> 12.3 us  [exchange(): return lax.all_to_all(v, axes, split_axis=0, concat_axis=0, tiled=True)]
    all_to_all x8, blocking collectives: 108 us -> 96.4 us  [exchange(): return lax.all_to_all(v, axes, split_axis=0, concat_axis=0, tiled=True)]
    all_to_all x0 -> x1, starting transfers between devices: none -> 10.2 us  [exchange(): return lax.all_to_all(v, axes, split_axis=0, concat_axis=0, tiled=True)]
    pallas_call x3 -> x1, Pallas kernels: 7.47 us -> 4.15 us  [micro_sum(): pl.pallas_call(sum_kernel, out_shape=(jax.ShapeDtypeStruct((C, X, ZL, ZH,...]
  transfers between devices with their start and end apart: 0 -> 1, of which waited for: 0 -> 1; matrix products, arithmetic and copies ran while one was open for 0% -> 0% of each run, Pallas kernels for 0% -> 0%
where the time goes in v3:
time: 136 us
  blocking collectives  103 us (76%)
  waiting for transfers between devices  12.3 us (9%)
  starting transfers between devices  10.2 us (7%)
  Pallas kernels  9.29 us (7%)
    all_to_all x8, blocking collectives, exchange(): return lax.all_to_all(v, axes, split_axis=0, concat_axis=0, tiled=True)  96.4 us
    all_to_all x1, waiting for transfers between devices, exchange(): return lax.all_to_all(v, axes, split_axis=0, concat_axis=0, tiled=True)  12.3 us
    all_to_all x1, starting transfers between devices, exchange(): return lax.all_to_all(v, axes, split_axis=0, concat_axis=0, tiled=True)  10.2 us
    all_gather x1, blocking collectives, shards(): w = lax.all_gather(w, 'c', axis=0, tiled=False)  6.33 us
    pallas_call x1, Pallas kernels, micro_sum(): pl.pallas_call(sum_kernel, out_shape=(jax.ShapeDtypeStruct((C, X, ZL, ZH,...  4.15 us
    pallas_call x1, Pallas kernels, place(): pl.pallas_call(place_kernel, out_shape=jax.ShapeDtypeStruct((ZH * rows, C...  3.31 us
  transfers between devices with their start and end apart: 1, of which 1 were waited for; matrix products, arithmetic and copies ran while one was open for 0% of the time, Pallas kernels for 0%

profile of v3, /device:TPU:1, one launch (start us, length us, event | category | flops | bytes accessed | tf_op | source)
XLA Modules:
  0.0 135.6 jit_solution(7094006109375724865)
XLA Ops:
  0.6 4.1 %micro_sum.1 = (f32[2,4,4,4,24,128]{5,4,3,2,1,0:T(8,128)}, f32[4,3,24,128]{3,2,1,0:T(8,128)}) custom-call(bf16[4,1536,256]{2,1,0:T(8,128)(2,1)} %bitcast.3, f32[12,256]{1,0:T(8,128)} %refs_3_.1, f32[12,256]{1,0:T(8,128)} %refs_4_.1, f32[12,256]{1,0:T(8,128)} %refs_5_.1), custom_call_target="tpu_custom_call" | custom-call | tf_op jit(solution)/shard_map/micro_sum/pallas_call | solution.py:51
  4.8 12.7 %all_to_all.45 = f32[2,4,4,4,24,128]{5,4,3,2,1,0:T(8,128)S(1)} all-to-all(f32[2,4,4,4,24,128]{5,4,3,2,1,0:T(8,128)} %get-tuple-element.14), channel_id=1, replica_groups=mesh['zh'=4,'zl'=4,'x'=4,'c'=2,'t'=4] {'c'}, dimensions={0} | all-to-all | bytes 3145728 | tf_op jit(solution)/shard_map/all_to_all | solution.py:119
  17.4 0.2 reduce_sum.54
  17.6 14.4 %all_to_all.46 = f32[4,4,4,24,128]{4,3,2,1,0:T(8,128)S(1)} all-to-all(f32[4,4,4,24,128]{4,3,2,1,0:T(8,128)S(1)} %reduce_sum.54), channel_id=1, replica_groups=mesh['zh'=4,'zl'=4,'x'=4,'c'=2,'t'=4] {'x'}, dimensions={0} | all-to-all | bytes 1572864 | tf_op jit(solution)/shard_map/all_to_all | solution.py:119
  32.1 10.2 %all-to-all-start.2 = ((f32[4,3,24,128]{3,2,1,0:T(8,128)}), f32[4,3,24,128]{3,2,1,0:T(8,128)S(1)}, u32[]{:S(2)}, u32[]{:S(2)}) async-start(f32[4,3,24,128]{3,2,1,0:T(8,128)} %get-tuple-element.15), calls=%async_computation.2 | async-start | bytes 294912 | tf_op jit(solution)/shard_map/all_to_all | solution.py:119
  42.3 12.3 %all-to-all-done.2.refs_2_ = f32[4,3,24,128]{3,2,1,0:T(8,128)S(1)} async-done(((f32[4,3,24,128]{3,2,1,0:T(8,128)}), f32[4,3,24,128]{3,2,1,0:T(8,128)S(1)}, u32[]{:S(2)}, u32[]{:S(2)}) %all-to-all-start.2) | async-done | bytes 147488 | tf_op jit(solution)/shard_map/all_to_all | solution.py:119
  54.6 0.0 copy-start.1
  54.7 8.8 %all_to_all.47 = f32[4,4,24,128]{3,2,1,0:T(8,128)S(1)} all-to-all(f32[4,4,24,128]{3,2,1,0:T(8,128)S(1)} %reduce_sum.55), channel_id=1, replica_groups=mesh['zh'=4,'zl'=4,'x'=4,'c'=2,'t'=4] {'zl'}, dimensions={0} | all-to-all | bytes 393216 | tf_op jit(solution)/shard_map/all_to_all | solution.py:119
  63.5 16.6 %all_to_all.48 = f32[4,4,24,128]{3,2,1,0:T(8,128)S(1)} all-to-all(f32[4,4,24,128]{3,2,1,0:T(8,128)S(1)} %broadcast_in_dim.8), channel_id=1, replica_groups=mesh['zh'=4,'zl'=4,'x'=4,'c'=2,'t'=4] {'zh'}, dimensions={0} | all-to-all | bytes 393216 | tf_op jit(solution)/shard_map/all_to_all | solution.py:119
  80.2 0.0 copy-start
  80.3 19.3 %all_to_all.49 = f32[32,8,128]{2,1,0:T(8,128)S(1)} all-to-all(f32[32,8,128]{2,1,0:T(8,128)S(1)} %broadcast_in_dim.9), channel_id=1, replica_groups=mesh['zh'=4,'zl'=4,'x'=4,'c'=2,'t'=4] {'x','c','t'}, dimensions={0} | all-to-all | bytes 262144 | tf_op jit(solution)/shard_map/all_to_all | solution.py:119
  99.6 7.9 %all_to_all.50.refs_0_ = f32[4,8,128]{2,1,0:T(8,128)} all-to-all(f32[4,8,128]{2,1,0:T(8,128)S(1)} %broadcast_in_dim.10), channel_id=1, replica_groups=mesh['zh'=4,'zl'=4,'x'=4,'c'=2,'t'=4] {'zl'}, dimensions={0} | all-to-all | bytes 32768 | tf_op jit(solution)/shard_map/all_to_all | solution.py:119
  107.5 0.0 copy-done.1
  107.5 0.0 copy-done
  107.5 1.8 %update.1 = (f32[12,256]{1,0:T(8,128)}, f32[12,256]{1,0:T(8,128)}, f32[12,256]{1,0:T(8,128)}, f32[12,256]{1,0:T(8,128)}, bf16[4,4,24,128]{3,2,1,0:T(8,128)(2,1)}) custom-call(f32[4,8,128]{2,1,0:T(8,128)} %all_to_all.50.refs_0_, f32[4,24,128]{2,1,0:T(8,128)} %copy-done, f32[4,3,24,128]{3,2,1,0:T(8,128)} %copy-done.1, f32[12,256]{1,0:T(8,128)} %refs_3_.1, ...), custom_call_target="tpu_custom_call" | custom-call | tf_op jit(solution)/shard_map/update/pallas_call | solution.py:142
  109.4 8.0 %all_to_all.51 = bf16[4,4,24,128]{3,2,1,0:T(8,128)(2,1)S(1)} all-to-all(bf16[4,4,24,128]{3,2,1,0:T(8,128)(2,1)} %get-tuple-element.22), channel_id=1, replica_groups=mesh['zh'=4,'zl'=4,'x'=4,'c'=2,'t'=4] {'zl'}, dimensions={0} | all-to-all | bytes 196608 | tf_op jit(solution)/shard_map/all_to_all | solution.py:119
  117.3 0.1 broadcast_in_dim.11
  117.4 8.6 %all_to_all.52 = bf16[4,4,4,24,128]{4,3,2,1,0:T(8,128)(2,1)S(1)} all-to-all(bf16[4,4,4,24,128]{4,3,2,1,0:T(8,128)(2,1)S(1)} %broadcast_in_dim.11), channel_id=1, replica_groups=mesh['zh'=4,'zl'=4,'x'=4,'c'=2,'t'=4] {'x'}, dimensions={0} | all-to-all | bytes 786432 | tf_op jit(solution)/shard_map/all_to_all | solution.py:119
  126.0 6.3 %all-gather = bf16[8,4,4,24,128]{4,3,2,1,0:T(8,128)(2,1)} all-gather(bf16[4,4,4,24,128]{4,3,2,1,0:T(8,128)(2,1)S(1)} %all_to_all.52), channel_id=2, replica_groups=mesh['zh'=4,'zl'=4,'x'=4,'c'=2,'t'=4] {'c'}, dimensions={0}, use_global_device_ids=true | all-gather | bytes 1179648 | tf_op jit(solution)/shard_map/all_gather | solution.py:150
  132.3 3.3 %place.1 = bf16[1536,256]{1,0:T(8,128)(2,1)} custom-call(bf16[2,4,4,4,24,128]{5,4,3,2,1,0:T(8,128)(2,1)} %bitcast.4), custom_call_target="tpu_custom_call" | custom-call | tf_op jit(solution)/shard_map/place/pallas_call | solution.py:108
  (9 shorter events, 0.2 us)
Async XLA Ops:
  32.1 22.6 %all-to-all-start.2 = ((f32[4,3,24,128]{3,2,1,0:T(8,128)}), f32[4,3,24,128]{3,2,1,0:T(8,128)S(1)}, u32[]{:S(2)}, u32[]{:S(2)}) async-start(f32[4,3,24,128]{3,2,1,0:T(8,128)} %get-tuple-element.15), calls=%async_computation.2 | async-start | bytes 294912 | tf_op jit(solution)/shard_map/all_to_all | solution.py:119
  54.6 52.9 %copy-start.1 = (f32[4,3,24,128]{3,2,1,0:T(8,128)}, f32[4,3,24,128]{3,2,1,0:T(8,128)S(1)}, u32[]{:S(2)}) copy-start(f32[4,3,24,128]{3,2,1,0:T(8,128)S(1)} %all-to-all-done.2.refs_2_) | copy-start | bytes 442372
  80.2 27.3 %copy-start = (f32[4,24,128]{2,1,0:T(8,128)}, f32[4,24,128]{2,1,0:T(8,128)S(1)}, u32[]{:S(2)}) copy-start(f32[4,24,128]{2,1,0:T(8,128)S(1)} %reduce_sum.57.refs_1_) | copy-start | bytes 147460

commit v4 on v3

v4 whole, which is shorter than its diff:
```python
import jax
import jax.numpy as jnp
from jax import lax
from jax.experimental import pallas as pl
from jax.experimental.pallas import tpu as pltpu
from jax.sharding import Mesh, PartitionSpec as P

STEP = 10
BETA_ONE = 0.9
BETA_TWO = 0.95
LEARN_RATE = 0.02
DECAY_WEIGHT = 0.1
EMA_KEEP = 0.99

ZH, ZL, X, C, T = 4, 4, 4, 2, 4
ROWS, COLS = 12, 256
PR, PC = 24, 128

F32 = jnp.float32
BF16 = jnp.bfloat16


def to_piece(v):
    return jnp.concatenate([v[0:8, :PC], v[0:8, PC:], v[8:12, :PC], v[8:12, PC:]], axis=0)


def from_piece(p):
    top = jnp.concatenate([p[0:8], p[8:16]], axis=1)
    low = jnp.concatenate([p[16:20], p[20:24]], axis=1)
    return jnp.concatenate([top, low], axis=0)


def sum_kernel(g_ref, o_ref):
    for zl in range(ZL):
        for pair in range(X // 2):
            at = zl * X * C * ROWS + pair * 48
            v = g_ref[0, at : at + 48, :].astype(F32)
            for m in range(1, g_ref.shape[0]):
                v = v + g_ref[m, at : at + 48, :].astype(F32)
            for k in range(4):
                o_ref[k % 2, pair * 2 + k // 2, zl, 0] = to_piece(v[k * ROWS : (k + 1) * ROWS])


def micro_sum(local):
    rows = ZL * X * C * ROWS
    return pl.pallas_call(
        sum_kernel,
        out_shape=jax.ShapeDtypeStruct((C, X, ZL, ZH, PR, PC), F32),
        grid=(ZH,),
        in_specs=[pl.BlockSpec((local.shape[0], rows, COLS), lambda i: (0, i, 0))],
        out_specs=pl.BlockSpec((C, X, ZL, 1, PR, PC), lambda i: (0, 0, 0, i, 0, 0)),
        name="micro_sum",
    )(local)


def adam(scale, total, master, moment1, moment2):
    clipped = scale * total
    m1 = BETA_ONE * moment1 + (1.0 - BETA_ONE) * clipped
    m2 = BETA_TWO * moment2 + (1.0 - BETA_TWO) * clipped * clipped
    first_hat = m1 / (1.0 - BETA_ONE**STEP)
    second_hat = m2 / (1.0 - BETA_TWO**STEP)
    new = master - LEARN_RATE * (
        first_hat / (jnp.sqrt(second_hat) + 1e-08) + DECAY_WEIGHT * master
    )
    return new, m1, m2


def update_kernel(elements, sq_ref, t_ref, ma_ref, m1_ref, m2_ref, em_ref, oma, om1, om2, oem, ow):
    sq = jnp.sum(jnp.sum(sq_ref[...], axis=0))
    sq = jnp.full((1, COLS), sq, F32)
    scale = jnp.minimum(1.0, 1.0 / jnp.sqrt(sq / elements + 1e-06))
    total = from_piece(t_ref[lax.axis_index("zh")])
    new, m1, m2 = adam(scale, total, ma_ref[...], m1_ref[...], m2_ref[...])
    oma[...] = new
    om1[...] = m1
    om2[...] = m2
    oem[...] = EMA_KEEP * em_ref[...] + (1.0 - EMA_KEEP) * new
    ow[...] = jnp.broadcast_to(to_piece(new).astype(BF16)[None, None], ow.shape)


def place_kernel(w_ref, o_ref):
    for zl in range(ZL):
        for pair in range(X // 2):
            parts = [
                from_piece(w_ref[k % 2, pair * 2 + k // 2, 0, zl].astype(F32)) for k in range(4)
            ]
            at = zl * X * C * ROWS + pair * 48
            o_ref[at : at + 48, :] = jnp.concatenate(parts, axis=0).astype(BF16)


def place(w):
    rows = ZL * X * C * ROWS
    return pl.pallas_call(
        place_kernel,
        out_shape=jax.ShapeDtypeStruct((ZH * rows, COLS), BF16),
        grid=(ZH,),
        in_specs=[pl.BlockSpec((C, X, 1, ZL, PR, PC), lambda i: (0, 0, i, 0, 0, 0))],
        out_specs=pl.BlockSpec((rows, COLS), lambda i: (i, 0)),
        name="place",
    )(w)


def exchange(v, axes):
    return lax.all_to_all(v, axes, split_axis=0, concat_axis=0, tiled=True)


def copies(v, n):
    return jnp.broadcast_to(v[None], (n,) + v.shape)


def shards(grads, master, moment1, moment2, ema):
    local = grads[0]
    elements = local.shape[1] * local.shape[2] * T

    part = micro_sum(local)
    part = jnp.sum(exchange(part, "c"), axis=0)
    part = jnp.sum(exchange(part, "x"), axis=0)
    part = jnp.sum(exchange(part, "zl"), axis=0)
    total = jnp.sum(exchange(copies(part, ZH), "zh"), axis=0)
    sq = jnp.sum((total * total).reshape(-1, 8, PC), axis=0)
    sq = jnp.sum(exchange(copies(sq, X * C * T), ("x", "c", "t")), axis=0)
    sq = exchange(copies(sq, ZL), "zl")

    state = jax.ShapeDtypeStruct((ROWS, COLS), F32)
    new_master, new_moment1, new_moment2, new_ema, w = pl.pallas_call(
        lambda *refs: update_kernel(elements, *refs),
        out_shape=(state, state, state, state, jax.ShapeDtypeStruct((ZH * ZL, 1, PR, PC), BF16)),
        name="update",
    )(sq, total, master, moment1, moment2, ema)

    w = exchange(w, ("zh", "zl")).reshape(ZH, ZL, PR, PC)
    w = exchange(copies(w, X), "x")
    w = lax.all_gather(w, "c", axis=0, tiled=False)
    weights = place(w)
    return (new_master, new_moment1, new_moment2, new_ema, weights)


def solution(mesh):
    fine = Mesh(mesh.devices.reshape(ZH, ZL, X, C, T), ("zh", "zl", "x", "c", "t"))
    rows = ("zh", "zl", "x", "c")
    return jax.shard_map(
        shards,
        mesh=fine,
        in_specs=(P(rows, None, None, "t"),) + (P(rows, "t"),) * 4,
        out_specs=(P(rows, "t"),) * 4 + (P(None, "t"),),
        check_vma=False,
    )
```

time: 136 us -> 126 us (0.926)
  waiting for transfers between devices: 12.3 us -> 0 us
  blocking collectives: 103 us -> 115 us
  starting transfers between devices: 10.2 us -> 0 us
    all_to_all x1 -> x0, waiting for transfers between devices: 12.3 us -> none  [exchange(): return lax.all_to_all(v, axes, split_axis=0, concat_axis=0, tiled=True)]
    all_to_all x8, blocking collectives: 96.4 us -> 109 us  [exchange(): return lax.all_to_all(v, axes, split_axis=0, concat_axis=0, tiled=True)]
    all_to_all x1 -> x0, starting transfers between devices: 10.2 us -> none  [exchange(): return lax.all_to_all(v, axes, split_axis=0, concat_axis=0, tiled=True)]
  transfers between devices with their start and end apart: 1 -> 0, of which waited for: 1 -> 0; matrix products, arithmetic and copies ran while one was open for 0% -> 0% of each run, Pallas kernels for 0% -> 0%
where the time goes in v4:
time: 126 us; the launch traced here: 125 us
  blocking collectives  115 us (91%)
  Pallas kernels  9.03 us (7%)
    all_to_all x8, blocking collectives, exchange(): return lax.all_to_all(v, axes, split_axis=0, concat_axis=0, tiled=True)  109 us
    all_gather x1, blocking collectives, shards(): w = lax.all_gather(w, 'c', axis=0, tiled=False)  6.49 us
    pallas_call x1, Pallas kernels, micro_sum(): pl.pallas_call(sum_kernel, out_shape=jax.ShapeDtypeStruct((C, X, ZL, ZH,...  4.1 us
    pallas_call x1, Pallas kernels, place(): pl.pallas_call(place_kernel, out_shape=jax.ShapeDtypeStruct((ZH * rows, C...  3.3 us

profile of v4, /device:TPU:1, one launch (start us, length us, event | category | flops | bytes accessed | tf_op | source)
XLA Modules:
  0.0 125.3 jit_solution(16948097940173329415)
XLA Ops:
  0.6 4.1 %micro_sum.1 = f32[2,4,4,4,24,128]{5,4,3,2,1,0:T(8,128)} custom-call(bf16[4,1536,256]{2,1,0:T(8,128)(2,1)} %bitcast.4), custom_call_target="tpu_custom_call" | custom-call | tf_op jit(solution)/shard_map/micro_sum/pallas_call | solution.py:46
  4.7 12.7 %all_to_all.40 = f32[2,4,4,4,24,128]{5,4,3,2,1,0:T(8,128)S(1)} all-to-all(f32[2,4,4,4,24,128]{5,4,3,2,1,0:T(8,128)} %micro_sum.1), channel_id=1, replica_groups=mesh['zh'=4,'zl'=4,'x'=4,'c'=2,'t'=4] {'c'}, dimensions={0} | all-to-all | bytes 3145728 | tf_op jit(solution)/shard_map/all_to_all | solution.py:104
  17.4 0.2 reduce_sum.54
  17.6 14.4 %all_to_all.41 = f32[4,4,4,24,128]{4,3,2,1,0:T(8,128)S(1)} all-to-all(f32[4,4,4,24,128]{4,3,2,1,0:T(8,128)S(1)} %reduce_sum.54), channel_id=1, replica_groups=mesh['zh'=4,'zl'=4,'x'=4,'c'=2,'t'=4] {'x'}, dimensions={0} | all-to-all | bytes 1572864 | tf_op jit(solution)/shard_map/all_to_all | solution.py:104
  32.1 8.1 %all_to_all.42 = f32[4,4,24,128]{3,2,1,0:T(8,128)S(1)} all-to-all(f32[4,4,24,128]{3,2,1,0:T(8,128)S(1)} %reduce_sum.55), channel_id=1, replica_groups=mesh['zh'=4,'zl'=4,'x'=4,'c'=2,'t'=4] {'zl'}, dimensions={0} | all-to-all | bytes 393216 | tf_op jit(solution)/shard_map/all_to_all | solution.py:104
  40.2 23.4 %all_to_all.43 = f32[4,4,24,128]{3,2,1,0:T(8,128)S(1)} all-to-all(f32[4,4,24,128]{3,2,1,0:T(8,128)S(1)} %broadcast_in_dim.10), channel_id=1, replica_groups=mesh['zh'=4,'zl'=4,'x'=4,'c'=2,'t'=4] {'zh'}, dimensions={0} | all-to-all | bytes 393216 | tf_op jit(solution)/shard_map/all_to_all | solution.py:104
  63.6 0.0 copy-start
  63.6 18.3 %all_to_all.44 = f32[32,8,128]{2,1,0:T(8,128)S(1)} all-to-all(f32[32,8,128]{2,1,0:T(8,128)S(1)} %broadcast_in_dim.11), channel_id=1, replica_groups=mesh['zh'=4,'zl'=4,'x'=4,'c'=2,'t'=4] {'x','c','t'}, dimensions={0} | all-to-all | bytes 262144 | tf_op jit(solution)/shard_map/all_to_all | solution.py:104
  82.0 8.0 %all_to_all.45.refs_0_ = f32[4,8,128]{2,1,0:T(8,128)} all-to-all(f32[4,8,128]{2,1,0:T(8,128)S(1)} %broadcast_in_dim.12), channel_id=1, replica_groups=mesh['zh'=4,'zl'=4,'x'=4,'c'=2,'t'=4] {'zl'}, dimensions={0} | all-to-all | bytes 32768 | tf_op jit(solution)/shard_map/all_to_all | solution.py:104
  89.9 0.0 copy-done
  89.9 1.6 %update.1 = (f32[12,256]{1,0:T(8,128)}, f32[12,256]{1,0:T(8,128)}, f32[12,256]{1,0:T(8,128)}, f32[12,256]{1,0:T(8,128)}, bf16[16,1,24,128]{3,2,1,0:T(8,128)(2,1)}) custom-call(f32[4,8,128]{2,1,0:T(8,128)} %all_to_all.45.refs_0_, f32[4,24,128]{2,1,0:T(8,128)} %copy-done, f32[12,256]{1,0:T(8,128)} %refs_2_.1, f32[12,256]{1,0:T(8,128)} %refs_3_.1, ...), custom_call_target="tpu_custom_call" | custom-call | tf_op jit(solution)/shard_map/update/pallas_call | solution.py:125
  91.6 15.2 %all_to_all.46 = bf16[16,1,24,128]{3,2,1,0:T(8,128)(2,1)S(1)} all-to-all(bf16[16,1,24,128]{3,2,1,0:T(8,128)(2,1)} %get-tuple-element.14), channel_id=1, replica_groups=mesh['zh'=4,'zl'=4,'x'=4,'c'=2,'t'=4] {'zh','zl'}, dimensions={0} | all-to-all | bytes 196608 | tf_op jit(solution)/shard_map/all_to_all | solution.py:104
  106.8 0.1 broadcast_in_dim.14
  106.9 8.6 %all_to_all.47 = bf16[4,4,4,24,128]{4,3,2,1,0:T(8,128)(2,1)S(1)} all-to-all(bf16[4,4,4,24,128]{4,3,2,1,0:T(8,128)(2,1)S(1)} %broadcast_in_dim.14), channel_id=1, replica_groups=mesh['zh'=4,'zl'=4,'x'=4,'c'=2,'t'=4] {'x'}, dimensions={0} | all-to-all | bytes 786432 | tf_op jit(solution)/shard_map/all_to_all | solution.py:104
  115.5 6.5 %all-gather = bf16[8,4,4,24,128]{4,3,2,1,0:T(8,128)(2,1)} all-gather(bf16[4,4,4,24,128]{4,3,2,1,0:T(8,128)(2,1)S(1)} %all_to_all.47), channel_id=2, replica_groups=mesh['zh'=4,'zl'=4,'x'=4,'c'=2,'t'=4] {'c'}, dimensions={0}, use_global_device_ids=true | all-gather | bytes 1179648 | tf_op jit(solution)/shard_map/all_gather | solution.py:133
  122.0 3.3 %place.1 = bf16[1536,256]{1,0:T(8,128)(2,1)} custom-call(bf16[2,4,4,4,24,128]{5,4,3,2,1,0:T(8,128)(2,1)} %bitcast.5), custom_call_target="tpu_custom_call" | custom-call | tf_op jit(solution)/shard_map/place/pallas_call | solution.py:93
  (9 shorter events, 0.2 us)
Async XLA Ops:
  63.6 26.4 %copy-start = (f32[4,24,128]{2,1,0:T(8,128)}, f32[4,24,128]{2,1,0:T(8,128)S(1)}, u32[]{:S(2)}) copy-start(f32[4,24,128]{2,1,0:T(8,128)S(1)} %reduce_sum.57.refs_1_) | copy-start | bytes 147460

commit v5 on v3

--- a/solution.py
+++ b/solution.py
@@ -40,10 +40,10 @@
             for k in range(4):
                 o_ref[k % 2, pair * 2 + k // 2, zl, 0] = to_piece(v[k * ROWS : (k + 1) * ROWS])
 
-    @pl.when(pl.program_id(0) == 0)
-    def _():
-        for j, r in enumerate((ma_ref, m1_ref, m2_ref)):
-            st_ref[:, j] = jnp.broadcast_to(to_piece(r[...])[None], (ZH, PR, PC))
+    mine = lax.axis_index("zh") == pl.program_id(0)
+    for j, r in enumerate((ma_ref, m1_ref, m2_ref)):
+        piece = jnp.where(mine, to_piece(r[...]), 0.0)
+        st_ref[:, 0, j] = jnp.broadcast_to(piece[None], (ZH, PR, PC))
 
 
 def micro_sum(local, *state):
@@ -52,14 +52,14 @@
         sum_kernel,
         out_shape=(
             jax.ShapeDtypeStruct((C, X, ZL, ZH, PR, PC), F32),
-            jax.ShapeDtypeStruct((ZH, 3, PR, PC), F32),
+            jax.ShapeDtypeStruct((ZH, ZH, 3, PR, PC), F32),
         ),
         grid=(ZH,),
         in_specs=[pl.BlockSpec((local.shape[0], rows, COLS), lambda i: (0, i, 0))]
         + [pl.BlockSpec((ROWS, COLS), lambda i: (0, 0))] * 3,
         out_specs=(
             pl.BlockSpec((C, X, ZL, 1, PR, PC), lambda i: (0, 0, 0, i, 0, 0)),
-            pl.BlockSpec((ZH, 3, PR, PC), lambda i: (0, 0, 0, 0)),
+            pl.BlockSpec((ZH, 1, 3, PR, PC), lambda i: (0, i, 0, 0, 0)),
         ),
         name="micro_sum",
     )(local, *state)
@@ -127,11 +127,10 @@
     local = grads[0]
     elements = local.shape[1] * local.shape[2] * T
 
-    part, held = micro_sum(local, master, moment1, moment2)
-    held = exchange(held, "zh")
+    part, slots = micro_sum(local, master, moment1, moment2)
+    held = lax.psum_scatter(slots, "zh", scatter_dimension=0, tiled=False)
     part = jnp.sum(exchange(part, "c"), axis=0)
     part = jnp.sum(exchange(part, "x"), axis=0)
-    part, held = lax.optimization_barrier((part, held))
     part = jnp.sum(exchange(part, "zl"), axis=0)
     total = jnp.sum(exchange(copies(part, ZH), "zh"), axis=0)
     sq = jnp.sum((total * total).reshape(-1, 8, PC), axis=0)

time: 136 us -> 142 us (1.044)
  between operations: 0.69 us -> 14.1 us
  blocking collectives: 103 us -> 99 us
  starting transfers between devices: 10.2 us -> 6.66 us
  waiting for transfers between devices: 12.3 us -> 9.52 us
    all_to_all x1 -> x2, starting transfers between devices: 10.2 us -> 6.62 us  [exchange(): return lax.all_to_all(v, axes, split_axis=0, concat_axis=0, tiled=True)]
    all_to_all x1 -> x2, waiting for transfers between devices: 12.3 us -> 8.82 us  [exchange(): return lax.all_to_all(v, axes, split_axis=0, concat_axis=0, tiled=True)]
    all_to_all x8 -> x6, blocking collectives: 96.4 us -> 93 us  [exchange(): return lax.all_to_all(v, axes, split_axis=0, concat_axis=0, tiled=True)]
  transfers between devices with their start and end apart: 1 -> 3, of which waited for: 1 -> 2; matrix products, arithmetic and copies ran while one was open for 0% -> 1% of each run, Pallas kernels for 0% -> 0%
where the time goes in v5:
time: 142 us; the launch traced here: 141 us
  blocking collectives  99 us (70%)
  between operations  14.1 us (10%)
  waiting for transfers between devices  9.52 us (7%)
  Pallas kernels  9.32 us (7%)
  starting transfers between devices  6.66 us (5%)
    all_to_all x6, blocking collectives, exchange(): return lax.all_to_all(v, axes, split_axis=0, concat_axis=0, tiled=True)  93 us
    all_to_all x2, waiting for transfers between devices, exchange(): return lax.all_to_all(v, axes, split_axis=0, concat_axis=0, tiled=True)  8.82 us
    all_to_all x2, starting transfers between devices, exchange(): return lax.all_to_all(v, axes, split_axis=0, concat_axis=0, tiled=True)  6.62 us
    all_gather x1, blocking collectives, shards(): w = lax.all_gather(w, 'c', axis=0, tiled=False)  6.05 us
    pallas_call x1, Pallas kernels, micro_sum(): pl.pallas_call(sum_kernel, out_shape=(jax.ShapeDtypeStruct((C, X, ZL, ZH,...  4.16 us
    pallas_call x1, Pallas kernels, place(): pl.pallas_call(place_kernel, out_shape=jax.ShapeDtypeStruct((ZH * rows, C...  3.31 us
  transfers between devices with their start and end apart: 3, of which 2 were waited for; matrix products, arithmetic and copies ran while one was open for 1% of the time, Pallas kernels for 0%

profile of v5, /device:TPU:1, one launch (start us, length us, event | category | flops | bytes accessed | tf_op | source)
XLA Modules:
  0.0 140.9 jit_solution(11833752837058244034)
XLA Ops:
  7.2 4.2 %micro_sum.1 = (f32[2,4,4,4,24,128]{5,4,3,2,1,0:T(8,128)}, f32[4,4,3,24,128]{4,3,2,1,0:T(8,128)}) custom-call(bf16[4,1536,256]{2,1,0:T(8,128)(2,1)} %bitcast.4, f32[12,256]{1,0:T(8,128)} %refs_3_.1, f32[12,256]{1,0:T(8,128)} %refs_4_.1, f32[12,256]{1,0:T(8,128)} %refs_5_.1), custom_call_target="tpu_custom_call" | custom-call | tf_op jit(solution)/shard_map/micro_sum/pallas_call | solution.py:51
  11.3 12.7 %all_to_all.40 = f32[2,4,4,4,24,128]{5,4,3,2,1,0:T(8,128)S(1)} all-to-all(f32[2,4,4,4,24,128]{5,4,3,2,1,0:T(8,128)} %get-tuple-element.12), channel_id=1, replica_groups=mesh['zh'=4,'zl'=4,'x'=4,'c'=2,'t'=4] {'c'}, dimensions={0} | all-to-all | bytes 3145728 | tf_op jit(solution)/shard_map/all_to_all | solution.py:119
  24.0 0.2 reduce_sum.54
  24.2 14.4 %all_to_all.41 = f32[4,4,4,24,128]{4,3,2,1,0:T(8,128)S(1)} all-to-all(f32[4,4,4,24,128]{4,3,2,1,0:T(8,128)S(1)} %reduce_sum.54), channel_id=1, replica_groups=mesh['zh'=4,'zl'=4,'x'=4,'c'=2,'t'=4] {'x'}, dimensions={0} | all-to-all | bytes 1572864 | tf_op jit(solution)/shard_map/all_to_all | solution.py:119
  38.6 0.7 reduce_sum.55
  39.3 3.4 %all-to-all-start.2 = ((f32[4,4,24,128]{3,2,1,0:T(8,128)}), f32[4,4,24,128]{3,2,1,0:T(8,128)S(1)}, u32[]{:S(2)}, u32[]{:S(2)}) async-start(f32[4,4,24,128]{3,2,1,0:T(8,128)} %reduce_sum.55), calls=%async_computation.2 | async-start | bytes 393216 | tf_op jit(solution)/shard_map/all_to_all | solution.py:119
  42.7 0.0 reduce-scatter.2.cloned.1.call-start
  42.7 0.7 reduce-scatter.2.cloned.1.call-update
  43.4 4.4 %all-to-all-done.2 = f32[4,4,24,128]{3,2,1,0:T(8,128)S(1)} async-done(((f32[4,4,24,128]{3,2,1,0:T(8,128)}), f32[4,4,24,128]{3,2,1,0:T(8,128)S(1)}, u32[]{:S(2)}, u32[]{:S(2)}) %all-to-all-start.2) | async-done | bytes 196640 | tf_op jit(solution)/shard_map/all_to_all | solution.py:119
  47.9 25.3 %all_to_all.42 = f32[4,4,24,128]{3,2,1,0:T(8,128)S(1)} all-to-all(f32[4,4,24,128]{3,2,1,0:T(8,128)S(1)} %broadcast_in_dim.8), channel_id=1, replica_groups=mesh['zh'=4,'zl'=4,'x'=4,'c'=2,'t'=4] {'zh'}, dimensions={0} | all-to-all | bytes 393216 | tf_op jit(solution)/shard_map/all_to_all | solution.py:119
  73.2 0.0 copy-start
  73.2 24.0 %all_to_all.43 = f32[32,8,128]{2,1,0:T(8,128)S(1)} all-to-all(f32[32,8,128]{2,1,0:T(8,128)S(1)} %broadcast_in_dim.9), channel_id=1, replica_groups=mesh['zh'=4,'zl'=4,'x'=4,'c'=2,'t'=4] {'x','c','t'}, dimensions={0} | all-to-all | bytes 262144 | tf_op jit(solution)/shard_map/all_to_all | solution.py:119
  97.3 0.6 broadcast_in_dim.10
  97.9 3.3 %all-to-all-start.5 = ((f32[4,8,128]{2,1,0:T(8,128)}), f32[4,8,128]{2,1,0:T(8,128)S(1)}, u32[]{:S(2)}, u32[]{:S(2)}) async-start(f32[4,8,128]{2,1,0:T(8,128)} %broadcast_in_dim.10), calls=%async_computation.5 | async-start | bytes 32768 | tf_op jit(solution)/shard_map/all_to_all | solution.py:119
  101.1 0.0 reduce-scatter.2.cloned.1.call-done
  101.2 4.4 %all-to-all-done.5.refs_0_ = f32[4,8,128]{2,1,0:T(8,128)S(1)} async-done(((f32[4,8,128]{2,1,0:T(8,128)}), f32[4,8,128]{2,1,0:T(8,128)S(1)}, u32[]{:S(2)}, u32[]{:S(2)}) %all-to-all-start.5) | async-done | bytes 16416 | tf_op jit(solution)/shard_map/all_to_all | solution.py:119
  105.6 0.0 copy-start.1
  105.6 0.0 copy-done
  105.6 0.6 copy-done.1
  106.2 1.8 %update.1 = (f32[12,256]{1,0:T(8,128)}, f32[12,256]{1,0:T(8,128)}, f32[12,256]{1,0:T(8,128)}, f32[12,256]{1,0:T(8,128)}, bf16[4,4,24,128]{3,2,1,0:T(8,128)(2,1)}) custom-call(f32[4,8,128]{2,1,0:T(8,128)} %copy-done.1, f32[4,24,128]{2,1,0:T(8,128)} %copy-done, f32[4,3,24,128]{3,2,1,0:T(8,128)} %bitcast.7, f32[12,256]{1,0:T(8,128)} %refs_3_.1, ...), custom_call_target="tpu_custom_call" | custom-call | tf_op jit(solution)/shard_map/update/pallas_call | solution.py:141
  108.0 8.0 %all_to_all.44 = bf16[4,4,24,128]{3,2,1,0:T(8,128)(2,1)S(1)} all-to-all(bf16[4,4,24,128]{3,2,1,0:T(8,128)(2,1)} %get-tuple-element.18), channel_id=1, replica_groups=mesh['zh'=4,'zl'=4,'x'=4,'c'=2,'t'=4] {'zl'}, dimensions={0} | all-to-all | bytes 196608 | tf_op jit(solution)/shard_map/all_to_all | solution.py:119
  116.0 0.1 broadcast_in_dim.11
  116.0 8.6 %all_to_all.45 = bf16[4,4,4,24,128]{4,3,2,1,0:T(8,128)(2,1)S(1)} all-to-all(bf16[4,4,4,24,128]{4,3,2,1,0:T(8,128)(2,1)S(1)} %broadcast_in_dim.11), channel_id=1, replica_groups=mesh['zh'=4,'zl'=4,'x'=4,'c'=2,'t'=4] {'x'}, dimensions={0} | all-to-all | bytes 786432 | tf_op jit(solution)/shard_map/all_to_all | solution.py:119
  124.7 6.1 %all-gather = bf16[8,4,4,24,128]{4,3,2,1,0:T(8,128)(2,1)} all-gather(bf16[4,4,4,24,128]{4,3,2,1,0:T(8,128)(2,1)S(1)} %all_to_all.45), channel_id=2, replica_groups=mesh['zh'=4,'zl'=4,'x'=4,'c'=2,'t'=4] {'c'}, dimensions={0}, use_global_device_ids=true | all-gather | bytes 1179648 | tf_op jit(solution)/shard_map/all_gather | solution.py:149
  130.7 3.3 %place.1 = bf16[1536,256]{1,0:T(8,128)(2,1)} custom-call(bf16[2,4,4,4,24,128]{5,4,3,2,1,0:T(8,128)(2,1)} %bitcast.5), custom_call_target="tpu_custom_call" | custom-call | tf_op jit(solution)/shard_map/place/pallas_call | solution.py:108
  (7 shorter events, 0.1 us)
Async XLA Ops:
  39.3 8.5 %all-to-all-start.2 = ((f32[4,4,24,128]{3,2,1,0:T(8,128)}), f32[4,4,24,128]{3,2,1,0:T(8,128)S(1)}, u32[]{:S(2)}, u32[]{:S(2)}) async-start(f32[4,4,24,128]{3,2,1,0:T(8,128)} %reduce_sum.55), calls=%async_computation.2 | async-start | bytes 393216 | tf_op jit(solution)/shard_map/all_to_all | solution.py:119
  42.7 58.5 %reduce-scatter.2.cloned.1.call-start = ((), (), s32[]{:S(2)}) async-start(), calls=%async_computation.9 | async-start | bytes 737280 | tf_op jit(solution)/shard_map/reduce_scatter | solution.py:131
  73.2 32.4 %copy-start = (f32[4,24,128]{2,1,0:T(8,128)}, f32[4,24,128]{2,1,0:T(8,128)S(1)}, u32[]{:S(2)}) copy-start(f32[4,24,128]{2,1,0:T(8,128)S(1)} %reduce_sum.57.refs_1_) | copy-start | bytes 147460
  97.9 7.7 %all-to-all-start.5 = ((f32[4,8,128]{2,1,0:T(8,128)}), f32[4,8,128]{2,1,0:T(8,128)S(1)}, u32[]{:S(2)}, u32[]{:S(2)}) async-start(f32[4,8,128]{2,1,0:T(8,128)} %broadcast_in_dim.10), calls=%async_computation.5 | async-start | bytes 32768 | tf_op jit(solution)/shard_map/all_to_all | solution.py:119
  105.6 0.6 copy-start.1
Sparse Core Ops, SparseCore 0:
  46.9 45.9 reduce-scatter.1

commit v6 on v3

v6 whole, which is shorter than its diff:
```python
import jax
import jax.numpy as jnp
from jax import lax
from jax.experimental import pallas as pl
from jax.experimental.pallas import tpu as pltpu
from jax.sharding import Mesh, PartitionSpec as P

STEP = 10
BETA_ONE = 0.9
BETA_TWO = 0.95
LEARN_RATE = 0.02
DECAY_WEIGHT = 0.1
EMA_KEEP = 0.99

ZH, ZL, X, C, T = 4, 4, 4, 2, 4
ROWS, COLS = 12, 256
PR, PC = 24, 128
GROUP = C * ROWS
STEPS = 2
NZH = ZH // STEPS

F32 = jnp.float32
BF16 = jnp.bfloat16


def upper():
    return lax.broadcasted_iota(jnp.int32, (8, PC), 0) < 4


def shared_tile(core, left, right):
    turned = pltpu.roll(right, 4, 0)
    return jnp.where(upper(), left, turned) if core == 0 else jnp.where(upper(), turned, left)


def to_piece(core, v):
    zero = [v[0:8, :PC], v[0:8, PC:], v[8:12, :PC], v[8:12, PC:]]
    one = [v[4:12, :PC], v[4:12, PC:], v[0:4, PC:], v[0:4, :PC]]
    return jnp.where(core == 0, jnp.concatenate(zero, axis=0), jnp.concatenate(one, axis=0))


def from_piece(core, p):
    full = jnp.concatenate([p[0:8], p[8:16]], axis=1)
    zero = jnp.concatenate([full, jnp.concatenate([p[16:20], p[20:24]], axis=1)], axis=0)
    one = jnp.concatenate([jnp.concatenate([p[20:24], p[16:20]], axis=1), full], axis=0)
    return jnp.where(core == 0, zero, one)


def half_body(core, g_ref, o_ref):
    me = lax.axis_index("x")
    for zh in range(NZH):
        for zl in range(ZL):
            for x in range(X):
                at = ((zh * ZL + zl) * X + x) * GROUP + 8 * core
                v = g_ref[0, at : at + 16, :].astype(F32)
                for m in range(1, g_ref.shape[0]):
                    v = v + g_ref[m, at : at + 16, :].astype(F32)
                own, both = (v[0:8], v[8:16]) if core == 0 else (v[8:16], v[0:8])
                o = o_ref.at[lax.rem(x + X - me, X), zl, zh]
                o[0:8] = own[:, :PC]
                o[8:16] = own[:, PC:]
                o[16:24] = shared_tile(core, both[:, :PC], both[:, PC:])


def half_pieces(core, g_ref, o_ref):
    for k in range(C):
        pl.when(core == k)(lambda k=k: half_body(k, g_ref, o_ref))


def other_kernel(g_ref, ma_ref, m1_ref, m2_ref, o_ref, st_ref):
    core = lax.axis_index("c")
    half_pieces(1 - core, g_ref, o_ref)

    @pl.when(pl.program_id(0) == 0)
    def _():
        for j, r in enumerate((ma_ref, m1_ref, m2_ref)):
            st_ref[:, j] = jnp.broadcast_to(to_piece(core, r[...])[None], (ZH, PR, PC))


def own_kernel(g_ref, o_ref):
    half_pieces(lax.axis_index("c"), g_ref, o_ref)


def half_specs(local):
    rows = NZH * ZL * X * GROUP
    shape = jax.ShapeDtypeStruct((X, ZL, ZH, PR, PC), F32)
    source = pl.BlockSpec((local.shape[0], rows, COLS), lambda i: (0, i, 0))
    target = pl.BlockSpec((X, ZL, NZH, PR, PC), lambda i: (0, 0, i, 0, 0))
    cost = pl.CostEstimate(flops=2_000_000, bytes_accessed=4_000_000, transcendentals=0)
    return shape, source, target, cost


def other_sum(local, *state):
    shape, source, target, cost = half_specs(local)
    return pl.pallas_call(
        other_kernel,
        out_shape=(shape, jax.ShapeDtypeStruct((ZH, 3, PR, PC), F32)),
        grid=(STEPS,),
        in_specs=[source] + [pl.BlockSpec((ROWS, COLS), lambda i: (0, 0))] * 3,
        out_specs=(target, pl.BlockSpec((ZH, 3, PR, PC), lambda i: (0, 0, 0, 0))),
        cost_estimate=cost,
        name="other_sum",
    )(local, *state)


def own_sum(local):
    shape, source, target, cost = half_specs(local)
    return pl.pallas_call(
        own_kernel,
        out_shape=shape,
        grid=(STEPS,),
        in_specs=[source],
        out_specs=target,
        cost_estimate=cost,
        name="own_sum",
    )(local)


def adam(scale, total, master, moment1, moment2):
    clipped = scale * total
    m1 = BETA_ONE * moment1 + (1.0 - BETA_ONE) * clipped
    m2 = BETA_TWO * moment2 + (1.0 - BETA_TWO) * clipped * clipped
    first_hat = m1 / (1.0 - BETA_ONE**STEP)
    second_hat = m2 / (1.0 - BETA_TWO**STEP)
    new = master - LEARN_RATE * (
        first_hat / (jnp.sqrt(second_hat) + 1e-08) + DECAY_WEIGHT * master
    )
    return new, m1, m2


def update_kernel(elements, sq_ref, t_ref, st_ref, ma_ref, m1_ref, m2_ref, em_ref, oma, om1, om2, oem, ow):
    sq = jnp.sum(jnp.sum(sq_ref[...], axis=0))
    sq = jnp.full((1, PC), sq, F32)
    scale = jnp.minimum(1.0, 1.0 / jnp.sqrt(sq / elements + 1e-06))
    for zh in range(ZH):
        new, _, _ = adam(scale, t_ref[zh], st_ref[zh, 0], st_ref[zh, 1], st_ref[zh, 2])
        ow[:, zh] = jnp.broadcast_to(new.astype(BF16)[None], (ow.shape[0], PR, PC))
    total = from_piece(lax.axis_index("c"), t_ref[lax.axis_index("zh")])
    wide = jnp.concatenate([scale, scale], axis=1)
    new, m1, m2 = adam(wide, total, ma_ref[...], m1_ref[...], m2_ref[...])
    oma[...] = new
    om1[...] = m1
    om2[...] = m2
    oem[...] = EMA_KEEP * em_ref[...] + (1.0 - EMA_KEEP) * new


def place_kernel(w_ref, o_ref):
    for zh in range(NZH):
        for zl in range(ZL):
            for x in range(X):
                at = ((zh * ZL + zl) * X + x) * GROUP
                a, b = w_ref.at[0, x, zl, zh], w_ref.at[1, x, zl, zh]
                o_ref[at : at + 8, :PC] = a[0:8]
                o_ref[at : at + 8, PC:] = a[8:16]
                o_ref[at + 16 : at + 24, :PC] = b[0:8]
                o_ref[at + 16 : at + 24, PC:] = b[8:16]
                p, q = a[16:24].astype(F32), b[16:24].astype(F32)
                left = jnp.where(upper(), p, q)
                right = pltpu.roll(jnp.where(upper(), q, p), 4, 0)
                o_ref[at + 8 : at + 16, :PC] = left.astype(BF16)
                o_ref[at + 8 : at + 16, PC:] = right.astype(BF16)


def place(w):
    rows = NZH * ZL * X * GROUP
    return pl.pallas_call(
        place_kernel,
        out_shape=jax.ShapeDtypeStruct((STEPS * rows, COLS), BF16),
        grid=(STEPS,),
        in_specs=[pl.BlockSpec((C, X, ZL, NZH, PR, PC), lambda i: (0, 0, 0, i, 0, 0))],
        out_specs=pl.BlockSpec((rows, COLS), lambda i: (i, 0)),
        name="place",
    )(w)


def exchange(v, axes):
    return lax.all_to_all(v, axes, split_axis=0, concat_axis=0, tiled=True)


def copies(v, n):
    return jnp.broadcast_to(v[None], (n,) + v.shape)


def shift(v, axis, n, k):
    return lax.ppermute(v, axis, [(i, (i + k) % n) for i in range(n)])


def shards(grads, master, moment1, moment2, ema):
    local = grads[0]
    elements = local.shape[1] * local.shape[2] * T

    other, held = other_sum(local, master, moment1, moment2)
    held = exchange(held, "zh")
    part = own_sum(local) + shift(other, "c", C, 1)
    part = part[0] + sum(shift(part[k], "x", X, k) for k in range(1, X))
    part, held = lax.optimization_barrier((part, held))
    part = jnp.sum(exchange(part, "zl"), axis=0)
    total = jnp.sum(exchange(copies(part, ZH), "zh"), axis=0)
    sq = jnp.sum((total * total).reshape(-1, 8, PC), axis=0)
    sq = jnp.sum(exchange(copies(sq, X * C * T), ("x", "c", "t")), axis=0)
    sq = exchange(copies(sq, ZL), "zl")

    state = jax.ShapeDtypeStruct((ROWS, COLS), F32)
    new_master, new_moment1, new_moment2, new_ema, w = pl.pallas_call(
        lambda *refs: update_kernel(elements, *refs),
        out_shape=(state, state, state, state, jax.ShapeDtypeStruct((ZL, ZH, PR, PC), BF16)),
        name="update",
    )(sq, total, held, master, moment1, moment2, ema)

    w = exchange(w, "zl")
    w = exchange(copies(w, X), "x")
    w = lax.all_gather(w, "c", axis=0, tiled=False)
    weights = place(w)
    return (new_master, new_moment1, new_moment2, new_ema, weights)


def solution(mesh):
    fine = Mesh(mesh.devices.reshape(ZH, ZL, X, C, T), ("zh", "zl", "x", "c", "t"))
    rows = ("zh", "zl", "x", "c")
    return jax.shard_map(
        shards,
        mesh=fine,
        in_specs=(P(rows, None, None, "t"),) + (P(rows, "t"),) * 4,
        out_specs=(P(rows, "t"),) * 4 + (P(None, "t"),),
        check_vma=False,
    )
```

time: 136 us -> 130 us (0.956)
  blocking collectives: 103 us -> 76.5 us
  starting transfers between devices: 10.2 us -> 28.8 us
    all_to_all x8 -> x6, blocking collectives: 96.4 us -> 70.2 us  [exchange(): return lax.all_to_all(v, axes, split_axis=0, concat_axis=0, tiled=True)]
    ppermute x0 -> x4, starting transfers between devices: none -> 17.2 us  [shift(): return lax.ppermute(v, axis, [(i, (i + k) % n) for i in range(n)])]
    pallas_call x2 -> x3, Pallas kernels: 7.46 us -> 7.64 us  [the longest x1 2.95 us: other_sum(): pl.pallas_call(other_kernel, out_shape=(shape, jax.ShapeDtypeStruct((ZH,...]
  transfers between devices with their start and end apart: 1 -> 5, of which waited for: 1 -> 1; matrix products, arithmetic and copies ran while one was open for 0% -> 0% of each run, Pallas kernels for 0% -> 2%
where the time goes in v6:
time: 130 us; the launch traced here: 129 us
  blocking collectives  76.5 us (59%)
  starting transfers between devices  28.8 us (22%)
  waiting for transfers between devices  12.2 us (9%)
  Pallas kernels  9.48 us (7%)
  other arithmetic  1.36 us (1%)
    all_to_all x6, blocking collectives, exchange(): return lax.all_to_all(v, axes, split_axis=0, concat_axis=0, tiled=True)  70.2 us
    ppermute x4, starting transfers between devices, shift(): return lax.ppermute(v, axis, [(i, (i + k) % n) for i in range(n)])  17.2 us
    all_to_all x1, waiting for transfers between devices, exchange(): return lax.all_to_all(v, axes, split_axis=0, concat_axis=0, tiled=True)  12.2 us
    all_to_all x1, starting transfers between devices, exchange(): return lax.all_to_all(v, axes, split_axis=0, concat_axis=0, tiled=True)  11.6 us
    all_gather x1, blocking collectives, shards(): w = lax.all_gather(w, 'c', axis=0, tiled=False)  6.33 us
    pallas_call x1, Pallas kernels, other_sum(): pl.pallas_call(other_kernel, out_shape=(shape, jax.ShapeDtypeStruct((ZH,...  2.95 us
    pallas_call x1, Pallas kernels, own_sum(): pl.pallas_call(own_kernel, out_shape=shape, grid=(STEPS,), in_specs=[sour...  2.78 us
  transfers between devices with their start and end apart: 5, of which 1 were waited for; matrix products, arithmetic and copies ran while one was open for 0% of the time, Pallas kernels for 2%

profile of v6, /device:TPU:1, one launch (start us, length us, event | category | flops | bytes accessed | tf_op | source)
XLA Modules:
  0.0 129.1 jit_solution(17914204158852939903)
XLA Ops:
  0.6 3.0 %other_sum.1 = (f32[4,4,4,24,128]{4,3,2,1,0:T(8,128)}, f32[4,3,24,128]{3,2,1,0:T(8,128)}) custom-call(bf16[4,1536,256]{2,1,0:T(8,128)(2,1)} %bitcast.13, f32[12,256]{1,0:T(8,128)} %refs_3_.1, f32[12,256]{1,0:T(8,128)} %refs_4_.1, f32[12,256]{1,0:T(8,128)} %refs_5_.1), custom_call_target="tpu_custom_call" | custom-call | flops 2000000 | bytes 4000000 | tf_op jit(solution)/shard_map/other_sum/pallas_call | solution.py:94
  3.6 8.8 %collective-permute-start = (f32[4,4,4,24,128]{4,3,2,1,0:T(8,128)}, f32[4,4,4,24,128]{4,3,2,1,0:T(8,128)S(1)}, u32[]{:S(2)}, u32[]{:S(2)}) collective-permute-start(f32[4,4,4,24,128]{4,3,2,1,0:T(8,128)} %get-tuple-element.14), channel_id=1, source_target_pairs={{0,4},{4,0},{1,5},{5,1},{2,6},{6,2},{3,7},{7,3},{8,12},{12,8},{9,1... | collective-permute-start | bytes 2359304 | tf_op jit(solution)/shard_map/ppermute | solution.py:184
  12.4 2.8 %own_sum.1 = f32[4,4,4,24,128]{4,3,2,1,0:T(8,128)} custom-call(bf16[4,1536,256]{2,1,0:T(8,128)(2,1)} %bitcast.14), custom_call_target="tpu_custom_call" | custom-call | flops 2000000 | bytes 4000000 | tf_op jit(solution)/shard_map/own_sum/pallas_call | solution.py:107
  15.1 0.0 collective-permute-done
  15.1 1.2 add.12
  16.4 1.9 %collective-permute-start.1 = (f32[4,4,24,128]{3,2,1,0:T(8,128)S(1)}, f32[4,4,24,128]{3,2,1,0:T(8,128)S(1)}, u32[]{:S(2)}, u32[]{:S(2)}) collective-permute-start(f32[4,4,24,128]{3,2,1,0:T(8,128)S(1)} %get-tuple-element.25), channel_id=1, source_target_pairs={{0,8},{8,16},{16,24},{24,0},{1,9},{9,17},{17,25},{25,1},{2,10},{10... | collective-permute-start | bytes 589832 | tf_op jit(solution)/shard_map/ppermute | solution.py:184
  18.4 1.9 %collective-permute-start.2 = (f32[4,4,24,128]{3,2,1,0:T(8,128)S(1)}, f32[4,4,24,128]{3,2,1,0:T(8,128)S(1)}, u32[]{:S(2)}, u32[]{:S(2)}) collective-permute-start(f32[4,4,24,128]{3,2,1,0:T(8,128)S(1)} %get-tuple-element.23), channel_id=1, source_target_pairs={{0,16},{8,24},{16,0},{24,8},{1,17},{9,25},{17,1},{25,9},{2,18},{10... | collective-permute-start | bytes 589832 | tf_op jit(solution)/shard_map/ppermute | solution.py:184
  20.3 4.6 %collective-permute-start.3 = (f32[4,4,24,128]{3,2,1,0:T(8,128)S(1)}, f32[4,4,24,128]{3,2,1,0:T(8,128)S(1)}, u32[]{:S(2)}, u32[]{:S(2)}) collective-permute-start(f32[4,4,24,128]{3,2,1,0:T(8,128)S(1)} %get-tuple-element.24), channel_id=1, source_target_pairs={{0,24},{8,0},{16,8},{24,16},{1,25},{9,1},{17,9},{25,17},{2,26},{10... | collective-permute-start | bytes 589832 | tf_op jit(solution)/shard_map/ppermute | solution.py:184
  24.9 11.6 %all-to-all-start = ((f32[4,3,24,128]{3,2,1,0:T(8,128)}), f32[4,3,24,128]{3,2,1,0:T(8,128)S(1)}, u32[]{:S(2)}, u32[]{:S(2)}) async-start(f32[4,3,24,128]{3,2,1,0:T(8,128)} %get-tuple-element.15), calls=%async_computation | async-start | bytes 294912 | tf_op jit(solution)/shard_map/all_to_all | solution.py:176
  36.4 0.0 collective-permute-done.1
  36.4 0.0 collective-permute-done.2
  36.4 0.0 collective-permute-done.3
  36.5 12.2 %all-to-all-done.refs_2_ = f32[4,3,24,128]{3,2,1,0:T(8,128)S(1)} async-done(((f32[4,3,24,128]{3,2,1,0:T(8,128)}), f32[4,3,24,128]{3,2,1,0:T(8,128)S(1)}, u32[]{:S(2)}, u32[]{:S(2)}) %all-to-all-start) | async-done | bytes 147488 | tf_op jit(solution)/shard_map/all_to_all | solution.py:176
  48.7 0.0 copy-start.1
  48.7 10.3 %all_to_all.35 = f32[4,4,24,128]{3,2,1,0:T(8,128)S(1)} all-to-all(f32[4,4,24,128]{3,2,1,0:T(8,128)S(1)} %fusion), channel_id=1, replica_groups=mesh['zh'=4,'zl'=4,'x'=4,'c'=2,'t'=4] {'zl'}, dimensions={0} | all-to-all | bytes 393216 | tf_op jit(solution)/shard_map/all_to_all | solution.py:176
  59.0 19.2 %all_to_all.36 = f32[4,4,24,128]{3,2,1,0:T(8,128)S(1)} all-to-all(f32[4,4,24,128]{3,2,1,0:T(8,128)S(1)} %broadcast_in_dim.8), channel_id=1, replica_groups=mesh['zh'=4,'zl'=4,'x'=4,'c'=2,'t'=4] {'zh'}, dimensions={0} | all-to-all | bytes 393216 | tf_op jit(solution)/shard_map/all_to_all | solution.py:176
  78.2 0.0 copy-start
  78.3 15.7 %all_to_all.37 = f32[32,8,128]{2,1,0:T(8,128)S(1)} all-to-all(f32[32,8,128]{2,1,0:T(8,128)S(1)} %broadcast_in_dim.9), channel_id=1, replica_groups=mesh['zh'=4,'zl'=4,'x'=4,'c'=2,'t'=4] {'x','c','t'}, dimensions={0} | all-to-all | bytes 262144 | tf_op jit(solution)/shard_map/all_to_all | solution.py:176
  94.1 8.3 %all_to_all.38.refs_0_ = f32[4,8,128]{2,1,0:T(8,128)} all-to-all(f32[4,8,128]{2,1,0:T(8,128)S(1)} %broadcast_in_dim.10), channel_id=1, replica_groups=mesh['zh'=4,'zl'=4,'x'=4,'c'=2,'t'=4] {'zl'}, dimensions={0} | all-to-all | bytes 32768 | tf_op jit(solution)/shard_map/all_to_all | solution.py:176
  102.4 0.0 copy-done.1
  102.4 0.0 copy-done
  102.4 1.8 %update.1 = (f32[12,256]{1,0:T(8,128)}, f32[12,256]{1,0:T(8,128)}, f32[12,256]{1,0:T(8,128)}, f32[12,256]{1,0:T(8,128)}, bf16[4,4,24,128]{3,2,1,0:T(8,128)(2,1)}) custom-call(f32[4,8,128]{2,1,0:T(8,128)} %all_to_all.38.refs_0_, f32[4,24,128]{2,1,0:T(8,128)} %copy-done, f32[4,3,24,128]{3,2,1,0:T(8,128)} %copy-done.1, f32[12,256]{1,0:T(8,128)} %refs_3_.1, ...), custom_call_target="tpu_custom_call" | custom-call | tf_op jit(solution)/shard_map/update/pallas_call | solution.py:203
  104.3 8.0 %all_to_all.39 = bf16[4,4,24,128]{3,2,1,0:T(8,128)(2,1)S(1)} all-to-all(bf16[4,4,24,128]{3,2,1,0:T(8,128)(2,1)} %get-tuple-element.22), channel_id=1, replica_groups=mesh['zh'=4,'zl'=4,'x'=4,'c'=2,'t'=4] {'zl'}, dimensions={0} | all-to-all | bytes 196608 | tf_op jit(solution)/shard_map/all_to_all | solution.py:176
  112.2 0.1 broadcast_in_dim.11
  112.3 8.6 %all_to_all.40 = bf16[4,4,4,24,128]{4,3,2,1,0:T(8,128)(2,1)S(1)} all-to-all(bf16[4,4,4,24,128]{4,3,2,1,0:T(8,128)(2,1)S(1)} %broadcast_in_dim.11), channel_id=1, replica_groups=mesh['zh'=4,'zl'=4,'x'=4,'c'=2,'t'=4] {'x'}, dimensions={0} | all-to-all | bytes 786432 | tf_op jit(solution)/shard_map/all_to_all | solution.py:176
  120.9 6.3 %all-gather = bf16[8,4,4,24,128]{4,3,2,1,0:T(8,128)(2,1)} all-gather(bf16[4,4,4,24,128]{4,3,2,1,0:T(8,128)(2,1)S(1)} %all_to_all.40), channel_id=2, replica_groups=mesh['zh'=4,'zl'=4,'x'=4,'c'=2,'t'=4] {'c'}, dimensions={0}, use_global_device_ids=true | all-gather | bytes 1179648 | tf_op jit(solution)/shard_map/all_gather | solution.py:211
  127.2 1.9 %place.1 = bf16[1536,256]{1,0:T(8,128)(2,1)} custom-call(bf16[2,4,4,4,24,128]{5,4,3,2,1,0:T(8,128)(2,1)} %bitcast.15), custom_call_target="tpu_custom_call" | custom-call | tf_op jit(solution)/shard_map/place/pallas_call | solution.py:165
  (10 shorter events, 0.2 us)
Async XLA Ops:
  3.6 11.6 %collective-permute-start = (f32[4,4,4,24,128]{4,3,2,1,0:T(8,128)}, f32[4,4,4,24,128]{4,3,2,1,0:T(8,128)S(1)}, u32[]{:S(2)}, u32[]{:S(2)}) collective-permute-start(f32[4,4,4,24,128]{4,3,2,1,0:T(8,128)} %get-tuple-element.14), channel_id=1, source_target_pairs={{0,4},{4,0},{1,5},{5,1},{2,6},{6,2},{3,7},{7,3},{8,12},{12,8},{9,1... | collective-permute-start | bytes 2359304 | tf_op jit(solution)/shard_map/ppermute | solution.py:184
  16.4 20.0 %collective-permute-start.1 = (f32[4,4,24,128]{3,2,1,0:T(8,128)S(1)}, f32[4,4,24,128]{3,2,1,0:T(8,128)S(1)}, u32[]{:S(2)}, u32[]{:S(2)}) collective-permute-start(f32[4,4,24,128]{3,2,1,0:T(8,128)S(1)} %get-tuple-element.25), channel_id=1, source_target_pairs={{0,8},{8,16},{16,24},{24,0},{1,9},{9,17},{17,25},{25,1},{2,10},{10... | collective-permute-start | bytes 589832 | tf_op jit(solution)/shard_map/ppermute | solution.py:184
  18.4 18.1 %collective-permute-start.2 = (f32[4,4,24,128]{3,2,1,0:T(8,128)S(1)}, f32[4,4,24,128]{3,2,1,0:T(8,128)S(1)}, u32[]{:S(2)}, u32[]{:S(2)}) collective-permute-start(f32[4,4,24,128]{3,2,1,0:T(8,128)S(1)} %get-tuple-element.23), channel_id=1, source_target_pairs={{0,16},{8,24},{16,0},{24,8},{1,17},{9,25},{17,1},{25,9},{2,18},{10... | collective-permute-start | bytes 589832 | tf_op jit(solution)/shard_map/ppermute | solution.py:184
  20.3 16.2 %collective-permute-start.3 = (f32[4,4,24,128]{3,2,1,0:T(8,128)S(1)}, f32[4,4,24,128]{3,2,1,0:T(8,128)S(1)}, u32[]{:S(2)}, u32[]{:S(2)}) collective-permute-start(f32[4,4,24,128]{3,2,1,0:T(8,128)S(1)} %get-tuple-element.24), channel_id=1, source_target_pairs={{0,24},{8,0},{16,8},{24,16},{1,25},{9,1},{17,9},{25,17},{2,26},{10... | collective-permute-start | bytes 589832 | tf_op jit(solution)/shard_map/ppermute | solution.py:184
  24.9 23.8 %all-to-all-start = ((f32[4,3,24,128]{3,2,1,0:T(8,128)}), f32[4,3,24,128]{3,2,1,0:T(8,128)S(1)}, u32[]{:S(2)}, u32[]{:S(2)}) async-start(f32[4,3,24,128]{3,2,1,0:T(8,128)} %get-tuple-element.15), calls=%async_computation | async-start | bytes 294912 | tf_op jit(solution)/shard_map/all_to_all | solution.py:176
  48.7 53.8 %copy-start.1 = (f32[4,3,24,128]{3,2,1,0:T(8,128)}, f32[4,3,24,128]{3,2,1,0:T(8,128)S(1)}, u32[]{:S(2)}) copy-start(f32[4,3,24,128]{3,2,1,0:T(8,128)S(1)} %all-to-all-done.refs_2_) | copy-start | bytes 442372
  78.2 24.2 %copy-start = (f32[4,24,128]{2,1,0:T(8,128)}, f32[4,24,128]{2,1,0:T(8,128)S(1)}, u32[]{:S(2)}) copy-start(f32[4,24,128]{2,1,0:T(8,128)S(1)} %reduce_sum.37.refs_1_) | copy-start | bytes 147460

commit v7 on v6

--- a/solution.py
+++ b/solution.py
@@ -73,7 +73,7 @@
     @pl.when(pl.program_id(0) == 0)
     def _():
         for j, r in enumerate((ma_ref, m1_ref, m2_ref)):
-            st_ref[:, j] = jnp.broadcast_to(to_piece(core, r[...])[None], (ZH, PR, PC))
+            st_ref[j] = to_piece(core, r[...])
 
 
 def own_kernel(g_ref, o_ref):
@@ -93,10 +93,10 @@
     shape, source, target, cost = half_specs(local)
     return pl.pallas_call(
         other_kernel,
-        out_shape=(shape, jax.ShapeDtypeStruct((ZH, 3, PR, PC), F32)),
+        out_shape=(shape, jax.ShapeDtypeStruct((3, PR, PC), F32)),
         grid=(STEPS,),
         in_specs=[source] + [pl.BlockSpec((ROWS, COLS), lambda i: (0, 0))] * 3,
-        out_specs=(target, pl.BlockSpec((ZH, 3, PR, PC), lambda i: (0, 0, 0, 0))),
+        out_specs=(target, pl.BlockSpec((3, PR, PC), lambda i: (0, 0, 0))),
         cost_estimate=cost,
         name="other_sum",
     )(local, *state)
@@ -127,14 +127,16 @@
     return new, m1, m2
 
 
-def update_kernel(elements, sq_ref, t_ref, st_ref, ma_ref, m1_ref, m2_ref, em_ref, oma, om1, om2, oem, ow):
+def update_kernel(elements, sq_ref, t_ref, s0, s1, s2, s3, ma_ref, m1_ref, m2_ref, em_ref, oma, om1, om2, oem, ow):
     sq = jnp.sum(jnp.sum(sq_ref[...], axis=0))
     sq = jnp.full((1, PC), sq, F32)
     scale = jnp.minimum(1.0, 1.0 / jnp.sqrt(sq / elements + 1e-06))
-    for zh in range(ZH):
-        new, _, _ = adam(scale, t_ref[zh], st_ref[zh, 0], st_ref[zh, 1], st_ref[zh, 2])
+    me = lax.axis_index("zh")
+    for k, st in enumerate((s0, s1, s2, s3)):
+        zh = lax.rem(me + ZH - k, ZH)
+        new, _, _ = adam(scale, t_ref[zh], st[0], st[1], st[2])
         ow[:, zh] = jnp.broadcast_to(new.astype(BF16)[None], (ow.shape[0], PR, PC))
-    total = from_piece(lax.axis_index("c"), t_ref[lax.axis_index("zh")])
+    total = from_piece(lax.axis_index("c"), t_ref[me])
     wide = jnp.concatenate([scale, scale], axis=1)
     new, m1, m2 = adam(wide, total, ma_ref[...], m1_ref[...], m2_ref[...])
     oma[...] = new
@@ -189,7 +191,7 @@
     elements = local.shape[1] * local.shape[2] * T
 
     other, held = other_sum(local, master, moment1, moment2)
-    held = exchange(held, "zh")
+    held = [held] + [shift(held, "zh", ZH, k) for k in range(1, ZH)]
     part = own_sum(local) + shift(other, "c", C, 1)
     part = part[0] + sum(shift(part[k], "x", X, k) for k in range(1, X))
     part, held = lax.optimization_barrier((part, held))
@@ -204,7 +206,7 @@
         lambda *refs: update_kernel(elements, *refs),
         out_shape=(state, state, state, state, jax.ShapeDtypeStruct((ZL, ZH, PR, PC), BF16)),
         name="update",
-    )(sq, total, held, master, moment1, moment2, ema)
+    )(sq, total, *held, master, moment1, moment2, ema)
 
     w = exchange(w, "zl")
     w = exchange(copies(w, X), "x")

time: 130 us -> 134 us (1.031)
  starting transfers between devices: 28.8 us -> 38.7 us
  waiting for transfers between devices: 12.2 us -> 4.56 us
  blocking collectives: 76.5 us -> 78.5 us
    ppermute x4 -> x7, starting transfers between devices: 17.2 us -> 38.7 us  [shift(): return lax.ppermute(v, axis, [(i, (i + k) % n) for i in range(n)])]
    all_to_all x1 -> x0, waiting for transfers between devices: 12.2 us -> none  [exchange(): return lax.all_to_all(v, axes, split_axis=0, concat_axis=0, tiled=True)]
    all_to_all x1 -> x0, starting transfers between devices: 11.6 us -> none  [exchange(): return lax.all_to_all(v, axes, split_axis=0, concat_axis=0, tiled=True)]
    ppermute x4 -> x7, waiting for transfers between devices: 0.01 us -> 4.56 us  [shift(): return lax.ppermute(v, axis, [(i, (i + k) % n) for i in range(n)])]
    all_to_all x6, blocking collectives: 70.2 us -> 72.2 us  [exchange(): return lax.all_to_all(v, axes, split_axis=0, concat_axis=0, tiled=True)]
  transfers between devices with their start and end apart: 5 -> 7, of which waited for: 1 -> 1; matrix products, arithmetic and copies ran while one was open for 0% -> 0% of each run, Pallas kernels for 2% -> 2%
where the time goes in v7:
time: 134 us; the launch traced here: 133 us
  blocking collectives  78.5 us (59%)
  starting transfers between devices  38.7 us (29%)
  Pallas kernels  9.34 us (7%)
  waiting for transfers between devices  4.56 us (3%)
  other arithmetic  1.38 us (1%)
    all_to_all x6, blocking collectives, exchange(): return lax.all_to_all(v, axes, split_axis=0, concat_axis=0, tiled=True)  72.2 us
    ppermute x7, starting transfers between devices, shift(): return lax.ppermute(v, axis, [(i, (i + k) % n) for i in range(n)])  38.7 us
    all_gather x1, blocking collectives, shards(): w = lax.all_gather(w, 'c', axis=0, tiled=False)  6.33 us
    ppermute x7, waiting for transfers between devices, shift(): return lax.ppermute(v, axis, [(i, (i + k) % n) for i in range(n)])  4.56 us
    pallas_call x1, Pallas kernels, other_sum(): pl.pallas_call(other_kernel, out_shape=(shape, jax.ShapeDtypeStruct((3, P...  2.91 us
    pallas_call x1, Pallas kernels, own_sum(): pl.pallas_call(own_kernel, out_shape=shape, grid=(STEPS,), in_specs=[sour...  2.78 us
  transfers between devices with their start and end apart: 7, of which 1 were waited for; matrix products, arithmetic and copies ran while one was open for 0% of the time, Pallas kernels for 2%

profile of v7, /device:TPU:1, one launch (start us, length us, event | category | flops | bytes accessed | tf_op | source)
XLA Modules:
  0.0 133.5 jit_solution(10212067471020834415)
XLA Ops:
  0.6 2.9 %other_sum.1 = (f32[4,4,4,24,128]{4,3,2,1,0:T(8,128)}, f32[3,24,128]{2,1,0:T(8,128)}) custom-call(bf16[4,1536,256]{2,1,0:T(8,128)(2,1)} %bitcast.13, f32[12,256]{1,0:T(8,128)} %refs_6_.1, f32[12,256]{1,0:T(8,128)} %refs_7_.1, f32[12,256]{1,0:T(8,128)} %refs_8_.1), custom_call_target="tpu_custom_call" | custom-call | flops 2000000 | bytes 4000000 | tf_op jit(solution)/shard_map/other_sum/pallas_call | solution.py:94
  3.5 0.0 copy-start.1
  3.5 8.9 %collective-permute-start = (f32[4,4,4,24,128]{4,3,2,1,0:T(8,128)}, f32[4,4,4,24,128]{4,3,2,1,0:T(8,128)S(1)}, u32[]{:S(2)}, u32[]{:S(2)}) collective-permute-start(f32[4,4,4,24,128]{4,3,2,1,0:T(8,128)} %get-tuple-element.17), channel_id=1, source_target_pairs={{0,4},{4,0},{1,5},{5,1},{2,6},{6,2},{3,7},{7,3},{8,12},{12,8},{9,1... | collective-permute-start | bytes 2359304 | tf_op jit(solution)/shard_map/ppermute | solution.py:186
  12.5 2.8 %own_sum.1 = f32[4,4,4,24,128]{4,3,2,1,0:T(8,128)} custom-call(bf16[4,1536,256]{2,1,0:T(8,128)(2,1)} %bitcast.14), custom_call_target="tpu_custom_call" | custom-call | flops 2000000 | bytes 4000000 | tf_op jit(solution)/shard_map/own_sum/pallas_call | solution.py:107
  15.2 0.0 collective-permute-done
  15.2 1.2 add.12
  16.5 1.9 %collective-permute-start.1 = (f32[4,4,24,128]{3,2,1,0:T(8,128)S(1)}, f32[4,4,24,128]{3,2,1,0:T(8,128)S(1)}, u32[]{:S(2)}, u32[]{:S(2)}) collective-permute-start(f32[4,4,24,128]{3,2,1,0:T(8,128)S(1)} %get-tuple-element.31), channel_id=1, source_target_pairs={{0,8},{8,16},{16,24},{24,0},{1,9},{9,17},{17,25},{25,1},{2,10},{10... | collective-permute-start | bytes 589832 | tf_op jit(solution)/shard_map/ppermute | solution.py:186
  18.4 1.9 %collective-permute-start.2 = (f32[4,4,24,128]{3,2,1,0:T(8,128)S(1)}, f32[4,4,24,128]{3,2,1,0:T(8,128)S(1)}, u32[]{:S(2)}, u32[]{:S(2)}) collective-permute-start(f32[4,4,24,128]{3,2,1,0:T(8,128)S(1)} %get-tuple-element.29), channel_id=1, source_target_pairs={{0,16},{8,24},{16,0},{24,8},{1,17},{9,25},{17,1},{25,9},{2,18},{10... | collective-permute-start | bytes 589832 | tf_op jit(solution)/shard_map/ppermute | solution.py:186
  20.4 4.6 %collective-permute-start.3 = (f32[4,4,24,128]{3,2,1,0:T(8,128)S(1)}, f32[4,4,24,128]{3,2,1,0:T(8,128)S(1)}, u32[]{:S(2)}, u32[]{:S(2)}) collective-permute-start(f32[4,4,24,128]{3,2,1,0:T(8,128)S(1)} %get-tuple-element.30), channel_id=1, source_target_pairs={{0,24},{8,0},{16,8},{24,16},{1,25},{9,1},{17,9},{25,17},{2,26},{10... | collective-permute-start | bytes 589832 | tf_op jit(solution)/shard_map/ppermute | solution.py:186
  25.0 0.0 copy-done.1
  25.0 5.6 %collective-permute-start.4 = (f32[3,24,128]{2,1,0:T(8,128)S(1)}, f32[3,24,128]{2,1,0:T(8,128)S(1)}, u32[]{:S(2)}, u32[]{:S(2)}) collective-permute-start(f32[3,24,128]{2,1,0:T(8,128)S(1)} %copy-done.1), channel_id=1, source_target_pairs={{0,128},{128,256},{256,384},{384,0},{1,129},{129,257},{257,385},{3... | collective-permute-start | bytes 110600 | tf_op jit(solution)/shard_map/ppermute | solution.py:186
  30.5 10.6 %collective-permute-start.5 = (f32[3,24,128]{2,1,0:T(8,128)S(1)}, f32[3,24,128]{2,1,0:T(8,128)S(1)}, u32[]{:S(2)}, u32[]{:S(2)}) collective-permute-start(f32[3,24,128]{2,1,0:T(8,128)S(1)} %copy-done.1), channel_id=1, source_target_pairs={{0,256},{128,384},{256,0},{384,128},{1,257},{129,385},{257,1},{385... | collective-permute-start | bytes 110600 | tf_op jit(solution)/shard_map/ppermute | solution.py:186
  41.2 0.0 collective-permute-done.1
  41.2 5.2 %collective-permute-start.6 = (f32[3,24,128]{2,1,0:T(8,128)S(1)}, f32[3,24,128]{2,1,0:T(8,128)S(1)}, u32[]{:S(2)}, u32[]{:S(2)}) collective-permute-start(f32[3,24,128]{2,1,0:T(8,128)S(1)} %copy-done.1), channel_id=1, source_target_pairs={{0,384},{128,0},{256,128},{384,256},{1,385},{129,1},{257,129},{385... | collective-permute-start | bytes 110600 | tf_op jit(solution)/shard_map/ppermute | solution.py:186
  46.4 0.0 collective-permute-done.2
  46.4 0.0 collective-permute-done.3
  46.4 0.1 fusion
  46.5 0.0 collective-permute-done.4.refs_3_
  46.5 0.0 copy-start.2
  46.5 0.0 collective-permute-done.5.refs_4_
  46.5 0.0 copy-start.3
  46.5 4.5 %collective-permute-done.6.refs_5_ = f32[3,24,128]{2,1,0:T(8,128)S(1)} collective-permute-done((f32[3,24,128]{2,1,0:T(8,128)S(1)}, f32[3,24,128]{2,1,0:T(8,128)S(1)}, u32[]{:S(2)}, u32[]{:S(2)}) %collective-permute-start.6) | collective-permute-done | bytes 36896 | tf_op jit(solution)/shard_map/ppermute | solution.py:186
  51.0 0.0 copy-start.4
  51.0 8.0 %all_to_all.30 = f32[4,4,24,128]{3,2,1,0:T(8,128)S(1)} all-to-all(f32[4,4,24,128]{3,2,1,0:T(8,128)S(1)} %fusion), channel_id=1, replica_groups=mesh['zh'=4,'zl'=4,'x'=4,'c'=2,'t'=4] {'zl'}, dimensions={0} | all-to-all | bytes 393216 | tf_op jit(solution)/shard_map/all_to_all | solution.py:178
  59.1 23.0 %all_to_all.31 = f32[4,4,24,128]{3,2,1,0:T(8,128)S(1)} all-to-all(f32[4,4,24,128]{3,2,1,0:T(8,128)S(1)} %broadcast_in_dim.8), channel_id=1, replica_groups=mesh['zh'=4,'zl'=4,'x'=4,'c'=2,'t'=4] {'zh'}, dimensions={0} | all-to-all | bytes 393216 | tf_op jit(solution)/shard_map/all_to_all | solution.py:178
  82.2 0.0 copy-start
  82.2 16.1 %all_to_all.32 = f32[32,8,128]{2,1,0:T(8,128)S(1)} all-to-all(f32[32,8,128]{2,1,0:T(8,128)S(1)} %broadcast_in_dim.9), channel_id=1, replica_groups=mesh['zh'=4,'zl'=4,'x'=4,'c'=2,'t'=4] {'x','c','t'}, dimensions={0} | all-to-all | bytes 262144 | tf_op jit(solution)/shard_map/all_to_all | solution.py:178
  98.4 8.4 %all_to_all.33.refs_0_ = f32[4,8,128]{2,1,0:T(8,128)} all-to-all(f32[4,8,128]{2,1,0:T(8,128)S(1)} %broadcast_in_dim.10), channel_id=1, replica_groups=mesh['zh'=4,'zl'=4,'x'=4,'c'=2,'t'=4] {'zl'}, dimensions={0} | all-to-all | bytes 32768 | tf_op jit(solution)/shard_map/all_to_all | solution.py:178
  106.8 0.0 copy-done.2
  106.8 0.0 copy-done.3
  106.8 0.0 copy-done.4
  106.8 0.0 copy-done
  106.8 1.7 %update.1 = (f32[12,256]{1,0:T(8,128)}, f32[12,256]{1,0:T(8,128)}, f32[12,256]{1,0:T(8,128)}, f32[12,256]{1,0:T(8,128)}, bf16[4,4,24,128]{3,2,1,0:T(8,128)(2,1)}) custom-call(f32[4,8,128]{2,1,0:T(8,128)} %all_to_all.33.refs_0_, f32[4,24,128]{2,1,0:T(8,128)} %copy-done, f32[3,24,128]{2,1,0:T(8,128)} %get-tuple-element.20.refs_2_, f32[3,24,128]{2,1,0:T(8,128)} %copy-done.2, ...), custom_call_target="tpu_custom_call" | custom-call | tf_op jit(solution)/shard_map/update/pallas_call | solution.py:205
  108.6 8.0 %all_to_all.34 = bf16[4,4,24,128]{3,2,1,0:T(8,128)(2,1)S(1)} all-to-all(bf16[4,4,24,128]{3,2,1,0:T(8,128)(2,1)} %get-tuple-element.28), channel_id=1, replica_groups=mesh['zh'=4,'zl'=4,'x'=4,'c'=2,'t'=4] {'zl'}, dimensions={0} | all-to-all | bytes 196608 | tf_op jit(solution)/shard_map/all_to_all | solution.py:178
  116.5 0.1 broadcast_in_dim.11
  116.6 8.6 %all_to_all.35 = bf16[4,4,4,24,128]{4,3,2,1,0:T(8,128)(2,1)S(1)} all-to-all(bf16[4,4,4,24,128]{4,3,2,1,0:T(8,128)(2,1)S(1)} %broadcast_in_dim.11), channel_id=1, replica_groups=mesh['zh'=4,'zl'=4,'x'=4,'c'=2,'t'=4] {'x'}, dimensions={0} | all-to-all | bytes 786432 | tf_op jit(solution)/shard_map/all_to_all | solution.py:178
  125.2 6.3 %all-gather = bf16[8,4,4,24,128]{4,3,2,1,0:T(8,128)(2,1)} all-gather(bf16[4,4,4,24,128]{4,3,2,1,0:T(8,128)(2,1)S(1)} %all_to_all.35), channel_id=2, replica_groups=mesh['zh'=4,'zl'=4,'x'=4,'c'=2,'t'=4] {'c'}, dimensions={0}, use_global_device_ids=true | all-gather | bytes 1179648 | tf_op jit(solution)/shard_map/all_gather | solution.py:213
  131.6 1.9 %place.1 = bf16[1536,256]{1,0:T(8,128)(2,1)} custom-call(bf16[2,4,4,4,24,128]{5,4,3,2,1,0:T(8,128)(2,1)} %bitcast.15), custom_call_target="tpu_custom_call" | custom-call | tf_op jit(solution)/shard_map/place/pallas_call | solution.py:167
  (9 shorter events, 0.2 us)
Async XLA Ops:
  3.5 21.4 %copy-start.1 = (f32[3,24,128]{2,1,0:T(8,128)S(1)}, f32[3,24,128]{2,1,0:T(8,128)}, u32[]{:S(2)}) copy-start(f32[3,24,128]{2,1,0:T(8,128)} %get-tuple-element.20.refs_2_) | copy-start | bytes 110596
  3.5 11.7 %collective-permute-start = (f32[4,4,4,24,128]{4,3,2,1,0:T(8,128)}, f32[4,4,4,24,128]{4,3,2,1,0:T(8,128)S(1)}, u32[]{:S(2)}, u32[]{:S(2)}) collective-permute-start(f32[4,4,4,24,128]{4,3,2,1,0:T(8,128)} %get-tuple-element.17), channel_id=1, source_target_pairs={{0,4},{4,0},{1,5},{5,1},{2,6},{6,2},{3,7},{7,3},{8,12},{12,8},{9,1... | collective-permute-start | bytes 2359304 | tf_op jit(solution)/shard_map/ppermute | solution.py:186
  16.5 24.7 %collective-permute-start.1 = (f32[4,4,24,128]{3,2,1,0:T(8,128)S(1)}, f32[4,4,24,128]{3,2,1,0:T(8,128)S(1)}, u32[]{:S(2)}, u32[]{:S(2)}) collective-permute-start(f32[4,4,24,128]{3,2,1,0:T(8,128)S(1)} %get-tuple-element.31), channel_id=1, source_target_pairs={{0,8},{8,16},{16,24},{24,0},{1,9},{9,17},{17,25},{25,1},{2,10},{10... | collective-permute-start | bytes 589832 | tf_op jit(solution)/shard_map/ppermute | solution.py:186
  18.4 27.9 %collective-permute-start.2 = (f32[4,4,24,128]{3,2,1,0:T(8,128)S(1)}, f32[4,4,24,128]{3,2,1,0:T(8,128)S(1)}, u32[]{:S(2)}, u32[]{:S(2)}) collective-permute-start(f32[4,4,24,128]{3,2,1,0:T(8,128)S(1)} %get-tuple-element.29), channel_id=1, source_target_pairs={{0,16},{8,24},{16,0},{24,8},{1,17},{9,25},{17,1},{25,9},{2,18},{10... | collective-permute-start | bytes 589832 | tf_op jit(solution)/shard_map/ppermute | solution.py:186
  20.4 26.0 %collective-permute-start.3 = (f32[4,4,24,128]{3,2,1,0:T(8,128)S(1)}, f32[4,4,24,128]{3,2,1,0:T(8,128)S(1)}, u32[]{:S(2)}, u32[]{:S(2)}) collective-permute-start(f32[4,4,24,128]{3,2,1,0:T(8,128)S(1)} %get-tuple-element.30), channel_id=1, source_target_pairs={{0,24},{8,0},{16,8},{24,16},{1,25},{9,1},{17,9},{25,17},{2,26},{10... | collective-permute-start | bytes 589832 | tf_op jit(solution)/shard_map/ppermute | solution.py:186
  25.0 21.5 %collective-permute-start.4 = (f32[3,24,128]{2,1,0:T(8,128)S(1)}, f32[3,24,128]{2,1,0:T(8,128)S(1)}, u32[]{:S(2)}, u32[]{:S(2)}) collective-permute-start(f32[3,24,128]{2,1,0:T(8,128)S(1)} %copy-done.1), channel_id=1, source_target_pairs={{0,128},{128,256},{256,384},{384,0},{1,129},{129,257},{257,385},{3... | collective-permute-start | bytes 110600 | tf_op jit(solution)/shard_map/ppermute | solution.py:186
  30.5 15.9 %collective-permute-start.5 = (f32[3,24,128]{2,1,0:T(8,128)S(1)}, f32[3,24,128]{2,1,0:T(8,128)S(1)}, u32[]{:S(2)}, u32[]{:S(2)}) collective-permute-start(f32[3,24,128]{2,1,0:T(8,128)S(1)} %copy-done.1), channel_id=1, source_target_pairs={{0,256},{128,384},{256,0},{384,128},{1,257},{129,385},{257,1},{385... | collective-permute-start | bytes 110600 | tf_op jit(solution)/shard_map/ppermute | solution.py:186
  41.2 9.8 %collective-permute-start.6 = (f32[3,24,128]{2,1,0:T(8,128)S(1)}, f32[3,24,128]{2,1,0:T(8,128)S(1)}, u32[]{:S(2)}, u32[]{:S(2)}) collective-permute-start(f32[3,24,128]{2,1,0:T(8,128)S(1)} %copy-done.1), channel_id=1, source_target_pairs={{0,384},{128,0},{256,128},{384,256},{1,385},{129,1},{257,129},{385... | collective-permute-start | bytes 110600 | tf_op jit(solution)/shard_map/ppermute | solution.py:186
  46.5 60.3 %copy-start.2 = (f32[3,24,128]{2,1,0:T(8,128)}, f32[3,24,128]{2,1,0:T(8,128)S(1)}, u32[]{:S(2)}) copy-start(f32[3,24,128]{2,1,0:T(8,128)S(1)} %collective-permute-done.4.refs_3_) | copy-start | bytes 110596
  46.5 60.3 %copy-start.3 = (f32[3,24,128]{2,1,0:T(8,128)}, f32[3,24,128]{2,1,0:T(8,128)S(1)}, u32[]{:S(2)}) copy-start(f32[3,24,128]{2,1,0:T(8,128)S(1)} %collective-permute-done.5.refs_4_) | copy-start | bytes 110596
  51.0 55.8 %copy-start.4 = (f32[3,24,128]{2,1,0:T(8,128)}, f32[3,24,128]{2,1,0:T(8,128)S(1)}, u32[]{:S(2)}) copy-start(f32[3,24,128]{2,1,0:T(8,128)S(1)} %collective-permute-done.6.refs_5_) | copy-start | bytes 110596
  82.2 24.7 %copy-start = (f32[4,24,128]{2,1,0:T(8,128)}, f32[4,24,128]{2,1,0:T(8,128)S(1)}, u32[]{:S(2)}) copy-start(f32[4,24,128]{2,1,0:T(8,128)S(1)} %reduce_sum.37.refs_1_) | copy-start | bytes 147460

commit v8 on v6

--- a/solution.py
+++ b/solution.py
@@ -191,8 +191,9 @@
     other, held = other_sum(local, master, moment1, moment2)
     held = exchange(held, "zh")
     part = own_sum(local) + shift(other, "c", C, 1)
-    part = part[0] + sum(shift(part[k], "x", X, k) for k in range(1, X))
-    part, held = lax.optimization_barrier((part, held))
+    parts = [part[0]] + [shift(part[k], "x", X, k) for k in range(1, X)]
+    parts, held = lax.optimization_barrier((parts, held))
+    part = parts[0] + parts[1] + parts[2] + parts[3]
     part = jnp.sum(exchange(part, "zl"), axis=0)
     total = jnp.sum(exchange(copies(part, ZH), "zh"), axis=0)
     sq = jnp.sum((total * total).reshape(-1, 8, PC), axis=0)

time: 130 us -> 131 us (level)
  blocking collectives: 76.5 us -> 84.9 us
  waiting for transfers between devices: 12.2 us -> 5.21 us
    all_to_all x1, waiting for transfers between devices: 12.2 us -> 0.01 us  [exchange(): return lax.all_to_all(v, axes, split_axis=0, concat_axis=0, tiled=True)]
    all_to_all x6, blocking collectives: 70.2 us -> 78.5 us  [exchange(): return lax.all_to_all(v, axes, split_axis=0, concat_axis=0, tiled=True)]
    ppermute x4, waiting for transfers between devices: 0.01 us -> 5.2 us  [shift(): return lax.ppermute(v, axis, [(i, (i + k) % n) for i in range(n)])]
    ppermute x4, starting transfers between devices: 17.2 us -> 19.3 us  [shift(): return lax.ppermute(v, axis, [(i, (i + k) % n) for i in range(n)])]
    all_to_all x1, starting transfers between devices: 11.6 us -> 9.44 us  [exchange(): return lax.all_to_all(v, axes, split_axis=0, concat_axis=0, tiled=True)]
  transfers between devices with their start and end apart: 5 -> 5, of which waited for: 1 -> 2; matrix products, arithmetic and copies ran while one was open for 0% -> 1% of each run, Pallas kernels for 2% -> 2%
where the time goes in v8:
time: 131 us
  blocking collectives  84.9 us (65%)
  starting transfers between devices  28.8 us (22%)
  Pallas kernels  9.45 us (7%)
  waiting for transfers between devices  5.21 us (4%)
  other arithmetic  1.36 us (1%)
    all_to_all x6, blocking collectives, exchange(): return lax.all_to_all(v, axes, split_axis=0, concat_axis=0, tiled=True)  78.5 us
    ppermute x4, starting transfers between devices, shift(): return lax.ppermute(v, axis, [(i, (i + k) % n) for i in range(n)])  19.3 us
    all_to_all x1, starting transfers between devices, exchange(): return lax.all_to_all(v, axes, split_axis=0, concat_axis=0, tiled=True)  9.44 us
    all_gather x1, blocking collectives, shards(): w = lax.all_gather(w, 'c', axis=0, tiled=False)  6.33 us
    ppermute x4, waiting for transfers between devices, shift(): return lax.ppermute(v, axis, [(i, (i + k) % n) for i in range(n)])  5.2 us
    pallas_call x1, Pallas kernels, other_sum(): pl.pallas_call(other_kernel, out_shape=(shape, jax.ShapeDtypeStruct((ZH,...  2.95 us
    pallas_call x1, Pallas kernels, own_sum(): pl.pallas_call(own_kernel, out_shape=shape, grid=(STEPS,), in_specs=[sour...  2.76 us
  transfers between devices with their start and end apart: 5, of which 2 were waited for; matrix products, arithmetic and copies ran while one was open for 1% of the time, Pallas kernels for 2%

profile of v8, /device:TPU:1, one launch (start us, length us, event | category | flops | bytes accessed | tf_op | source)
XLA Modules:
  0.0 130.5 jit_solution(19033377419198452)
XLA Ops:
  0.6 3.0 %other_sum.1 = (f32[4,4,4,24,128]{4,3,2,1,0:T(8,128)}, f32[4,3,24,128]{3,2,1,0:T(8,128)}) custom-call(bf16[4,1536,256]{2,1,0:T(8,128)(2,1)} %bitcast.11, f32[12,256]{1,0:T(8,128)} %refs_3_.1, f32[12,256]{1,0:T(8,128)} %refs_4_.1, f32[12,256]{1,0:T(8,128)} %refs_5_.1), custom_call_target="tpu_custom_call" | custom-call | flops 2000000 | bytes 4000000 | tf_op jit(solution)/shard_map/other_sum/pallas_call | solution.py:94
  3.6 8.8 %collective-permute-start = (f32[4,4,4,24,128]{4,3,2,1,0:T(8,128)}, f32[4,4,4,24,128]{4,3,2,1,0:T(8,128)S(1)}, u32[]{:S(2)}, u32[]{:S(2)}) collective-permute-start(f32[4,4,4,24,128]{4,3,2,1,0:T(8,128)} %get-tuple-element.17), channel_id=1, source_target_pairs={{0,4},{4,0},{1,5},{5,1},{2,6},{6,2},{3,7},{7,3},{8,12},{12,8},{9,1... | collective-permute-start | bytes 2359304 | tf_op jit(solution)/shard_map/ppermute | solution.py:184
  12.4 9.4 %all-to-all-start = ((f32[4,3,24,128]{3,2,1,0:T(8,128)}), f32[4,3,24,128]{3,2,1,0:T(8,128)S(1)}, u32[]{:S(2)}, u32[]{:S(2)}) async-start(f32[4,3,24,128]{3,2,1,0:T(8,128)} %get-tuple-element.18), calls=%async_computation | async-start | bytes 294912 | tf_op jit(solution)/shard_map/all_to_all | solution.py:176
  21.8 2.8 %own_sum.1 = f32[4,4,4,24,128]{4,3,2,1,0:T(8,128)} custom-call(bf16[4,1536,256]{2,1,0:T(8,128)(2,1)} %bitcast.12), custom_call_target="tpu_custom_call" | custom-call | flops 2000000 | bytes 4000000 | tf_op jit(solution)/shard_map/own_sum/pallas_call | solution.py:107
  24.6 0.0 collective-permute-done
  24.6 1.2 add.12
  25.8 0.1 slice_bitcast_fusion
  25.9 3.1 %collective-permute-start.1 = (f32[4,4,24,128]{3,2,1,0:T(8,128)S(1)}, f32[4,4,24,128]{3,2,1,0:T(8,128)S(1)}, u32[]{:S(2)}, u32[]{:S(2)}) collective-permute-start(f32[4,4,24,128]{3,2,1,0:T(8,128)S(1)} %get-tuple-element.31), channel_id=1, source_target_pairs={{0,8},{8,16},{16,24},{24,0},{1,9},{9,17},{17,25},{25,1},{2,10},{10... | collective-permute-start | bytes 589832 | tf_op jit(solution)/shard_map/ppermute | solution.py:184
  29.0 4.4 %collective-permute-start.2 = (f32[4,4,24,128]{3,2,1,0:T(8,128)S(1)}, f32[4,4,24,128]{3,2,1,0:T(8,128)S(1)}, u32[]{:S(2)}, u32[]{:S(2)}) collective-permute-start(f32[4,4,24,128]{3,2,1,0:T(8,128)S(1)} %get-tuple-element.30), channel_id=1, source_target_pairs={{0,16},{8,24},{16,0},{24,8},{1,17},{9,25},{17,1},{25,9},{2,18},{10... | collective-permute-start | bytes 589832 | tf_op jit(solution)/shard_map/ppermute | solution.py:184
  33.4 3.1 %collective-permute-start.3 = (f32[4,4,24,128]{3,2,1,0:T(8,128)S(1)}, f32[4,4,24,128]{3,2,1,0:T(8,128)S(1)}, u32[]{:S(2)}, u32[]{:S(2)}) collective-permute-start(f32[4,4,24,128]{3,2,1,0:T(8,128)S(1)} %get-tuple-element.29), channel_id=1, source_target_pairs={{0,24},{8,0},{16,8},{24,16},{1,25},{9,1},{17,9},{25,17},{2,26},{10... | collective-permute-start | bytes 589832 | tf_op jit(solution)/shard_map/ppermute | solution.py:184
  36.4 0.0 all-to-all-done.refs_2_
  36.4 0.0 copy-start.1
  36.5 0.0 collective-permute-done.1
  36.5 3.9 %collective-permute-done.2 = f32[4,4,24,128]{3,2,1,0:T(8,128)S(1)} collective-permute-done((f32[4,4,24,128]{3,2,1,0:T(8,128)S(1)}, f32[4,4,24,128]{3,2,1,0:T(8,128)S(1)}, u32[]{:S(2)}, u32[]{:S(2)}) %collective-permute-start.2) | collective-permute-done | bytes 196640 | tf_op jit(solution)/shard_map/ppermute | solution.py:184
  40.4 1.3 collective-permute-done.3
  41.7 8.4 %all_to_all.35 = f32[4,4,24,128]{3,2,1,0:T(8,128)S(1)} all-to-all(f32[4,4,24,128]{3,2,1,0:T(8,128)S(1)} %add_add_fusion), channel_id=1, replica_groups=mesh['zh'=4,'zl'=4,'x'=4,'c'=2,'t'=4] {'zl'}, dimensions={0} | all-to-all | bytes 393216 | tf_op jit(solution)/shard_map/all_to_all | solution.py:176
  50.1 23.9 %all_to_all.36 = f32[4,4,24,128]{3,2,1,0:T(8,128)S(1)} all-to-all(f32[4,4,24,128]{3,2,1,0:T(8,128)S(1)} %broadcast_in_dim.8), channel_id=1, replica_groups=mesh['zh'=4,'zl'=4,'x'=4,'c'=2,'t'=4] {'zh'}, dimensions={0} | all-to-all | bytes 393216 | tf_op jit(solution)/shard_map/all_to_all | solution.py:176
  74.1 0.0 copy-start
  74.1 21.0 %all_to_all.37 = f32[32,8,128]{2,1,0:T(8,128)S(1)} all-to-all(f32[32,8,128]{2,1,0:T(8,128)S(1)} %broadcast_in_dim.9), channel_id=1, replica_groups=mesh['zh'=4,'zl'=4,'x'=4,'c'=2,'t'=4] {'x','c','t'}, dimensions={0} | all-to-all | bytes 262144 | tf_op jit(solution)/shard_map/all_to_all | solution.py:176
  95.1 8.7 %all_to_all.38.refs_0_ = f32[4,8,128]{2,1,0:T(8,128)} all-to-all(f32[4,8,128]{2,1,0:T(8,128)S(1)} %broadcast_in_dim.10), channel_id=1, replica_groups=mesh['zh'=4,'zl'=4,'x'=4,'c'=2,'t'=4] {'zl'}, dimensions={0} | all-to-all | bytes 32768 | tf_op jit(solution)/shard_map/all_to_all | solution.py:176
  103.8 0.0 copy-done.1
  103.8 0.0 copy-done
  103.8 1.8 %update.1 = (f32[12,256]{1,0:T(8,128)}, f32[12,256]{1,0:T(8,128)}, f32[12,256]{1,0:T(8,128)}, f32[12,256]{1,0:T(8,128)}, bf16[4,4,24,128]{3,2,1,0:T(8,128)(2,1)}) custom-call(f32[4,8,128]{2,1,0:T(8,128)} %all_to_all.38.refs_0_, f32[4,24,128]{2,1,0:T(8,128)} %copy-done, f32[4,3,24,128]{3,2,1,0:T(8,128)} %copy-done.1, f32[12,256]{1,0:T(8,128)} %refs_3_.1, ...), custom_call_target="tpu_custom_call" | custom-call | tf_op jit(solution)/shard_map/update/pallas_call | solution.py:204
  105.7 8.0 %all_to_all.39 = bf16[4,4,24,128]{3,2,1,0:T(8,128)(2,1)S(1)} all-to-all(bf16[4,4,24,128]{3,2,1,0:T(8,128)(2,1)} %get-tuple-element.28), channel_id=1, replica_groups=mesh['zh'=4,'zl'=4,'x'=4,'c'=2,'t'=4] {'zl'}, dimensions={0} | all-to-all | bytes 196608 | tf_op jit(solution)/shard_map/all_to_all | solution.py:176
  113.6 0.1 broadcast_in_dim.11
  113.7 8.6 %all_to_all.40 = bf16[4,4,4,24,128]{4,3,2,1,0:T(8,128)(2,1)S(1)} all-to-all(bf16[4,4,4,24,128]{4,3,2,1,0:T(8,128)(2,1)S(1)} %broadcast_in_dim.11), channel_id=1, replica_groups=mesh['zh'=4,'zl'=4,'x'=4,'c'=2,'t'=4] {'x'}, dimensions={0} | all-to-all | bytes 786432 | tf_op jit(solution)/shard_map/all_to_all | solution.py:176
  122.3 6.3 %all-gather = bf16[8,4,4,24,128]{4,3,2,1,0:T(8,128)(2,1)} all-gather(bf16[4,4,4,24,128]{4,3,2,1,0:T(8,128)(2,1)S(1)} %all_to_all.40), channel_id=2, replica_groups=mesh['zh'=4,'zl'=4,'x'=4,'c'=2,'t'=4] {'c'}, dimensions={0}, use_global_device_ids=true | all-gather | bytes 1179648 | tf_op jit(solution)/shard_map/all_gather | solution.py:212
  128.6 1.9 %place.1 = bf16[1536,256]{1,0:T(8,128)(2,1)} custom-call(bf16[2,4,4,4,24,128]{5,4,3,2,1,0:T(8,128)(2,1)} %bitcast.13), custom_call_target="tpu_custom_call" | custom-call | tf_op jit(solution)/shard_map/place/pallas_call | solution.py:165
  (9 shorter events, 0.2 us)
Async XLA Ops:
  3.6 21.0 %collective-permute-start = (f32[4,4,4,24,128]{4,3,2,1,0:T(8,128)}, f32[4,4,4,24,128]{4,3,2,1,0:T(8,128)S(1)}, u32[]{:S(2)}, u32[]{:S(2)}) collective-permute-start(f32[4,4,4,24,128]{4,3,2,1,0:T(8,128)} %get-tuple-element.17), channel_id=1, source_target_pairs={{0,4},{4,0},{1,5},{5,1},{2,6},{6,2},{3,7},{7,3},{8,12},{12,8},{9,1... | collective-permute-start | bytes 2359304 | tf_op jit(solution)/shard_map/ppermute | solution.py:184
  12.4 24.1 %all-to-all-start = ((f32[4,3,24,128]{3,2,1,0:T(8,128)}), f32[4,3,24,128]{3,2,1,0:T(8,128)S(1)}, u32[]{:S(2)}, u32[]{:S(2)}) async-start(f32[4,3,24,128]{3,2,1,0:T(8,128)} %get-tuple-element.18), calls=%async_computation | async-start | bytes 294912 | tf_op jit(solution)/shard_map/all_to_all | solution.py:176
  25.9 10.6 %collective-permute-start.1 = (f32[4,4,24,128]{3,2,1,0:T(8,128)S(1)}, f32[4,4,24,128]{3,2,1,0:T(8,128)S(1)}, u32[]{:S(2)}, u32[]{:S(2)}) collective-permute-start(f32[4,4,24,128]{3,2,1,0:T(8,128)S(1)} %get-tuple-element.31), channel_id=1, source_target_pairs={{0,8},{8,16},{16,24},{24,0},{1,9},{9,17},{17,25},{25,1},{2,10},{10... | collective-permute-start | bytes 589832 | tf_op jit(solution)/shard_map/ppermute | solution.py:184
  29.0 11.4 %collective-permute-start.2 = (f32[4,4,24,128]{3,2,1,0:T(8,128)S(1)}, f32[4,4,24,128]{3,2,1,0:T(8,128)S(1)}, u32[]{:S(2)}, u32[]{:S(2)}) collective-permute-start(f32[4,4,24,128]{3,2,1,0:T(8,128)S(1)} %get-tuple-element.30), channel_id=1, source_target_pairs={{0,16},{8,24},{16,0},{24,8},{1,17},{9,25},{17,1},{25,9},{2,18},{10... | collective-permute-start | bytes 589832 | tf_op jit(solution)/shard_map/ppermute | solution.py:184
  33.4 8.3 %collective-permute-start.3 = (f32[4,4,24,128]{3,2,1,0:T(8,128)S(1)}, f32[4,4,24,128]{3,2,1,0:T(8,128)S(1)}, u32[]{:S(2)}, u32[]{:S(2)}) collective-permute-start(f32[4,4,24,128]{3,2,1,0:T(8,128)S(1)} %get-tuple-element.29), channel_id=1, source_target_pairs={{0,24},{8,0},{16,8},{24,16},{1,25},{9,1},{17,9},{25,17},{2,26},{10... | collective-permute-start | bytes 589832 | tf_op jit(solution)/shard_map/ppermute | solution.py:184
  36.4 67.4 %copy-start.1 = (f32[4,3,24,128]{3,2,1,0:T(8,128)}, f32[4,3,24,128]{3,2,1,0:T(8,128)S(1)}, u32[]{:S(2)}) copy-start(f32[4,3,24,128]{3,2,1,0:T(8,128)S(1)} %all-to-all-done.refs_2_) | copy-start | bytes 442372
  74.1 29.8 %copy-start = (f32[4,24,128]{2,1,0:T(8,128)}, f32[4,24,128]{2,1,0:T(8,128)S(1)}, u32[]{:S(2)}) copy-start(f32[4,24,128]{2,1,0:T(8,128)S(1)} %reduce_sum.37.refs_1_) | copy-start | bytes 147460

commit v9 on v4

v9 whole, which is shorter than its diff:
```python
import jax
import jax.numpy as jnp
from jax import lax
from jax.experimental import pallas as pl
from jax.experimental.pallas import tpu as pltpu
from jax.sharding import Mesh, PartitionSpec as P

STEP = 10
BETA_ONE = 0.9
BETA_TWO = 0.95
LEARN_RATE = 0.02
DECAY_WEIGHT = 0.1
EMA_KEEP = 0.99

Z, X, C, T = 16, 4, 2, 4
ROWS, COLS = 12, 256
PR, PC = 24, 128
GROUP = C * ROWS
STEPS = 2
NZ = Z // STEPS

F32 = jnp.float32
BF16 = jnp.bfloat16


def upper():
    return lax.broadcasted_iota(jnp.int32, (8, PC), 0) < 4


def shared_tile(core, left, right):
    turned = pltpu.roll(right, 4, 0)
    return jnp.where(upper(), left, turned) if core == 0 else jnp.where(upper(), turned, left)


def to_piece(core, v):
    zero = [v[0:8, :PC], v[0:8, PC:], v[8:12, :PC], v[8:12, PC:]]
    one = [v[4:12, :PC], v[4:12, PC:], v[0:4, PC:], v[0:4, :PC]]
    return jnp.where(core == 0, jnp.concatenate(zero, axis=0), jnp.concatenate(one, axis=0))


def from_piece(core, p):
    full = jnp.concatenate([p[0:8], p[8:16]], axis=1)
    zero = jnp.concatenate([full, jnp.concatenate([p[16:20], p[20:24]], axis=1)], axis=0)
    one = jnp.concatenate([jnp.concatenate([p[20:24], p[16:20]], axis=1), full], axis=0)
    return jnp.where(core == 0, zero, one)


def sum_kernel(g_ref, o_ref):
    for z in range(NZ):
        for pair in range(X // 2):
            at = (z * X + 2 * pair) * GROUP
            v = g_ref[0, at : at + 2 * GROUP, :].astype(F32)
            for m in range(1, g_ref.shape[0]):
                v = v + g_ref[m, at : at + 2 * GROUP, :].astype(F32)
            for k in range(2):
                first, both, last = [v[k * GROUP + j : k * GROUP + j + 8] for j in (0, 8, 16)]
                for core, own in ((0, first), (1, last)):
                    o = o_ref.at[core, 2 * pair + k, z]
                    o[0:8] = own[:, :PC]
                    o[8:16] = own[:, PC:]
                    o[16:24] = shared_tile(core, both[:, :PC], both[:, PC:])


def micro_sum(local):
    rows = NZ * X * GROUP
    return pl.pallas_call(
        sum_kernel,
        out_shape=jax.ShapeDtypeStruct((C, X, Z, PR, PC), F32),
        grid=(STEPS,),
        in_specs=[pl.BlockSpec((local.shape[0], rows, COLS), lambda i: (0, i, 0))],
        out_specs=pl.BlockSpec((C, X, NZ, PR, PC), lambda i: (0, 0, i, 0, 0)),
        name="micro_sum",
    )(local)


def adam(scale, total, master, moment1, moment2):
    clipped = scale * total
    m1 = BETA_ONE * moment1 + (1.0 - BETA_ONE) * clipped
    m2 = BETA_TWO * moment2 + (1.0 - BETA_TWO) * clipped * clipped
    first_hat = m1 / (1.0 - BETA_ONE**STEP)
    second_hat = m2 / (1.0 - BETA_TWO**STEP)
    new = master - LEARN_RATE * (
        first_hat / (jnp.sqrt(second_hat) + 1e-08) + DECAY_WEIGHT * master
    )
    return new, m1, m2


def update_kernel(elements, sq_ref, t_ref, ma_ref, m1_ref, m2_ref, em_ref, oma, om1, om2, oem, ow):
    core = lax.axis_index("c")
    sq = jnp.sum(jnp.sum(sq_ref[...], axis=0))
    sq = jnp.full((1, COLS), sq, F32)
    scale = jnp.minimum(1.0, 1.0 / jnp.sqrt(sq / elements + 1e-06))
    new, m1, m2 = adam(scale, from_piece(core, t_ref[...]), ma_ref[...], m1_ref[...], m2_ref[...])
    oma[...] = new
    om1[...] = m1
    om2[...] = m2
    oem[...] = EMA_KEEP * em_ref[...] + (1.0 - EMA_KEEP) * new
    ow[...] = jnp.broadcast_to(to_piece(core, new).astype(BF16)[None], ow.shape)


def place_kernel(w_ref, o_ref):
    for z in range(NZ):
        for x in range(X):
            at = (z * X + x) * GROUP
            a, b = w_ref.at[0, x, z], w_ref.at[1, x, z]
            o_ref[at : at + 8, :PC] = a[0:8]
            o_ref[at : at + 8, PC:] = a[8:16]
            o_ref[at + 16 : at + 24, :PC] = b[0:8]
            o_ref[at + 16 : at + 24, PC:] = b[8:16]
            p, q = a[16:24].astype(F32), b[16:24].astype(F32)
            left = jnp.where(upper(), p, q)
            right = pltpu.roll(jnp.where(upper(), q, p), 4, 0)
            o_ref[at + 8 : at + 16, :PC] = left.astype(BF16)
            o_ref[at + 8 : at + 16, PC:] = right.astype(BF16)


def place(w):
    rows = NZ * X * GROUP
    return pl.pallas_call(
        place_kernel,
        out_shape=jax.ShapeDtypeStruct((STEPS * rows, COLS), BF16),
        grid=(STEPS,),
        in_specs=[pl.BlockSpec((C, X, NZ, PR, PC), lambda i: (0, 0, i, 0, 0))],
        out_specs=pl.BlockSpec((rows, COLS), lambda i: (i, 0)),
        name="place",
    )(w)


def exchange(v, axes):
    return lax.all_to_all(v, axes, split_axis=0, concat_axis=0, tiled=True)


def copies(v, n):
    return jnp.broadcast_to(v[None], (n,) + v.shape)


def shards(grads, master, moment1, moment2, ema):
    local = grads[0]
    elements = local.shape[1] * local.shape[2] * T

    part = micro_sum(local)
    part = jnp.sum(exchange(part, "c"), axis=0)
    part = jnp.sum(exchange(part, "x"), axis=0)
    total = jnp.sum(exchange(part, "z"), axis=0)
    sq = jnp.sum((total * total).reshape(-1, 8, PC), axis=0)
    sq = jnp.sum(exchange(copies(sq, X * C * T), ("x", "c", "t")), axis=0)
    sq = exchange(copies(sq, Z), "z")

    state = jax.ShapeDtypeStruct((ROWS, COLS), F32)
    new_master, new_moment1, new_moment2, new_ema, w = pl.pallas_call(
        lambda *refs: update_kernel(elements, *refs),
        out_shape=(state, state, state, state, jax.ShapeDtypeStruct((Z, PR, PC), BF16)),
        name="update",
    )(sq, total, master, moment1, moment2, ema)

    w = exchange(w, "z")
    w = exchange(copies(w, X), "x")
    w = lax.all_gather(w, "c", axis=0, tiled=False)
    weights = place(w)
    return (new_master, new_moment1, new_moment2, new_ema, weights)


def solution(mesh):
    fine = Mesh(mesh.devices.reshape(Z, X, C, T), ("z", "x", "c", "t"))
    rows = ("z", "x", "c")
    return jax.shard_map(
        shards,
        mesh=fine,
        in_specs=(P(rows, None, None, "t"),) + (P(rows, "t"),) * 4,
        out_specs=(P(rows, "t"),) * 4 + (P(None, "t"),),
        check_vma=False,
    )
```

time: 126 us -> 122 us (0.968)
  Pallas kernels: 9.03 us -> 6.59 us
    pallas_call x2, Pallas kernels: 7.41 us -> 4.88 us  [the longest x1 2.98 us: micro_sum(): pl.pallas_call(sum_kernel, out_shape=jax.ShapeDtypeStruct((C, X, Z, PR, P...]
    all_to_all x8 -> x7, blocking collectives: 109 us -> 108 us  [exchange(): return lax.all_to_all(v, axes, split_axis=0, concat_axis=0, tiled=True)]
where the time goes in v9:
time: 122 us
  blocking collectives  114 us (93%)
  Pallas kernels  6.59 us (5%)
    all_to_all x7, blocking collectives, exchange(): return lax.all_to_all(v, axes, split_axis=0, concat_axis=0, tiled=True)  108 us
    all_gather x1, blocking collectives, shards(): w = lax.all_gather(w, 'c', axis=0, tiled=False)  6.28 us
    pallas_call x1, Pallas kernels, micro_sum(): pl.pallas_call(sum_kernel, out_shape=jax.ShapeDtypeStruct((C, X, Z, PR, P...  2.98 us

profile of v9, /device:TPU:1, one launch (start us, length us, event | category | flops | bytes accessed | tf_op | source)
XLA Modules:
  0.0 121.7 jit_solution(6128424789241730184)
XLA Ops:
  0.6 3.0 %micro_sum.1 = f32[2,4,16,24,128]{4,3,2,1,0:T(8,128)} custom-call(bf16[4,1536,256]{2,1,0:T(8,128)(2,1)} %bitcast.4), custom_call_target="tpu_custom_call" | custom-call | tf_op jit(solution)/shard_map/micro_sum/pallas_call | solution.py:66
  3.6 12.7 %all_to_all.35 = f32[2,4,16,24,128]{4,3,2,1,0:T(8,128)S(1)} all-to-all(f32[2,4,16,24,128]{4,3,2,1,0:T(8,128)} %micro_sum.1), channel_id=1, replica_groups=mesh['z'=16,'x'=4,'c'=2,'t'=4] {'c'}, dimensions={0} | all-to-all | bytes 3145728 | tf_op jit(solution)/shard_map/all_to_all | solution.py:130
  16.3 0.2 reduce_sum.45
  16.4 14.4 %all_to_all.36 = f32[4,16,24,128]{3,2,1,0:T(8,128)S(1)} all-to-all(f32[4,16,24,128]{3,2,1,0:T(8,128)S(1)} %reduce_sum.45), channel_id=1, replica_groups=mesh['z'=16,'x'=4,'c'=2,'t'=4] {'x'}, dimensions={0} | all-to-all | bytes 1572864 | tf_op jit(solution)/shard_map/all_to_all | solution.py:130
  30.9 22.5 %all_to_all.37 = f32[16,24,128]{2,1,0:T(8,128)S(1)} all-to-all(f32[16,24,128]{2,1,0:T(8,128)S(1)} %reduce_sum.46), channel_id=1, replica_groups=mesh['z'=16,'x'=4,'c'=2,'t'=4] {'z'}, dimensions={0} | all-to-all | bytes 393216 | tf_op jit(solution)/shard_map/all_to_all | solution.py:130
  53.4 0.0 copy-start
  53.5 17.9 %all_to_all.38 = f32[32,8,128]{2,1,0:T(8,128)S(1)} all-to-all(f32[32,8,128]{2,1,0:T(8,128)S(1)} %broadcast_in_dim.6), channel_id=1, replica_groups=mesh['z'=16,'x'=4,'c'=2,'t'=4] {'x','c','t'}, dimensions={0} | all-to-all | bytes 262144 | tf_op jit(solution)/shard_map/all_to_all | solution.py:130
  71.4 15.8 %all_to_all.39.refs_0_ = f32[16,8,128]{2,1,0:T(8,128)} all-to-all(f32[16,8,128]{2,1,0:T(8,128)S(1)} %broadcast_in_dim.7), channel_id=1, replica_groups=mesh['z'=16,'x'=4,'c'=2,'t'=4] {'z'}, dimensions={0} | all-to-all | bytes 131072 | tf_op jit(solution)/shard_map/all_to_all | solution.py:130
  87.3 0.0 copy-done
  87.3 1.7 %update.1 = (f32[12,256]{1,0:T(8,128)}, f32[12,256]{1,0:T(8,128)}, f32[12,256]{1,0:T(8,128)}, f32[12,256]{1,0:T(8,128)}, bf16[16,24,128]{2,1,0:T(8,128)(2,1)}) custom-call(f32[16,8,128]{2,1,0:T(8,128)} %all_to_all.39.refs_0_, f32[24,128]{1,0:T(8,128)} %copy-done, f32[12,256]{1,0:T(8,128)} %refs_2_.1, f32[12,256]{1,0:T(8,128)} %refs_3_.1, f32[12,256]{1,0:T(8,128)} %refs_4_.1, ...), custom_call_target="tpu_custom_call" | custom-call | tf_op jit(solution)/shard_map/update/pallas_call | solution.py:150
  89.0 15.9 %all_to_all.40 = bf16[16,24,128]{2,1,0:T(8,128)(2,1)S(1)} all-to-all(bf16[16,24,128]{2,1,0:T(8,128)(2,1)} %get-tuple-element.14), channel_id=1, replica_groups=mesh['z'=16,'x'=4,'c'=2,'t'=4] {'z'}, dimensions={0} | all-to-all | bytes 196608 | tf_op jit(solution)/shard_map/all_to_all | solution.py:130
  104.8 0.1 broadcast_in_dim.8
  104.9 8.6 %all_to_all.41 = bf16[4,16,24,128]{3,2,1,0:T(8,128)(2,1)S(1)} all-to-all(bf16[4,16,24,128]{3,2,1,0:T(8,128)(2,1)S(1)} %broadcast_in_dim.8), channel_id=1, replica_groups=mesh['z'=16,'x'=4,'c'=2,'t'=4] {'x'}, dimensions={0} | all-to-all | bytes 786432 | tf_op jit(solution)/shard_map/all_to_all | solution.py:130
  113.5 6.3 %all-gather = bf16[8,16,24,128]{3,2,1,0:T(8,128)(2,1)} all-gather(bf16[4,16,24,128]{3,2,1,0:T(8,128)(2,1)S(1)} %all_to_all.41), channel_id=2, replica_groups=mesh['z'=16,'x'=4,'c'=2,'t'=4] {'c'}, dimensions={0}, use_global_device_ids=true | all-gather | bytes 1179648 | tf_op jit(solution)/shard_map/all_gather | solution.py:158
  119.8 1.9 %place.1 = bf16[1536,256]{1,0:T(8,128)(2,1)} custom-call(bf16[2,4,16,24,128]{4,3,2,1,0:T(8,128)(2,1)} %bitcast.5), custom_call_target="tpu_custom_call" | custom-call | tf_op jit(solution)/shard_map/place/pallas_call | solution.py:119
  (6 shorter events, 0.1 us)
Async XLA Ops:
  53.4 33.8 %copy-start = (f32[24,128]{1,0:T(8,128)}, f32[24,128]{1,0:T(8,128)S(1)}, u32[]{:S(2)}) copy-start(f32[24,128]{1,0:T(8,128)S(1)} %reduce_sum.47.refs_1_) | copy-start | bytes 36868

commit v10 on v9

--- a/solution.py
+++ b/solution.py
@@ -21,6 +21,9 @@
 
 F32 = jnp.float32
 BF16 = jnp.bfloat16
+F16 = jnp.float16
+
+LIFT = 8.0
 
 
 def upper():
@@ -141,7 +144,8 @@
     part = micro_sum(local)
     part = jnp.sum(exchange(part, "c"), axis=0)
     part = jnp.sum(exchange(part, "x"), axis=0)
-    total = jnp.sum(exchange(part, "z"), axis=0)
+    part = exchange((part * LIFT).astype(F16), "z")
+    total = jnp.sum(part.astype(F32), axis=0) * (1.0 / LIFT)
     sq = jnp.sum((total * total).reshape(-1, 8, PC), axis=0)
     sq = jnp.sum(exchange(copies(sq, X * C * T), ("x", "c", "t")), axis=0)
     sq = exchange(copies(sq, Z), "z")

time: 122 us -> 120 us (0.984)
  blocking collectives: 114 us -> 95.5 us
  waiting for transfers between devices: 0 us -> 11 us
  starting transfers between devices: 0 us -> 3.5 us
  local copies, waits for them, and re-layouts: 0.08 us -> 1.32 us
    all_to_all x7 -> x6, blocking collectives: 108 us -> 89.3 us  [exchange(): return lax.all_to_all(v, axes, split_axis=0, concat_axis=0, tiled=True)]
    all_to_all x0 -> x1, waiting for transfers between devices: none -> 11 us  [exchange(): return lax.all_to_all(v, axes, split_axis=0, concat_axis=0, tiled=True)]
    all_to_all x0 -> x1, starting transfers between devices: none -> 3.5 us  [exchange(): return lax.all_to_all(v, axes, split_axis=0, concat_axis=0, tiled=True)]
  transfers between devices with their start and end apart: 0 -> 1, of which waited for: 0 -> 1; matrix products, arithmetic and copies ran while one was open for 0% -> 1% of each run, Pallas kernels for 0% -> 0%
where the time goes in v10:
time: 120 us; the launch traced here: 119 us
  blocking collectives  95.5 us (80%)
  waiting for transfers between devices  11 us (9%)
  Pallas kernels  6.59 us (5%)
  starting transfers between devices  3.5 us (3%)
  local copies, waits for them, and re-layouts  1.32 us (1%)
    all_to_all x6, blocking collectives, exchange(): return lax.all_to_all(v, axes, split_axis=0, concat_axis=0, tiled=True)  89.3 us
    all_to_all x1, waiting for transfers between devices, exchange(): return lax.all_to_all(v, axes, split_axis=0, concat_axis=0, tiled=True)  11 us
    all_gather x1, blocking collectives, shards(): w = lax.all_gather(w, 'c', axis=0, tiled=False)  6.15 us
    all_to_all x1, starting transfers between devices, exchange(): return lax.all_to_all(v, axes, split_axis=0, concat_axis=0, tiled=True)  3.5 us
    pallas_call x1, Pallas kernels, micro_sum(): pl.pallas_call(sum_kernel, out_shape=jax.ShapeDtypeStruct((C, X, Z, PR, P...  2.98 us
  transfers between devices with their start and end apart: 1, of which 1 were waited for; matrix products, arithmetic and copies ran while one was open for 1% of the time, Pallas kernels for 0%

profile of v10, /device:TPU:1, one launch (start us, length us, event | category | flops | bytes accessed | tf_op | source)
XLA Modules:
  0.0 119.5 jit_solution(5288138014379563742)
XLA Ops:
  0.6 3.0 %micro_sum.1 = f32[2,4,16,24,128]{4,3,2,1,0:T(8,128)} custom-call(bf16[4,1536,256]{2,1,0:T(8,128)(2,1)} %bitcast.4), custom_call_target="tpu_custom_call" | custom-call | tf_op jit(solution)/shard_map/micro_sum/pallas_call | solution.py:69
  3.6 12.7 %all_to_all.35 = f32[2,4,16,24,128]{4,3,2,1,0:T(8,128)S(1)} all-to-all(f32[2,4,16,24,128]{4,3,2,1,0:T(8,128)} %micro_sum.1), channel_id=1, replica_groups=mesh['z'=16,'x'=4,'c'=2,'t'=4] {'c'}, dimensions={0} | all-to-all | bytes 3145728 | tf_op jit(solution)/shard_map/all_to_all | solution.py:133
  16.3 0.2 reduce_sum.45
  16.4 14.4 %all_to_all.36 = f32[4,16,24,128]{3,2,1,0:T(8,128)S(1)} all-to-all(f32[4,16,24,128]{3,2,1,0:T(8,128)S(1)} %reduce_sum.45), channel_id=1, replica_groups=mesh['z'=16,'x'=4,'c'=2,'t'=4] {'x'}, dimensions={0} | all-to-all | bytes 1572864 | tf_op jit(solution)/shard_map/all_to_all | solution.py:133
  31.0 22.0 %all_to_all.37 = f16[16,24,128]{2,1,0:T(8,128)(2,1)S(1)} all-to-all(f16[16,24,128]{2,1,0:T(8,128)(2,1)S(1)} %multiply_convert_fusion), channel_id=1, replica_groups=mesh['z'=16,'x'=4,'c'=2,'t'=4] {'z'}, dimensions={0} | all-to-all | bytes 196608 | tf_op jit(solution)/shard_map/all_to_all | solution.py:133
  53.0 15.9 %all_to_all.38 = f32[32,8,128]{2,1,0:T(8,128)S(1)} all-to-all(f32[32,8,128]{2,1,0:T(8,128)S(1)} %broadcast_in_dim.6), channel_id=1, replica_groups=mesh['z'=16,'x'=4,'c'=2,'t'=4] {'x','c','t'}, dimensions={0} | all-to-all | bytes 262144 | tf_op jit(solution)/shard_map/all_to_all | solution.py:133
  68.9 0.6 broadcast_in_dim.7
  69.5 3.5 %all-to-all-start.4 = ((f32[16,8,128]{2,1,0:T(8,128)}), f32[16,8,128]{2,1,0:T(8,128)S(1)}, u32[]{:S(2)}, u32[]{:S(2)}) async-start(f32[16,8,128]{2,1,0:T(8,128)} %broadcast_in_dim.7), calls=%async_computation.4 | async-start | bytes 131072 | tf_op jit(solution)/shard_map/all_to_all | solution.py:133
  73.0 0.6 broadcast_multiply_fusion.refs_1_
  73.6 11.0 %all-to-all-done.4.refs_0_ = f32[16,8,128]{2,1,0:T(8,128)S(1)} async-done(((f32[16,8,128]{2,1,0:T(8,128)}), f32[16,8,128]{2,1,0:T(8,128)S(1)}, u32[]{:S(2)}, u32[]{:S(2)}) %all-to-all-start.4) | async-done | bytes 65568 | tf_op jit(solution)/shard_map/all_to_all | solution.py:133
  84.7 0.0 copy-start
  84.7 0.6 copy-done
  85.3 1.7 %update.1 = (f32[12,256]{1,0:T(8,128)}, f32[12,256]{1,0:T(8,128)}, f32[12,256]{1,0:T(8,128)}, f32[12,256]{1,0:T(8,128)}, bf16[16,24,128]{2,1,0:T(8,128)(2,1)}) custom-call(f32[16,8,128]{2,1,0:T(8,128)} %copy-done, f32[24,128]{1,0:T(8,128)} %broadcast_multiply_fusion.refs_1_, f32[12,256]{1,0:T(8,128)} %refs_2_.1, f32[12,256]{1,0:T(8,128)} %refs_3_.1, ...), custom_call_target="tpu_custom_call" | custom-call | tf_op jit(solution)/shard_map/update/pallas_call | solution.py:154
  87.0 15.8 %all_to_all.39 = bf16[16,24,128]{2,1,0:T(8,128)(2,1)S(1)} all-to-all(bf16[16,24,128]{2,1,0:T(8,128)(2,1)} %get-tuple-element.14), channel_id=1, replica_groups=mesh['z'=16,'x'=4,'c'=2,'t'=4] {'z'}, dimensions={0} | all-to-all | bytes 196608 | tf_op jit(solution)/shard_map/all_to_all | solution.py:133
  102.8 0.1 broadcast_in_dim.8
  102.8 8.6 %all_to_all.40 = bf16[4,16,24,128]{3,2,1,0:T(8,128)(2,1)S(1)} all-to-all(bf16[4,16,24,128]{3,2,1,0:T(8,128)(2,1)S(1)} %broadcast_in_dim.8), channel_id=1, replica_groups=mesh['z'=16,'x'=4,'c'=2,'t'=4] {'x'}, dimensions={0} | all-to-all | bytes 786432 | tf_op jit(solution)/shard_map/all_to_all | solution.py:133
  111.4 6.2 %all-gather = bf16[8,16,24,128]{3,2,1,0:T(8,128)(2,1)} all-gather(bf16[4,16,24,128]{3,2,1,0:T(8,128)(2,1)S(1)} %all_to_all.40), channel_id=2, replica_groups=mesh['z'=16,'x'=4,'c'=2,'t'=4] {'c'}, dimensions={0}, use_global_device_ids=true | all-gather | bytes 1179648 | tf_op jit(solution)/shard_map/all_gather | solution.py:162
  117.6 1.9 %place.1 = bf16[1536,256]{1,0:T(8,128)(2,1)} custom-call(bf16[2,4,16,24,128]{4,3,2,1,0:T(8,128)(2,1)} %bitcast.5), custom_call_target="tpu_custom_call" | custom-call | tf_op jit(solution)/shard_map/place/pallas_call | solution.py:122
  (6 shorter events, 0.1 us)
Async XLA Ops:
  69.5 15.1 %all-to-all-start.4 = ((f32[16,8,128]{2,1,0:T(8,128)}), f32[16,8,128]{2,1,0:T(8,128)S(1)}, u32[]{:S(2)}, u32[]{:S(2)}) async-start(f32[16,8,128]{2,1,0:T(8,128)} %broadcast_in_dim.7), calls=%async_computation.4 | async-start | bytes 131072 | tf_op jit(solution)/shard_map/all_to_all | solution.py:133
  84.7 0.6 copy-start

commit v11 on v9

--- a/solution.py
+++ b/solution.py
@@ -18,6 +18,7 @@
 GROUP = C * ROWS
 STEPS = 2
 NZ = Z // STEPS
+SUM_Z = 4
 
 F32 = jnp.float32
 BF16 = jnp.bfloat16
@@ -46,7 +47,8 @@
 
 
 def sum_kernel(g_ref, o_ref):
-    for z in range(NZ):
+    base = pl.program_id(0) * SUM_Z
+    for z in range(SUM_Z):
         for pair in range(X // 2):
             at = (z * X + 2 * pair) * GROUP
             v = g_ref[0, at : at + 2 * GROUP, :].astype(F32)
@@ -55,20 +57,20 @@
             for k in range(2):
                 first, both, last = [v[k * GROUP + j : k * GROUP + j + 8] for j in (0, 8, 16)]
                 for core, own in ((0, first), (1, last)):
-                    o = o_ref.at[core, 2 * pair + k, z]
+                    o = o_ref.at[core, 2 * pair + k, base + z]
                     o[0:8] = own[:, :PC]
                     o[8:16] = own[:, PC:]
                     o[16:24] = shared_tile(core, both[:, :PC], both[:, PC:])
 
 
 def micro_sum(local):
-    rows = NZ * X * GROUP
+    rows = SUM_Z * X * GROUP
     return pl.pallas_call(
         sum_kernel,
-        out_shape=jax.ShapeDtypeStruct((C, X, Z, PR, PC), F32),
-        grid=(STEPS,),
+        out_shape=pltpu.VMEM((C, X, Z, PR, PC), F32),
+        grid=(Z // SUM_Z,),
         in_specs=[pl.BlockSpec((local.shape[0], rows, COLS), lambda i: (0, i, 0))],
-        out_specs=pl.BlockSpec((C, X, NZ, PR, PC), lambda i: (0, 0, i, 0, 0)),
+        out_specs=pl.BlockSpec(memory_space=pltpu.VMEM),
         name="micro_sum",
     )(local)
 
@@ -99,10 +101,11 @@
 
 
 def place_kernel(w_ref, o_ref):
+    base = pl.program_id(0) * NZ
     for z in range(NZ):
         for x in range(X):
             at = (z * X + x) * GROUP
-            a, b = w_ref.at[0, x, z], w_ref.at[1, x, z]
+            a, b = w_ref.at[0, x, base + z], w_ref.at[1, x, base + z]
             o_ref[at : at + 8, :PC] = a[0:8]
             o_ref[at : at + 8, PC:] = a[8:16]
             o_ref[at + 16 : at + 24, :PC] = b[0:8]
@@ -120,14 +123,18 @@
         place_kernel,
         out_shape=jax.ShapeDtypeStruct((STEPS * rows, COLS), BF16),
         grid=(STEPS,),
-        in_specs=[pl.BlockSpec((C, X, NZ, PR, PC), lambda i: (0, 0, i, 0, 0))],
+        in_specs=[pl.BlockSpec(memory_space=pltpu.VMEM)],
         out_specs=pl.BlockSpec((rows, COLS), lambda i: (i, 0)),
         name="place",
-    )(w)
+    )(*near(w))
 
 
 def exchange(v, axes):
     return lax.all_to_all(v, axes, split_axis=0, concat_axis=0, tiled=True)
+
+
+def near(*arrays):
+    return [pltpu.with_memory_space_constraint(v, pltpu.VMEM) for v in arrays]
 
 
 def copies(v, n):
@@ -146,12 +153,15 @@
     sq = jnp.sum(exchange(copies(sq, X * C * T), ("x", "c", "t")), axis=0)
     sq = exchange(copies(sq, Z), "z")
 
-    state = jax.ShapeDtypeStruct((ROWS, COLS), F32)
+    state = pltpu.VMEM((ROWS, COLS), F32)
+    whole = pl.BlockSpec(memory_space=pltpu.VMEM)
     new_master, new_moment1, new_moment2, new_ema, w = pl.pallas_call(
         lambda *refs: update_kernel(elements, *refs),
-        out_shape=(state, state, state, state, jax.ShapeDtypeStruct((Z, PR, PC), BF16)),
+        out_shape=(state, state, state, state, pltpu.VMEM((Z, PR, PC), BF16)),
+        in_specs=[whole] * 6,
+        out_specs=(whole,) * 5,
         name="update",
-    )(sq, total, master, moment1, moment2, ema)
+    )(*near(sq, total, master, moment1, moment2, ema))
 
     w = exchange(w, "z")
     w = exchange(copies(w, X), "x")

time: 122 us -> 120 us (0.984)
  blocking collectives: 114 us -> 104 us
  waiting for transfers between devices: 0 us -> 3.77 us
  starting transfers between devices: 0 us -> 3.46 us
  local copies, waits for them, and re-layouts: 0.08 us -> 3.26 us
  Pallas kernels: 6.59 us -> 3.89 us
    all_to_all x7 -> x6, blocking collectives: 108 us -> 97.8 us  [exchange(): return lax.all_to_all(v, axes, split_axis=0, concat_axis=0, tiled=True)]
    all_to_all x0 -> x1, waiting for transfers between devices: none -> 3.77 us  [exchange(): return lax.all_to_all(v, axes, split_axis=0, concat_axis=0, tiled=True)]
    all_to_all x0 -> x1, starting transfers between devices: none -> 3.46 us  [exchange(): return lax.all_to_all(v, axes, split_axis=0, concat_axis=0, tiled=True)]
    unnamed x2 -> x12, local copies, waits for them, and re-layouts: 0.01 us -> 2.45 us
    pallas_call x1, Pallas kernels: 1.71 us -> 0.18 us  [shards(): pl.pallas_call(lambda *refs: update_kernel(elements, *refs), out_shape=(s...]
  transfers between devices with their start and end apart: 0 -> 1, of which waited for: 0 -> 1; matrix products, arithmetic and copies ran while one was open for 0% -> 2% of each run, Pallas kernels for 0% -> 0%
where the time goes in v11:
time: 120 us; the launch traced here: 119 us
  blocking collectives  104 us (87%)
  Pallas kernels  3.89 us (3%)
  waiting for transfers between devices  3.77 us (3%)
  starting transfers between devices  3.46 us (3%)
  local copies, waits for them, and re-layouts  3.26 us (3%)
    all_to_all x6, blocking collectives, exchange(): return lax.all_to_all(v, axes, split_axis=0, concat_axis=0, tiled=True)  97.8 us
    all_gather x1, blocking collectives, shards(): w = lax.all_gather(w, 'c', axis=0, tiled=False)  5.92 us
    all_to_all x1, waiting for transfers between devices, exchange(): return lax.all_to_all(v, axes, split_axis=0, concat_axis=0, tiled=True)  3.77 us
    all_to_all x1, starting transfers between devices, exchange(): return lax.all_to_all(v, axes, split_axis=0, concat_axis=0, tiled=True)  3.46 us
    pallas_call x1, Pallas kernels, micro_sum(): pl.pallas_call(sum_kernel, out_shape=pltpu.VMEM((C, X, Z, PR, PC), F32),...  2.8 us
    unnamed x12, local copies, waits for them, and re-layouts  2.45 us
  transfers between devices with their start and end apart: 1, of which 1 were waited for; matrix products, arithmetic and copies ran while one was open for 2% of the time, Pallas kernels for 0%

profile of v11, /device:TPU:1, one launch (start us, length us, event | category | flops | bytes accessed | tf_op | source)
XLA Modules:
  0.0 119.1 jit_solution(1734828196888812274)
XLA Ops:
  0.6 2.8 %micro_sum.1 = f32[2,4,16,24,128]{4,3,2,1,0:T(8,128)S(1)} custom-call(bf16[4,1536,256]{2,1,0:T(8,128)(2,1)} %bitcast.5), custom_call_target="tpu_custom_call" | custom-call | tf_op jit(solution)/shard_map/micro_sum/pallas_call | solution.py:68
  3.4 11.5 %all_to_all.35 = f32[2,4,16,24,128]{4,3,2,1,0:T(8,128)S(1)} all-to-all(f32[2,4,16,24,128]{4,3,2,1,0:T(8,128)S(1)} %micro_sum.1), channel_id=1, replica_groups=mesh['z'=16,'x'=4,'c'=2,'t'=4] {'c'}, dimensions={0} | all-to-all | bytes 3145728 | tf_op jit(solution)/shard_map/all_to_all | solution.py:133
  14.9 0.2 reduce_sum.45
  15.1 0.0 copy-start
  15.1 0.0 copy-start.1
  15.1 0.0 copy-start.2
  15.1 0.0 copy-start.3
  15.2 14.6 %all_to_all.36 = f32[4,16,24,128]{3,2,1,0:T(8,128)S(1)} all-to-all(f32[4,16,24,128]{3,2,1,0:T(8,128)S(1)} %reduce_sum.45), channel_id=1, replica_groups=mesh['z'=16,'x'=4,'c'=2,'t'=4] {'x'}, dimensions={0} | all-to-all | bytes 1572864 | tf_op jit(solution)/shard_map/all_to_all | solution.py:133
  29.8 22.5 %all_to_all.37 = f32[16,24,128]{2,1,0:T(8,128)S(1)} all-to-all(f32[16,24,128]{2,1,0:T(8,128)S(1)} %reduce_sum.46), channel_id=1, replica_groups=mesh['z'=16,'x'=4,'c'=2,'t'=4] {'z'}, dimensions={0} | all-to-all | bytes 393216 | tf_op jit(solution)/shard_map/all_to_all | solution.py:133
  52.3 17.9 %all_to_all.38 = f32[32,8,128]{2,1,0:T(8,128)S(1)} all-to-all(f32[32,8,128]{2,1,0:T(8,128)S(1)} %broadcast_in_dim.6), channel_id=1, replica_groups=mesh['z'=16,'x'=4,'c'=2,'t'=4] {'x','c','t'}, dimensions={0} | all-to-all | bytes 262144 | tf_op jit(solution)/shard_map/all_to_all | solution.py:133
  70.3 15.7 %all_to_all.39.refs_0_ = f32[16,8,128]{2,1,0:T(8,128)S(1)} all-to-all(f32[16,8,128]{2,1,0:T(8,128)S(1)} %broadcast_in_dim.7), channel_id=1, replica_groups=mesh['z'=16,'x'=4,'c'=2,'t'=4] {'z'}, dimensions={0} | all-to-all | bytes 131072 | tf_op jit(solution)/shard_map/all_to_all | solution.py:133
  86.0 0.0 copy-done
  86.0 0.0 copy-done.1
  86.0 0.0 copy-done.2
  86.0 0.0 copy-done.3
  86.0 0.2 update.1
  86.2 15.6 %all_to_all.40 = bf16[16,24,128]{2,1,0:T(8,128)(2,1)S(1)} all-to-all(bf16[16,24,128]{2,1,0:T(8,128)(2,1)S(1)} %get-tuple-element.14), channel_id=1, replica_groups=mesh['z'=16,'x'=4,'c'=2,'t'=4] {'z'}, dimensions={0} | all-to-all | bytes 196608 | tf_op jit(solution)/shard_map/all_to_all | solution.py:133
  101.8 0.8 broadcast_in_dim.8
  102.6 3.5 %all-to-all-start.6 = ((bf16[4,16,24,128]{3,2,1,0:T(8,128)(2,1)}), bf16[4,16,24,128]{3,2,1,0:T(8,128)(2,1)S(1)}, u32[]{:S(2)}, u32[]{:S(2)}) async-start(bf16[4,16,24,128]{3,2,1,0:T(8,128)(2,1)} %broadcast_in_dim.8), calls=%async_computation.6 | async-start | bytes 786432 | tf_op jit(solution)/shard_map/all_to_all | solution.py:133
  106.1 0.6 copy.10
  106.7 0.6 copy.11
  107.3 0.6 copy.12
  107.9 0.6 copy.13
  108.5 3.8 %all-to-all-done.6 = bf16[4,16,24,128]{3,2,1,0:T(8,128)(2,1)S(1)} async-done(((bf16[4,16,24,128]{3,2,1,0:T(8,128)(2,1)}), bf16[4,16,24,128]{3,2,1,0:T(8,128)(2,1)S(1)}, u32[]{:S(2)}, u32[]{:S(2)}) %all-to-all-start.6) | async-done | bytes 393248 | tf_op jit(solution)/shard_map/all_to_all | solution.py:133
  112.3 5.9 %all-gather = bf16[8,16,24,128]{3,2,1,0:T(8,128)(2,1)S(1)} all-gather(bf16[4,16,24,128]{3,2,1,0:T(8,128)(2,1)S(1)} %all-to-all-done.6), channel_id=2, replica_groups=mesh['z'=16,'x'=4,'c'=2,'t'=4] {'c'}, dimensions={0}, use_global_device_ids=true | all-gather | bytes 1179648 | tf_op jit(solution)/shard_map/all_gather | solution.py:168
  118.2 0.9 place.1
  (6 shorter events, 0.1 us)
Async XLA Ops:
  15.1 70.9 %copy-start = (f32[12,256]{1,0:T(8,128)S(1)}, f32[12,256]{1,0:T(8,128)}, u32[]{:S(2)}) copy-start(f32[12,256]{1,0:T(8,128)} %refs_2_.1) | copy-start | bytes 36868
  15.1 70.9 %copy-start.1 = (f32[12,256]{1,0:T(8,128)S(1)}, f32[12,256]{1,0:T(8,128)}, u32[]{:S(2)}) copy-start(f32[12,256]{1,0:T(8,128)} %refs_3_.1) | copy-start | bytes 36868
  15.1 70.9 %copy-start.2 = (f32[12,256]{1,0:T(8,128)S(1)}, f32[12,256]{1,0:T(8,128)}, u32[]{:S(2)}) copy-start(f32[12,256]{1,0:T(8,128)} %refs_4_.1) | copy-start | bytes 36868
  15.1 70.9 %copy-start.3 = (f32[12,256]{1,0:T(8,128)S(1)}, f32[12,256]{1,0:T(8,128)}, u32[]{:S(2)}) copy-start(f32[12,256]{1,0:T(8,128)} %refs_5_.1) | copy-start | bytes 36868
  102.6 9.7 %all-to-all-start.6 = ((bf16[4,16,24,128]{3,2,1,0:T(8,128)(2,1)}), bf16[4,16,24,128]{3,2,1,0:T(8,128)(2,1)S(1)}, u32[]{:S(2)}, u32[]{:S(2)}) async-start(bf16[4,16,24,128]{3,2,1,0:T(8,128)(2,1)} %broadcast_in_dim.8), calls=%async_computation.6 | async-start | bytes 786432 | tf_op jit(solution)/shard_map/all_to_all | solution.py:133

commit v12 on v11

--- a/solution.py
+++ b/solution.py
@@ -46,32 +46,38 @@
     return jnp.where(core == 0, zero, one)
 
 
-def sum_kernel(g_ref, o_ref):
+def half_body(core, g_ref, o_ref):
     base = pl.program_id(0) * SUM_Z
     for z in range(SUM_Z):
-        for pair in range(X // 2):
-            at = (z * X + 2 * pair) * GROUP
-            v = g_ref[0, at : at + 2 * GROUP, :].astype(F32)
+        for x in range(X):
+            at = (z * X + x) * GROUP + 8 * core
+            v = g_ref[0, at : at + 16, :].astype(F32)
             for m in range(1, g_ref.shape[0]):
-                v = v + g_ref[m, at : at + 2 * GROUP, :].astype(F32)
-            for k in range(2):
-                first, both, last = [v[k * GROUP + j : k * GROUP + j + 8] for j in (0, 8, 16)]
-                for core, own in ((0, first), (1, last)):
-                    o = o_ref.at[core, 2 * pair + k, base + z]
-                    o[0:8] = own[:, :PC]
-                    o[8:16] = own[:, PC:]
-                    o[16:24] = shared_tile(core, both[:, :PC], both[:, PC:])
+                v = v + g_ref[m, at : at + 16, :].astype(F32)
+            own, both = (v[0:8], v[8:16]) if core == 0 else (v[8:16], v[0:8])
+            o = o_ref.at[x, base + z]
+            o[0:8] = own[:, :PC]
+            o[8:16] = own[:, PC:]
+            o[16:24] = shared_tile(core, both[:, :PC], both[:, PC:])
 
 
-def micro_sum(local):
+def half_kernel(own, g_ref, o_ref):
+    me = lax.axis_index("c")
+    core = me if own else 1 - me
+    for k in range(C):
+        pl.when(core == k)(lambda k=k: half_body(k, g_ref, o_ref))
+
+
+def half_sum(local, own):
     rows = SUM_Z * X * GROUP
     return pl.pallas_call(
-        sum_kernel,
-        out_shape=pltpu.VMEM((C, X, Z, PR, PC), F32),
+        lambda *refs: half_kernel(own, *refs),
+        out_shape=pltpu.VMEM((X, Z, PR, PC), F32),
         grid=(Z // SUM_Z,),
         in_specs=[pl.BlockSpec((local.shape[0], rows, COLS), lambda i: (0, i, 0))],
         out_specs=pl.BlockSpec(memory_space=pltpu.VMEM),
-        name="micro_sum",
+        cost_estimate=pl.CostEstimate(flops=2_000_000, bytes_accessed=4_000_000, transcendentals=0),
+        name="own_half" if own else "other_half",
     )(local)
 
 
@@ -145,11 +151,11 @@
     local = grads[0]
     elements = local.shape[1] * local.shape[2] * T
 
-    part = micro_sum(local)
-    part = jnp.sum(exchange(part, "c"), axis=0)
+    other = lax.ppermute(half_sum(local, False), "c", [(0, 1), (1, 0)])
+    part = half_sum(local, True) + other
     part = jnp.sum(exchange(part, "x"), axis=0)
     total = jnp.sum(exchange(part, "z"), axis=0)
-    sq = jnp.sum((total * total).reshape(-1, 8, PC), axis=0)
+    sq = jnp.sum(total * total, axis=0, keepdims=True)
     sq = jnp.sum(exchange(copies(sq, X * C * T), ("x", "c", "t")), axis=0)
     sq = exchange(copies(sq, Z), "z")
 

time: 120 us -> 119 us (level)
  blocking collectives: 104 us -> 91.5 us
  starting transfers between devices: 3.46 us -> 12.2 us
  Pallas kernels: 3.89 us -> 6.58 us
    all_to_all x6 -> x5, blocking collectives: 97.8 us -> 84.7 us  [exchange(): return lax.all_to_all(v, axes, split_axis=0, concat_axis=0, tiled=True)]
    ppermute x0 -> x1, starting transfers between devices: none -> 8.78 us  [shards(): other = lax.ppermute(half_sum(local, False), 'c', [(0, 1), (1, 0)])]
    pallas_call x1 -> x2, Pallas kernels: 2.8 us -> 5.49 us  [half_sum(): pl.pallas_call(lambda *refs: half_kernel(own, *refs), out_shape=pltpu.VME...]
  transfers between devices with their start and end apart: 1 -> 2, of which waited for: 1 -> 1; matrix products, arithmetic and copies ran while one was open for 2% -> 2% of each run, Pallas kernels for 0% -> 2%
where the time goes in v12:
time: 119 us; the launch traced here: 118 us
  blocking collectives  91.5 us (77%)
  starting transfers between devices  12.2 us (10%)
  Pallas kernels  6.58 us (6%)
  waiting for transfers between devices  3.77 us (3%)
  local copies, waits for them, and re-layouts  3.27 us (3%)
    all_to_all x5, blocking collectives, exchange(): return lax.all_to_all(v, axes, split_axis=0, concat_axis=0, tiled=True)  84.7 us
    ppermute x1, starting transfers between devices, shards(): other = lax.ppermute(half_sum(local, False), 'c', [(0, 1), (1, 0)])  8.78 us
    all_gather x1, blocking collectives, shards(): w = lax.all_gather(w, 'c', axis=0, tiled=False)  6.77 us
    pallas_call x2, Pallas kernels, half_sum(): pl.pallas_call(lambda *refs: half_kernel(own, *refs), out_shape=pltpu.VME...  5.49 us
    all_to_all x1, waiting for transfers between devices, exchange(): return lax.all_to_all(v, axes, split_axis=0, concat_axis=0, tiled=True)  3.77 us
    all_to_all x1, starting transfers between devices, exchange(): return lax.all_to_all(v, axes, split_axis=0, concat_axis=0, tiled=True)  3.46 us
    unnamed x12, local copies, waits for them, and re-layouts  2.45 us
  transfers between devices with their start and end apart: 2, of which 1 were waited for; matrix products, arithmetic and copies ran while one was open for 2% of the time, Pallas kernels for 2%

profile of v12, /device:TPU:1, one launch (start us, length us, event | category | flops | bytes accessed | tf_op | source)
XLA Modules:
  0.0 118.3 jit_solution(3146191587785661019)
XLA Ops:
  0.6 2.7 %other_half.1 = f32[4,16,24,128]{3,2,1,0:T(8,128)S(1)} custom-call(bf16[4,1536,256]{2,1,0:T(8,128)(2,1)} %bitcast.4), custom_call_target="tpu_custom_call" | custom-call | flops 2000000 | bytes 4000000 | tf_op jit(solution)/shard_map/other_half/pallas_call | solution.py:73
  3.4 8.8 %collective-permute-start = (f32[4,16,24,128]{3,2,1,0:T(8,128)S(1)}, f32[4,16,24,128]{3,2,1,0:T(8,128)S(1)}, u32[]{:S(2)}, u32[]{:S(2)}) collective-permute-start(f32[4,16,24,128]{3,2,1,0:T(8,128)S(1)} %other_half.1), channel_id=1, source_target_pairs={{0,4},{4,0},{1,5},{5,1},{2,6},{6,2},{3,7},{7,3},{8,12},{12,8},{9,1... | collective-permute-start | bytes 2359304 | tf_op jit(solution)/shard_map/ppermute | solution.py:154
  12.2 2.7 %own_half.1 = f32[4,16,24,128]{3,2,1,0:T(8,128)S(1)} custom-call(bf16[4,1536,256]{2,1,0:T(8,128)(2,1)} %bitcast.5), custom_call_target="tpu_custom_call" | custom-call | flops 2000000 | bytes 4000000 | tf_op jit(solution)/shard_map/own_half/pallas_call | solution.py:73
  14.9 0.0 copy-start
  14.9 0.0 copy-start.1
  14.9 0.0 copy-start.2
  15.0 0.0 copy-start.3
  15.0 0.0 collective-permute-done
  15.0 0.1 add.3
  15.1 14.6 %all_to_all.30 = f32[4,16,24,128]{3,2,1,0:T(8,128)S(1)} all-to-all(f32[4,16,24,128]{3,2,1,0:T(8,128)S(1)} %add.3), channel_id=1, replica_groups=mesh['z'=16,'x'=4,'c'=2,'t'=4] {'x'}, dimensions={0} | all-to-all | bytes 1572864 | tf_op jit(solution)/shard_map/all_to_all | solution.py:139
  29.7 23.1 %all_to_all.31 = f32[16,24,128]{2,1,0:T(8,128)S(1)} all-to-all(f32[16,24,128]{2,1,0:T(8,128)S(1)} %reduce_sum.36), channel_id=1, replica_groups=mesh['z'=16,'x'=4,'c'=2,'t'=4] {'z'}, dimensions={0} | all-to-all | bytes 393216 | tf_op jit(solution)/shard_map/all_to_all | solution.py:139
  52.8 17.1 %all_to_all.32 = f32[32,1,128]{2,1,0:T(1,128)S(1)} all-to-all(f32[32,1,128]{2,1,0:T(1,128)S(1)} %broadcast_in_dim.6), channel_id=1, replica_groups=mesh['z'=16,'x'=4,'c'=2,'t'=4] {'x','c','t'}, dimensions={0} | all-to-all | bytes 32768 | tf_op jit(solution)/shard_map/all_to_all | solution.py:139
  69.9 15.7 %all_to_all.33.refs_0_ = f32[16,1,128]{2,1,0:T(1,128)S(1)} all-to-all(f32[16,1,128]{2,1,0:T(1,128)S(1)} %broadcast_in_dim.7), channel_id=1, replica_groups=mesh['z'=16,'x'=4,'c'=2,'t'=4] {'z'}, dimensions={0} | all-to-all | bytes 16384 | tf_op jit(solution)/shard_map/all_to_all | solution.py:139
  85.5 0.0 copy-done
  85.5 0.0 copy-done.1
  85.5 0.0 copy-done.2
  85.5 0.0 copy-done.3
  85.6 0.2 update.1
  85.7 14.4 %all_to_all.34 = bf16[16,24,128]{2,1,0:T(8,128)(2,1)S(1)} all-to-all(bf16[16,24,128]{2,1,0:T(8,128)(2,1)S(1)} %get-tuple-element.14), channel_id=1, replica_groups=mesh['z'=16,'x'=4,'c'=2,'t'=4] {'z'}, dimensions={0} | all-to-all | bytes 196608 | tf_op jit(solution)/shard_map/all_to_all | solution.py:139
  100.1 0.8 broadcast_in_dim.8
  100.9 3.5 %all-to-all-start.5 = ((bf16[4,16,24,128]{3,2,1,0:T(8,128)(2,1)}), bf16[4,16,24,128]{3,2,1,0:T(8,128)(2,1)S(1)}, u32[]{:S(2)}, u32[]{:S(2)}) async-start(bf16[4,16,24,128]{3,2,1,0:T(8,128)(2,1)} %broadcast_in_dim.8), calls=%async_computation.5 | async-start | bytes 786432 | tf_op jit(solution)/shard_map/all_to_all | solution.py:139
  104.4 0.6 copy.11
  105.0 0.6 copy.12
  105.6 0.6 copy.13
  106.2 0.6 copy.14
  106.8 3.8 %all-to-all-done.5 = bf16[4,16,24,128]{3,2,1,0:T(8,128)(2,1)S(1)} async-done(((bf16[4,16,24,128]{3,2,1,0:T(8,128)(2,1)}), bf16[4,16,24,128]{3,2,1,0:T(8,128)(2,1)S(1)}, u32[]{:S(2)}, u32[]{:S(2)}) %all-to-all-start.5) | async-done | bytes 393248 | tf_op jit(solution)/shard_map/all_to_all | solution.py:139
  110.6 6.8 %all-gather = bf16[8,16,24,128]{3,2,1,0:T(8,128)(2,1)S(1)} all-gather(bf16[4,16,24,128]{3,2,1,0:T(8,128)(2,1)S(1)} %all-to-all-done.5), channel_id=2, replica_groups=mesh['z'=16,'x'=4,'c'=2,'t'=4] {'c'}, dimensions={0}, use_global_device_ids=true | all-gather | bytes 1179648 | tf_op jit(solution)/shard_map/all_gather | solution.py:174
  117.4 0.9 place.1
  (6 shorter events, 0.1 us)
Async XLA Ops:
  3.4 11.6 %collective-permute-start = (f32[4,16,24,128]{3,2,1,0:T(8,128)S(1)}, f32[4,16,24,128]{3,2,1,0:T(8,128)S(1)}, u32[]{:S(2)}, u32[]{:S(2)}) collective-permute-start(f32[4,16,24,128]{3,2,1,0:T(8,128)S(1)} %other_half.1), channel_id=1, source_target_pairs={{0,4},{4,0},{1,5},{5,1},{2,6},{6,2},{3,7},{7,3},{8,12},{12,8},{9,1... | collective-permute-start | bytes 2359304 | tf_op jit(solution)/shard_map/ppermute | solution.py:154
  14.9 70.6 %copy-start = (f32[12,256]{1,0:T(8,128)S(1)}, f32[12,256]{1,0:T(8,128)}, u32[]{:S(2)}) copy-start(f32[12,256]{1,0:T(8,128)} %refs_2_.1) | copy-start | bytes 36868
  14.9 70.6 %copy-start.1 = (f32[12,256]{1,0:T(8,128)S(1)}, f32[12,256]{1,0:T(8,128)}, u32[]{:S(2)}) copy-start(f32[12,256]{1,0:T(8,128)} %refs_3_.1) | copy-start | bytes 36868
  14.9 70.6 %copy-start.2 = (f32[12,256]{1,0:T(8,128)S(1)}, f32[12,256]{1,0:T(8,128)}, u32[]{:S(2)}) copy-start(f32[12,256]{1,0:T(8,128)} %refs_4_.1) | copy-start | bytes 36868
  15.0 70.6 %copy-start.3 = (f32[12,256]{1,0:T(8,128)S(1)}, f32[12,256]{1,0:T(8,128)}, u32[]{:S(2)}) copy-start(f32[12,256]{1,0:T(8,128)} %refs_5_.1) | copy-start | bytes 36868
  100.9 9.7 %all-to-all-start.5 = ((bf16[4,16,24,128]{3,2,1,0:T(8,128)(2,1)}), bf16[4,16,24,128]{3,2,1,0:T(8,128)(2,1)S(1)}, u32[]{:S(2)}, u32[]{:S(2)}) async-start(bf16[4,16,24,128]{3,2,1,0:T(8,128)(2,1)} %broadcast_in_dim.8), calls=%async_computation.5 | async-start | bytes 786432 | tf_op jit(solution)/shard_map/all_to_all | solution.py:139

commit v13 on v12

--- a/solution.py
+++ b/solution.py
@@ -46,14 +46,12 @@
     return jnp.where(core == 0, zero, one)
 
 
-def half_body(core, g_ref, o_ref):
+def half_body(core, g_refs, o_ref):
     base = pl.program_id(0) * SUM_Z
     for z in range(SUM_Z):
         for x in range(X):
             at = (z * X + x) * GROUP + 8 * core
-            v = g_ref[0, at : at + 16, :].astype(F32)
-            for m in range(1, g_ref.shape[0]):
-                v = v + g_ref[m, at : at + 16, :].astype(F32)
+            v = sum(g_ref[0, at : at + 16, :].astype(F32) for g_ref in g_refs)
             own, both = (v[0:8], v[8:16]) if core == 0 else (v[8:16], v[0:8])
             o = o_ref.at[x, base + z]
             o[0:8] = own[:, :PC]
@@ -61,11 +59,11 @@
             o[16:24] = shared_tile(core, both[:, :PC], both[:, PC:])
 
 
-def half_kernel(own, g_ref, o_ref):
+def half_kernel(own, *refs):
     me = lax.axis_index("c")
     core = me if own else 1 - me
     for k in range(C):
-        pl.when(core == k)(lambda k=k: half_body(k, g_ref, o_ref))
+        pl.when(core == k)(lambda k=k: half_body(k, refs[:-1], refs[-1]))
 
 
 def half_sum(local, own):
@@ -74,11 +72,13 @@
         lambda *refs: half_kernel(own, *refs),
         out_shape=pltpu.VMEM((X, Z, PR, PC), F32),
         grid=(Z // SUM_Z,),
-        in_specs=[pl.BlockSpec((local.shape[0], rows, COLS), lambda i: (0, i, 0))],
+        in_specs=[
+            pl.BlockSpec((1, rows, COLS), lambda i, m=m: (m, i, 0)) for m in range(local.shape[0])
+        ],
         out_specs=pl.BlockSpec(memory_space=pltpu.VMEM),
         cost_estimate=pl.CostEstimate(flops=2_000_000, bytes_accessed=4_000_000, transcendentals=0),
         name="own_half" if own else "other_half",
-    )(local)
+    )(*[local] * local.shape[0])
 
 
 def adam(scale, total, master, moment1, moment2):
@@ -159,13 +159,13 @@
     sq = jnp.sum(exchange(copies(sq, X * C * T), ("x", "c", "t")), axis=0)
     sq = exchange(copies(sq, Z), "z")
 
-    state = pltpu.VMEM((ROWS, COLS), F32)
+    state = jax.ShapeDtypeStruct((ROWS, COLS), F32)
     whole = pl.BlockSpec(memory_space=pltpu.VMEM)
     new_master, new_moment1, new_moment2, new_ema, w = pl.pallas_call(
         lambda *refs: update_kernel(elements, *refs),
         out_shape=(state, state, state, state, pltpu.VMEM((Z, PR, PC), BF16)),
         in_specs=[whole] * 6,
-        out_specs=(whole,) * 5,
+        out_specs=(pl.BlockSpec(),) * 4 + (whole,),
         name="update",
     )(*near(sq, total, master, moment1, moment2, ema))
 

time: 119 us -> 118 us (level)
  blocking collectives: 91.5 us -> 100 us
  waiting for transfers between devices: 3.77 us -> 0.01 us
  starting transfers between devices: 12.2 us -> 8.78 us
  local copies, waits for them, and re-layouts: 3.27 us -> 0.1 us
    all_to_all x5 -> x6, blocking collectives: 84.7 us -> 93.3 us  [exchange(): return lax.all_to_all(v, axes, split_axis=0, concat_axis=0, tiled=True)]
    all_to_all x1 -> x0, waiting for transfers between devices: 3.77 us -> none  [exchange(): return lax.all_to_all(v, axes, split_axis=0, concat_axis=0, tiled=True)]
    all_to_all x1 -> x0, starting transfers between devices: 3.46 us -> none  [exchange(): return lax.all_to_all(v, axes, split_axis=0, concat_axis=0, tiled=True)]
    unnamed x12 -> x8, local copies, waits for them, and re-layouts: 2.45 us -> 0.03 us
  transfers between devices with their start and end apart: 2 -> 1, of which waited for: 1 -> 0; matrix products, arithmetic and copies ran while one was open for 2% -> 0% of each run, Pallas kernels for 2% -> 2%
where the time goes in v13:
time: 118 us; the launch traced here: 117 us
  blocking collectives  100 us (85%)
  starting transfers between devices  8.78 us (7%)
  Pallas kernels  7.31 us (6%)
    all_to_all x6, blocking collectives, exchange(): return lax.all_to_all(v, axes, split_axis=0, concat_axis=0, tiled=True)  93.3 us
    ppermute x1, starting transfers between devices, shards(): other = lax.ppermute(half_sum(local, False), 'c', [(0, 1), (1, 0)])  8.78 us
    all_gather x1, blocking collectives, shards(): w = lax.all_gather(w, 'c', axis=0, tiled=False)  6.77 us
    pallas_call x2, Pallas kernels, half_sum(): pl.pallas_call(lambda *refs: half_kernel(own, *refs), out_shape=pltpu.VME...  5.61 us
  transfers between devices with their start and end apart: 1, of which 0 were waited for; matrix products, arithmetic and copies ran while one was open for 0% of the time, Pallas kernels for 2%

profile of v13, /device:TPU:1, one launch (start us, length us, event | category | flops | bytes accessed | tf_op | source)
XLA Modules:
  0.0 117.2 jit_solution(17798002198062619456)
XLA Ops:
  0.6 2.8 %other_half.1 = f32[4,16,24,128]{3,2,1,0:T(8,128)S(1)} custom-call(bf16[4,1536,256]{2,1,0:T(8,128)(2,1)} %bitcast.4, bf16[4,1536,256]{2,1,0:T(8,128)(2,1)} %bitcast.5, bf16[4,1536,256]{2,1,0:T(8,128)(2,1)} %bitcast.6, bf16[4,1536,256]{2,1,0:T(8,128)(2,1)} %bitcast.7), custom_call_target="tpu_custom_call" | custom-call | flops 2000000 | bytes 4000000 | tf_op jit(solution)/shard_map/other_half/pallas_call | solution.py:71
  3.5 8.8 %collective-permute-start = (f32[4,16,24,128]{3,2,1,0:T(8,128)S(1)}, f32[4,16,24,128]{3,2,1,0:T(8,128)S(1)}, u32[]{:S(2)}, u32[]{:S(2)}) collective-permute-start(f32[4,16,24,128]{3,2,1,0:T(8,128)S(1)} %other_half.1), channel_id=1, source_target_pairs={{0,4},{4,0},{1,5},{5,1},{2,6},{6,2},{3,7},{7,3},{8,12},{12,8},{9,1... | collective-permute-start | bytes 2359304 | tf_op jit(solution)/shard_map/ppermute | solution.py:154
  12.2 2.8 %own_half.1 = f32[4,16,24,128]{3,2,1,0:T(8,128)S(1)} custom-call(bf16[4,1536,256]{2,1,0:T(8,128)(2,1)} %bitcast.8, bf16[4,1536,256]{2,1,0:T(8,128)(2,1)} %bitcast.9, bf16[4,1536,256]{2,1,0:T(8,128)(2,1)} %bitcast.10, bf16[4,1536,256]{2,1,0:T(8,128)(2,1)} %bitcast.11), custom_call_target="tpu_custom_call" | custom-call | flops 2000000 | bytes 4000000 | tf_op jit(solution)/shard_map/own_half/pallas_call | solution.py:71
  15.0 0.0 copy-start
  15.1 0.0 copy-start.1
  15.1 0.0 copy-start.2
  15.1 0.0 copy-start.3
  15.1 0.0 collective-permute-done
  15.1 0.1 add.3
  15.2 14.6 %all_to_all.30 = f32[4,16,24,128]{3,2,1,0:T(8,128)S(1)} all-to-all(f32[4,16,24,128]{3,2,1,0:T(8,128)S(1)} %add.3), channel_id=1, replica_groups=mesh['z'=16,'x'=4,'c'=2,'t'=4] {'x'}, dimensions={0} | all-to-all | bytes 1572864 | tf_op jit(solution)/shard_map/all_to_all | solution.py:139
  29.8 23.1 %all_to_all.31 = f32[16,24,128]{2,1,0:T(8,128)S(1)} all-to-all(f32[16,24,128]{2,1,0:T(8,128)S(1)} %reduce_sum.36), channel_id=1, replica_groups=mesh['z'=16,'x'=4,'c'=2,'t'=4] {'z'}, dimensions={0} | all-to-all | bytes 393216 | tf_op jit(solution)/shard_map/all_to_all | solution.py:139
  52.9 17.1 %all_to_all.32 = f32[32,1,128]{2,1,0:T(1,128)S(1)} all-to-all(f32[32,1,128]{2,1,0:T(1,128)S(1)} %broadcast_in_dim.6), channel_id=1, replica_groups=mesh['z'=16,'x'=4,'c'=2,'t'=4] {'x','c','t'}, dimensions={0} | all-to-all | bytes 32768 | tf_op jit(solution)/shard_map/all_to_all | solution.py:139
  70.0 15.7 %all_to_all.33.refs_0_ = f32[16,1,128]{2,1,0:T(1,128)S(1)} all-to-all(f32[16,1,128]{2,1,0:T(1,128)S(1)} %broadcast_in_dim.7), channel_id=1, replica_groups=mesh['z'=16,'x'=4,'c'=2,'t'=4] {'z'}, dimensions={0} | all-to-all | bytes 16384 | tf_op jit(solution)/shard_map/all_to_all | solution.py:139
  85.7 0.0 copy-done
  85.7 0.0 copy-done.1
  85.7 0.0 copy-done.2
  85.7 0.0 copy-done.3
  85.7 0.8 update.1
  86.5 14.4 %all_to_all.34 = bf16[16,24,128]{2,1,0:T(8,128)(2,1)S(1)} all-to-all(bf16[16,24,128]{2,1,0:T(8,128)(2,1)S(1)} %get-tuple-element.14), channel_id=1, replica_groups=mesh['z'=16,'x'=4,'c'=2,'t'=4] {'z'}, dimensions={0} | all-to-all | bytes 196608 | tf_op jit(solution)/shard_map/all_to_all | solution.py:139
  100.9 0.1 broadcast_in_dim.8
  100.9 8.6 %all_to_all.35 = bf16[4,16,24,128]{3,2,1,0:T(8,128)(2,1)S(1)} all-to-all(bf16[4,16,24,128]{3,2,1,0:T(8,128)(2,1)S(1)} %broadcast_in_dim.8), channel_id=1, replica_groups=mesh['z'=16,'x'=4,'c'=2,'t'=4] {'x'}, dimensions={0} | all-to-all | bytes 786432 | tf_op jit(solution)/shard_map/all_to_all | solution.py:139
  109.5 6.8 %all-gather = bf16[8,16,24,128]{3,2,1,0:T(8,128)(2,1)S(1)} all-gather(bf16[4,16,24,128]{3,2,1,0:T(8,128)(2,1)S(1)} %all_to_all.35), channel_id=2, replica_groups=mesh['z'=16,'x'=4,'c'=2,'t'=4] {'c'}, dimensions={0}, use_global_device_ids=true | all-gather | bytes 1179648 | tf_op jit(solution)/shard_map/all_gather | solution.py:174
  116.3 0.9 place.1
  (6 shorter events, 0.1 us)
Async XLA Ops:
  3.5 11.6 %collective-permute-start = (f32[4,16,24,128]{3,2,1,0:T(8,128)S(1)}, f32[4,16,24,128]{3,2,1,0:T(8,128)S(1)}, u32[]{:S(2)}, u32[]{:S(2)}) collective-permute-start(f32[4,16,24,128]{3,2,1,0:T(8,128)S(1)} %other_half.1), channel_id=1, source_target_pairs={{0,4},{4,0},{1,5},{5,1},{2,6},{6,2},{3,7},{7,3},{8,12},{12,8},{9,1... | collective-permute-start | bytes 2359304 | tf_op jit(solution)/shard_map/ppermute | solution.py:154
  15.0 70.6 %copy-start = (f32[12,256]{1,0:T(8,128)S(1)}, f32[12,256]{1,0:T(8,128)}, u32[]{:S(2)}) copy-start(f32[12,256]{1,0:T(8,128)} %refs_2_.1) | copy-start | bytes 36868
  15.1 70.6 %copy-start.1 = (f32[12,256]{1,0:T(8,128)S(1)}, f32[12,256]{1,0:T(8,128)}, u32[]{:S(2)}) copy-start(f32[12,256]{1,0:T(8,128)} %refs_3_.1) | copy-start | bytes 36868
  15.1 70.6 %copy-start.2 = (f32[12,256]{1,0:T(8,128)S(1)}, f32[12,256]{1,0:T(8,128)}, u32[]{:S(2)}) copy-start(f32[12,256]{1,0:T(8,128)} %refs_4_.1) | copy-start | bytes 36868
  15.1 70.6 %copy-start.3 = (f32[12,256]{1,0:T(8,128)S(1)}, f32[12,256]{1,0:T(8,128)}, u32[]{:S(2)}) copy-start(f32[12,256]{1,0:T(8,128)} %refs_5_.1) | copy-start | bytes 36868

commit v14 on v13

--- a/solution.py
+++ b/solution.py
@@ -22,6 +22,9 @@
 
 F32 = jnp.float32
 BF16 = jnp.bfloat16
+F16 = jnp.float16
+
+LIFT = 32.0
 
 
 def upper():
@@ -153,7 +156,8 @@
 
     other = lax.ppermute(half_sum(local, False), "c", [(0, 1), (1, 0)])
     part = half_sum(local, True) + other
-    part = jnp.sum(exchange(part, "x"), axis=0)
+    part = exchange((part * LIFT).astype(F16), "x")
+    part = jnp.sum(part.astype(F32), axis=0) * (1.0 / LIFT)
     total = jnp.sum(exchange(part, "z"), axis=0)
     sq = jnp.sum(total * total, axis=0, keepdims=True)
     sq = jnp.sum(exchange(copies(sq, X * C * T), ("x", "c", "t")), axis=0)

time: 118 us -> 114 us (0.966)
  blocking collectives: 100 us -> 95.9 us
    all_to_all x6, blocking collectives: 93.3 us -> 89.1 us  [exchange(): return lax.all_to_all(v, axes, split_axis=0, concat_axis=0, tiled=True)]
where the time goes in v14:
time: 114 us; the launch traced here: 113 us
  blocking collectives  95.9 us (84%)
  starting transfers between devices  8.78 us (8%)
  Pallas kernels  7.31 us (6%)
    all_to_all x6, blocking collectives, exchange(): return lax.all_to_all(v, axes, split_axis=0, concat_axis=0, tiled=True)  89.1 us
    ppermute x1, starting transfers between devices, shards(): other = lax.ppermute(half_sum(local, False), 'c', [(0, 1), (1, 0)])  8.78 us
    all_gather x1, blocking collectives, shards(): w = lax.all_gather(w, 'c', axis=0, tiled=False)  6.77 us
    pallas_call x2, Pallas kernels, half_sum(): pl.pallas_call(lambda *refs: half_kernel(own, *refs), out_shape=pltpu.VME...  5.61 us
  transfers between devices with their start and end apart: 1, of which 0 were waited for; matrix products, arithmetic and copies ran while one was open for 0% of the time, Pallas kernels for 2%

profile of v14, /device:TPU:1, one launch (start us, length us, event | category | flops | bytes accessed | tf_op | source)
XLA Modules:
  0.0 113.1 jit_solution(10809918381303057018)
XLA Ops:
  0.6 2.8 %other_half.1 = f32[4,16,24,128]{3,2,1,0:T(8,128)S(1)} custom-call(bf16[4,1536,256]{2,1,0:T(8,128)(2,1)} %bitcast.4, bf16[4,1536,256]{2,1,0:T(8,128)(2,1)} %bitcast.5, bf16[4,1536,256]{2,1,0:T(8,128)(2,1)} %bitcast.6, bf16[4,1536,256]{2,1,0:T(8,128)(2,1)} %bitcast.7), custom_call_target="tpu_custom_call" | custom-call | flops 2000000 | bytes 4000000 | tf_op jit(solution)/shard_map/other_half/pallas_call | solution.py:74
  3.5 8.8 %collective-permute-start = (f32[4,16,24,128]{3,2,1,0:T(8,128)S(1)}, f32[4,16,24,128]{3,2,1,0:T(8,128)S(1)}, u32[]{:S(2)}, u32[]{:S(2)}) collective-permute-start(f32[4,16,24,128]{3,2,1,0:T(8,128)S(1)} %other_half.1), channel_id=1, source_target_pairs={{0,4},{4,0},{1,5},{5,1},{2,6},{6,2},{3,7},{7,3},{8,12},{12,8},{9,1... | collective-permute-start | bytes 2359304 | tf_op jit(solution)/shard_map/ppermute | solution.py:157
  12.2 2.8 %own_half.1 = f32[4,16,24,128]{3,2,1,0:T(8,128)S(1)} custom-call(bf16[4,1536,256]{2,1,0:T(8,128)(2,1)} %bitcast.8, bf16[4,1536,256]{2,1,0:T(8,128)(2,1)} %bitcast.9, bf16[4,1536,256]{2,1,0:T(8,128)(2,1)} %bitcast.10, bf16[4,1536,256]{2,1,0:T(8,128)(2,1)} %bitcast.11), custom_call_target="tpu_custom_call" | custom-call | flops 2000000 | bytes 4000000 | tf_op jit(solution)/shard_map/own_half/pallas_call | solution.py:74
  15.0 0.0 copy-start
  15.1 0.0 copy-start.1
  15.1 0.0 copy-start.2
  15.1 0.0 copy-start.3
  15.1 0.0 collective-permute-done
  15.1 0.1 multiply_convert_fusion
  15.2 10.3 %all_to_all.30 = f16[4,16,24,128]{3,2,1,0:T(8,128)(2,1)S(1)} all-to-all(f16[4,16,24,128]{3,2,1,0:T(8,128)(2,1)S(1)} %multiply_convert_fusion), channel_id=1, replica_groups=mesh['z'=16,'x'=4,'c'=2,'t'=4] {'x'}, dimensions={0} | all-to-all | bytes 786432 | tf_op jit(solution)/shard_map/all_to_all | solution.py:142
  25.6 23.1 %all_to_all.31 = f32[16,24,128]{2,1,0:T(8,128)S(1)} all-to-all(f32[16,24,128]{2,1,0:T(8,128)S(1)} %broadcast_multiply_fusion), channel_id=1, replica_groups=mesh['z'=16,'x'=4,'c'=2,'t'=4] {'z'}, dimensions={0} | all-to-all | bytes 393216 | tf_op jit(solution)/shard_map/all_to_all | solution.py:142
  48.8 17.1 %all_to_all.32 = f32[32,1,128]{2,1,0:T(1,128)S(1)} all-to-all(f32[32,1,128]{2,1,0:T(1,128)S(1)} %broadcast_in_dim.6), channel_id=1, replica_groups=mesh['z'=16,'x'=4,'c'=2,'t'=4] {'x','c','t'}, dimensions={0} | all-to-all | bytes 32768 | tf_op jit(solution)/shard_map/all_to_all | solution.py:142
  65.8 15.7 %all_to_all.33.refs_0_ = f32[16,1,128]{2,1,0:T(1,128)S(1)} all-to-all(f32[16,1,128]{2,1,0:T(1,128)S(1)} %broadcast_in_dim.7), channel_id=1, replica_groups=mesh['z'=16,'x'=4,'c'=2,'t'=4] {'z'}, dimensions={0} | all-to-all | bytes 16384 | tf_op jit(solution)/shard_map/all_to_all | solution.py:142
  81.5 0.0 copy-done
  81.5 0.0 copy-done.1
  81.5 0.0 copy-done.2
  81.5 0.0 copy-done.3
  81.5 0.8 update.1
  82.3 14.4 %all_to_all.34 = bf16[16,24,128]{2,1,0:T(8,128)(2,1)S(1)} all-to-all(bf16[16,24,128]{2,1,0:T(8,128)(2,1)S(1)} %get-tuple-element.14), channel_id=1, replica_groups=mesh['z'=16,'x'=4,'c'=2,'t'=4] {'z'}, dimensions={0} | all-to-all | bytes 196608 | tf_op jit(solution)/shard_map/all_to_all | solution.py:142
  96.7 0.1 broadcast_in_dim.8
  96.8 8.6 %all_to_all.35 = bf16[4,16,24,128]{3,2,1,0:T(8,128)(2,1)S(1)} all-to-all(bf16[4,16,24,128]{3,2,1,0:T(8,128)(2,1)S(1)} %broadcast_in_dim.8), channel_id=1, replica_groups=mesh['z'=16,'x'=4,'c'=2,'t'=4] {'x'}, dimensions={0} | all-to-all | bytes 786432 | tf_op jit(solution)/shard_map/all_to_all | solution.py:142
  105.4 6.8 %all-gather = bf16[8,16,24,128]{3,2,1,0:T(8,128)(2,1)S(1)} all-gather(bf16[4,16,24,128]{3,2,1,0:T(8,128)(2,1)S(1)} %all_to_all.35), channel_id=2, replica_groups=mesh['z'=16,'x'=4,'c'=2,'t'=4] {'c'}, dimensions={0}, use_global_device_ids=true | all-gather | bytes 1179648 | tf_op jit(solution)/shard_map/all_gather | solution.py:178
  112.2 0.9 place.1
  (7 shorter events, 0.1 us)
Async XLA Ops:
  3.5 11.6 %collective-permute-start = (f32[4,16,24,128]{3,2,1,0:T(8,128)S(1)}, f32[4,16,24,128]{3,2,1,0:T(8,128)S(1)}, u32[]{:S(2)}, u32[]{:S(2)}) collective-permute-start(f32[4,16,24,128]{3,2,1,0:T(8,128)S(1)} %other_half.1), channel_id=1, source_target_pairs={{0,4},{4,0},{1,5},{5,1},{2,6},{6,2},{3,7},{7,3},{8,12},{12,8},{9,1... | collective-permute-start | bytes 2359304 | tf_op jit(solution)/shard_map/ppermute | solution.py:157
  15.0 66.5 %copy-start = (f32[12,256]{1,0:T(8,128)S(1)}, f32[12,256]{1,0:T(8,128)}, u32[]{:S(2)}) copy-start(f32[12,256]{1,0:T(8,128)} %refs_2_.1) | copy-start | bytes 36868
  15.1 66.5 %copy-start.1 = (f32[12,256]{1,0:T(8,128)S(1)}, f32[12,256]{1,0:T(8,128)}, u32[]{:S(2)}) copy-start(f32[12,256]{1,0:T(8,128)} %refs_3_.1) | copy-start | bytes 36868
  15.1 66.4 %copy-start.2 = (f32[12,256]{1,0:T(8,128)S(1)}, f32[12,256]{1,0:T(8,128)}, u32[]{:S(2)}) copy-start(f32[12,256]{1,0:T(8,128)} %refs_4_.1) | copy-start | bytes 36868
  15.1 66.4 %copy-start.3 = (f32[12,256]{1,0:T(8,128)S(1)}, f32[12,256]{1,0:T(8,128)}, u32[]{:S(2)}) copy-start(f32[12,256]{1,0:T(8,128)} %refs_5_.1) | copy-start | bytes 36868

commit v15 on v11

--- a/solution.py
+++ b/solution.py
@@ -22,6 +22,9 @@
 
 F32 = jnp.float32
 BF16 = jnp.bfloat16
+F16 = jnp.float16
+
+LIFT = 32.0
 
 
 def upper():
@@ -46,8 +49,9 @@
     return jnp.where(core == 0, zero, one)
 
 
-def sum_kernel(g_ref, o_ref):
+def sum_body(me, g_ref, own_ref, other_ref):
     base = pl.program_id(0) * SUM_Z
+    refs = (own_ref, other_ref) if me == 0 else (other_ref, own_ref)
     for z in range(SUM_Z):
         for pair in range(X // 2):
             at = (z * X + 2 * pair) * GROUP
@@ -56,21 +60,27 @@
                 v = v + g_ref[m, at : at + 2 * GROUP, :].astype(F32)
             for k in range(2):
                 first, both, last = [v[k * GROUP + j : k * GROUP + j + 8] for j in (0, 8, 16)]
-                for core, own in ((0, first), (1, last)):
-                    o = o_ref.at[core, 2 * pair + k, base + z]
-                    o[0:8] = own[:, :PC]
-                    o[8:16] = own[:, PC:]
+                for core, owned in ((0, first), (1, last)):
+                    o = refs[core].at[2 * pair + k, base + z]
+                    o[0:8] = owned[:, :PC]
+                    o[8:16] = owned[:, PC:]
                     o[16:24] = shared_tile(core, both[:, :PC], both[:, PC:])
+
+
+def sum_kernel(*refs):
+    me = lax.axis_index("c")
+    for k in range(C):
+        pl.when(me == k)(lambda k=k: sum_body(k, *refs))
 
 
 def micro_sum(local):
     rows = SUM_Z * X * GROUP
     return pl.pallas_call(
         sum_kernel,
-        out_shape=pltpu.VMEM((C, X, Z, PR, PC), F32),
+        out_shape=(pltpu.VMEM((X, Z, PR, PC), F32),) * 2,
         grid=(Z // SUM_Z,),
         in_specs=[pl.BlockSpec((local.shape[0], rows, COLS), lambda i: (0, i, 0))],
-        out_specs=pl.BlockSpec(memory_space=pltpu.VMEM),
+        out_specs=(pl.BlockSpec(memory_space=pltpu.VMEM),) * 2,
         name="micro_sum",
     )(local)
 
@@ -145,21 +155,22 @@
     local = grads[0]
     elements = local.shape[1] * local.shape[2] * T
 
-    part = micro_sum(local)
-    part = jnp.sum(exchange(part, "c"), axis=0)
-    part = jnp.sum(exchange(part, "x"), axis=0)
+    part, other = micro_sum(local)
+    part = part + lax.ppermute(other, "c", [(0, 1), (1, 0)])
+    part = exchange((part * LIFT).astype(F16), "x")
+    part = jnp.sum(part.astype(F32), axis=0) * (1.0 / LIFT)
     total = jnp.sum(exchange(part, "z"), axis=0)
-    sq = jnp.sum((total * total).reshape(-1, 8, PC), axis=0)
+    sq = jnp.sum(total * total, axis=0, keepdims=True)
     sq = jnp.sum(exchange(copies(sq, X * C * T), ("x", "c", "t")), axis=0)
     sq = exchange(copies(sq, Z), "z")
 
-    state = pltpu.VMEM((ROWS, COLS), F32)
+    state = jax.ShapeDtypeStruct((ROWS, COLS), F32)
     whole = pl.BlockSpec(memory_space=pltpu.VMEM)
     new_master, new_moment1, new_moment2, new_ema, w = pl.pallas_call(
         lambda *refs: update_kernel(elements, *refs),
         out_shape=(state, state, state, state, pltpu.VMEM((Z, PR, PC), BF16)),
         in_specs=[whole] * 6,
-        out_specs=(whole,) * 5,
+        out_specs=(pl.BlockSpec(),) * 4 + (whole,),
         name="update",
     )(*near(sq, total, master, moment1, moment2, ema))
 

time: 120 us -> 112 us (0.933)
  blocking collectives: 104 us -> 95.2 us
  starting transfers between devices: 3.46 us -> 8.8 us
  local copies, waits for them, and re-layouts: 3.26 us -> 0.09 us
  waiting for transfers between devices: 3.77 us -> 1.89 us
    all_to_all x6, blocking collectives: 97.8 us -> 88.4 us  [exchange(): return lax.all_to_all(v, axes, split_axis=0, concat_axis=0, tiled=True)]
    ppermute x0 -> x1, starting transfers between devices: none -> 8.8 us  [shards(): part = part + lax.ppermute(other, 'c', [(0, 1), (1, 0)])]
    all_to_all x1 -> x0, waiting for transfers between devices: 3.77 us -> none  [exchange(): return lax.all_to_all(v, axes, split_axis=0, concat_axis=0, tiled=True)]
    all_to_all x1 -> x0, starting transfers between devices: 3.46 us -> none  [exchange(): return lax.all_to_all(v, axes, split_axis=0, concat_axis=0, tiled=True)]
    unnamed x12 -> x8, local copies, waits for them, and re-layouts: 2.45 us -> 0.02 us
    ppermute x0 -> x1, waiting for transfers between devices: none -> 1.89 us  [shards(): part = part + lax.ppermute(other, 'c', [(0, 1), (1, 0)])]
  transfers between devices with their start and end apart: 1 -> 1, of which waited for: 1 -> 1; matrix products, arithmetic and copies ran while one was open for 2% -> 0% of each run, Pallas kernels for 0% -> 0%
where the time goes in v15:
time: 112 us; the launch traced here: 111 us
  blocking collectives  95.2 us (85%)
  starting transfers between devices  8.8 us (8%)
  Pallas kernels  4.51 us (4%)
  waiting for transfers between devices  1.89 us (2%)
    all_to_all x6, blocking collectives, exchange(): return lax.all_to_all(v, axes, split_axis=0, concat_axis=0, tiled=True)  88.4 us
    ppermute x1, starting transfers between devices, shards(): part = part + lax.ppermute(other, 'c', [(0, 1), (1, 0)])  8.8 us
    all_gather x1, blocking collectives, shards(): w = lax.all_gather(w, 'c', axis=0, tiled=False)  6.77 us
    pallas_call x1, Pallas kernels, micro_sum(): pl.pallas_call(sum_kernel, out_shape=(pltpu.VMEM((X, Z, PR, PC), F32),) *...  2.81 us
  transfers between devices with their start and end apart: 1, of which 1 were waited for; matrix products, arithmetic and copies ran while one was open for 0% of the time, Pallas kernels for 0%

profile of v15, /device:TPU:1, one launch (start us, length us, event | category | flops | bytes accessed | tf_op | source)
XLA Modules:
  0.0 111.4 jit_solution(5929737952260275996)
XLA Ops:
  0.6 0.0 copy-start
  0.6 0.0 copy-start.1
  0.7 0.0 copy-start.2
  0.7 0.0 copy-start.3
  0.7 2.8 %micro_sum.1 = (f32[4,16,24,128]{3,2,1,0:T(8,128)S(1)}, f32[4,16,24,128]{3,2,1,0:T(8,128)S(1)}) custom-call(bf16[4,1536,256]{2,1,0:T(8,128)(2,1)} %bitcast.4), custom_call_target="tpu_custom_call" | custom-call | tf_op jit(solution)/shard_map/micro_sum/pallas_call | solution.py:78
  3.5 8.8 %collective-permute-start = (f32[4,16,24,128]{3,2,1,0:T(8,128)S(1)}, f32[4,16,24,128]{3,2,1,0:T(8,128)S(1)}, u32[]{:S(2)}, u32[]{:S(2)}) collective-permute-start(f32[4,16,24,128]{3,2,1,0:T(8,128)S(1)} %get-tuple-element.13), channel_id=1, source_target_pairs={{0,4},{4,0},{1,5},{5,1},{2,6},{6,2},{3,7},{7,3},{8,12},{12,8},{9,1... | collective-permute-start | bytes 2359304 | tf_op jit(solution)/shard_map/ppermute | solution.py:159
  12.3 1.9 %collective-permute-done = f32[4,16,24,128]{3,2,1,0:T(8,128)S(1)} collective-permute-done((f32[4,16,24,128]{3,2,1,0:T(8,128)S(1)}, f32[4,16,24,128]{3,2,1,0:T(8,128)S(1)}, u32[]{:S(2)}, u32[]{:S(2)}) %collective-permute-start) | collective-permute-done | bytes 786464 | tf_op jit(solution)/shard_map/ppermute | solution.py:159
  14.2 0.1 multiply_convert_fusion
  14.3 10.2 %all_to_all.30 = f16[4,16,24,128]{3,2,1,0:T(8,128)(2,1)S(1)} all-to-all(f16[4,16,24,128]{3,2,1,0:T(8,128)(2,1)S(1)} %multiply_convert_fusion), channel_id=1, replica_groups=mesh['z'=16,'x'=4,'c'=2,'t'=4] {'x'}, dimensions={0} | all-to-all | bytes 786432 | tf_op jit(solution)/shard_map/all_to_all | solution.py:143
  24.6 22.5 %all_to_all.31 = f32[16,24,128]{2,1,0:T(8,128)S(1)} all-to-all(f32[16,24,128]{2,1,0:T(8,128)S(1)} %broadcast_multiply_fusion), channel_id=1, replica_groups=mesh['z'=16,'x'=4,'c'=2,'t'=4] {'z'}, dimensions={0} | all-to-all | bytes 393216 | tf_op jit(solution)/shard_map/all_to_all | solution.py:143
  47.1 17.3 %all_to_all.32 = f32[32,1,128]{2,1,0:T(1,128)S(1)} all-to-all(f32[32,1,128]{2,1,0:T(1,128)S(1)} %broadcast_in_dim.6), channel_id=1, replica_groups=mesh['z'=16,'x'=4,'c'=2,'t'=4] {'x','c','t'}, dimensions={0} | all-to-all | bytes 32768 | tf_op jit(solution)/shard_map/all_to_all | solution.py:143
  64.5 15.4 %all_to_all.33.refs_0_ = f32[16,1,128]{2,1,0:T(1,128)S(1)} all-to-all(f32[16,1,128]{2,1,0:T(1,128)S(1)} %broadcast_in_dim.7), channel_id=1, replica_groups=mesh['z'=16,'x'=4,'c'=2,'t'=4] {'z'}, dimensions={0} | all-to-all | bytes 16384 | tf_op jit(solution)/shard_map/all_to_all | solution.py:143
  79.9 0.0 copy-done
  79.9 0.0 copy-done.1
  79.9 0.0 copy-done.2
  79.9 0.0 copy-done.3
  79.9 0.8 update.1
  80.7 14.4 %all_to_all.34 = bf16[16,24,128]{2,1,0:T(8,128)(2,1)S(1)} all-to-all(bf16[16,24,128]{2,1,0:T(8,128)(2,1)S(1)} %get-tuple-element.18), channel_id=1, replica_groups=mesh['z'=16,'x'=4,'c'=2,'t'=4] {'z'}, dimensions={0} | all-to-all | bytes 196608 | tf_op jit(solution)/shard_map/all_to_all | solution.py:143
  95.1 0.1 broadcast_in_dim.8
  95.1 8.6 %all_to_all.35 = bf16[4,16,24,128]{3,2,1,0:T(8,128)(2,1)S(1)} all-to-all(bf16[4,16,24,128]{3,2,1,0:T(8,128)(2,1)S(1)} %broadcast_in_dim.8), channel_id=1, replica_groups=mesh['z'=16,'x'=4,'c'=2,'t'=4] {'x'}, dimensions={0} | all-to-all | bytes 786432 | tf_op jit(solution)/shard_map/all_to_all | solution.py:143
  103.8 6.8 %all-gather = bf16[8,16,24,128]{3,2,1,0:T(8,128)(2,1)S(1)} all-gather(bf16[4,16,24,128]{3,2,1,0:T(8,128)(2,1)S(1)} %all_to_all.35), channel_id=2, replica_groups=mesh['z'=16,'x'=4,'c'=2,'t'=4] {'c'}, dimensions={0}, use_global_device_ids=true | all-gather | bytes 1179648 | tf_op jit(solution)/shard_map/all_gather | solution.py:179
  110.5 0.9 place.1
  (7 shorter events, 0.1 us)
Async XLA Ops:
  0.6 79.3 %copy-start = (f32[12,256]{1,0:T(8,128)S(1)}, f32[12,256]{1,0:T(8,128)}, u32[]{:S(2)}) copy-start(f32[12,256]{1,0:T(8,128)} %refs_2_.1) | copy-start | bytes 36868
  0.6 79.3 %copy-start.1 = (f32[12,256]{1,0:T(8,128)S(1)}, f32[12,256]{1,0:T(8,128)}, u32[]{:S(2)}) copy-start(f32[12,256]{1,0:T(8,128)} %refs_3_.1) | copy-start | bytes 36868
  0.7 79.3 %copy-start.2 = (f32[12,256]{1,0:T(8,128)S(1)}, f32[12,256]{1,0:T(8,128)}, u32[]{:S(2)}) copy-start(f32[12,256]{1,0:T(8,128)} %refs_4_.1) | copy-start | bytes 36868
  0.7 79.2 %copy-start.3 = (f32[12,256]{1,0:T(8,128)S(1)}, f32[12,256]{1,0:T(8,128)}, u32[]{:S(2)}) copy-start(f32[12,256]{1,0:T(8,128)} %refs_5_.1) | copy-start | bytes 36868
  3.5 10.7 %collective-permute-start = (f32[4,16,24,128]{3,2,1,0:T(8,128)S(1)}, f32[4,16,24,128]{3,2,1,0:T(8,128)S(1)}, u32[]{:S(2)}, u32[]{:S(2)}) collective-permute-start(f32[4,16,24,128]{3,2,1,0:T(8,128)S(1)} %get-tuple-element.13), channel_id=1, source_target_pairs={{0,4},{4,0},{1,5},{5,1},{2,6},{6,2},{3,7},{7,3},{8,12},{12,8},{9,1... | collective-permute-start | bytes 2359304 | tf_op jit(solution)/shard_map/ppermute | solution.py:159

commit v16 on v15

--- a/solution.py
+++ b/solution.py
@@ -18,7 +18,7 @@
 GROUP = C * ROWS
 STEPS = 2
 NZ = Z // STEPS
-SUM_Z = 4
+SUM_Z = 8
 
 F32 = jnp.float32
 BF16 = jnp.bfloat16

time: 112 us -> 111 us (level)
  no operation moved by 1% of the time
where the time goes in v16:
time: 111 us
  blocking collectives  95.2 us (86%)
  starting transfers between devices  8.79 us (8%)
  Pallas kernels  3.82 us (3%)
  waiting for transfers between devices  1.89 us (2%)
    all_to_all x6, blocking collectives, exchange(): return lax.all_to_all(v, axes, split_axis=0, concat_axis=0, tiled=True)  88.4 us
    ppermute x1, starting transfers between devices, shards(): part = part + lax.ppermute(other, 'c', [(0, 1), (1, 0)])  8.79 us
    all_gather x1, blocking collectives, shards(): w = lax.all_gather(w, 'c', axis=0, tiled=False)  6.77 us
  transfers between devices with their start and end apart: 1, of which 1 were waited for; matrix products, arithmetic and copies ran while one was open for 0% of the time, Pallas kernels for 0%

profile of v16, /device:TPU:1, one launch (start us, length us, event | category | flops | bytes accessed | tf_op | source)
XLA Modules:
  0.0 110.8 jit_solution(9031231007338956376)
XLA Ops:
  0.6 0.0 copy-start
  0.6 0.0 copy-start.1
  0.7 0.0 copy-start.2
  0.7 0.0 copy-start.3
  0.7 2.1 %micro_sum.1 = (f32[4,16,24,128]{3,2,1,0:T(8,128)S(1)}, f32[4,16,24,128]{3,2,1,0:T(8,128)S(1)}) custom-call(bf16[4,1536,256]{2,1,0:T(8,128)(2,1)} %bitcast.4), custom_call_target="tpu_custom_call" | custom-call | tf_op jit(solution)/shard_map/micro_sum/pallas_call | solution.py:78
  2.8 8.8 %collective-permute-start = (f32[4,16,24,128]{3,2,1,0:T(8,128)S(1)}, f32[4,16,24,128]{3,2,1,0:T(8,128)S(1)}, u32[]{:S(2)}, u32[]{:S(2)}) collective-permute-start(f32[4,16,24,128]{3,2,1,0:T(8,128)S(1)} %get-tuple-element.13), channel_id=1, source_target_pairs={{0,4},{4,0},{1,5},{5,1},{2,6},{6,2},{3,7},{7,3},{8,12},{12,8},{9,1... | collective-permute-start | bytes 2359304 | tf_op jit(solution)/shard_map/ppermute | solution.py:159
  11.6 1.9 %collective-permute-done = f32[4,16,24,128]{3,2,1,0:T(8,128)S(1)} collective-permute-done((f32[4,16,24,128]{3,2,1,0:T(8,128)S(1)}, f32[4,16,24,128]{3,2,1,0:T(8,128)S(1)}, u32[]{:S(2)}, u32[]{:S(2)}) %collective-permute-start) | collective-permute-done | bytes 786464 | tf_op jit(solution)/shard_map/ppermute | solution.py:159
  13.5 0.1 multiply_convert_fusion
  13.6 10.2 %all_to_all.30 = f16[4,16,24,128]{3,2,1,0:T(8,128)(2,1)S(1)} all-to-all(f16[4,16,24,128]{3,2,1,0:T(8,128)(2,1)S(1)} %multiply_convert_fusion), channel_id=1, replica_groups=mesh['z'=16,'x'=4,'c'=2,'t'=4] {'x'}, dimensions={0} | all-to-all | bytes 786432 | tf_op jit(solution)/shard_map/all_to_all | solution.py:143
  23.9 22.5 %all_to_all.31 = f32[16,24,128]{2,1,0:T(8,128)S(1)} all-to-all(f32[16,24,128]{2,1,0:T(8,128)S(1)} %broadcast_multiply_fusion), channel_id=1, replica_groups=mesh['z'=16,'x'=4,'c'=2,'t'=4] {'z'}, dimensions={0} | all-to-all | bytes 393216 | tf_op jit(solution)/shard_map/all_to_all | solution.py:143
  46.4 17.3 %all_to_all.32 = f32[32,1,128]{2,1,0:T(1,128)S(1)} all-to-all(f32[32,1,128]{2,1,0:T(1,128)S(1)} %broadcast_in_dim.6), channel_id=1, replica_groups=mesh['z'=16,'x'=4,'c'=2,'t'=4] {'x','c','t'}, dimensions={0} | all-to-all | bytes 32768 | tf_op jit(solution)/shard_map/all_to_all | solution.py:143
  63.8 15.4 %all_to_all.33.refs_0_ = f32[16,1,128]{2,1,0:T(1,128)S(1)} all-to-all(f32[16,1,128]{2,1,0:T(1,128)S(1)} %broadcast_in_dim.7), channel_id=1, replica_groups=mesh['z'=16,'x'=4,'c'=2,'t'=4] {'z'}, dimensions={0} | all-to-all | bytes 16384 | tf_op jit(solution)/shard_map/all_to_all | solution.py:143
  79.2 0.0 copy-done
  79.2 0.0 copy-done.1
  79.2 0.0 copy-done.2
  79.2 0.0 copy-done.3
  79.2 0.8 update.1
  80.0 14.4 %all_to_all.34 = bf16[16,24,128]{2,1,0:T(8,128)(2,1)S(1)} all-to-all(bf16[16,24,128]{2,1,0:T(8,128)(2,1)S(1)} %get-tuple-element.18), channel_id=1, replica_groups=mesh['z'=16,'x'=4,'c'=2,'t'=4] {'z'}, dimensions={0} | all-to-all | bytes 196608 | tf_op jit(solution)/shard_map/all_to_all | solution.py:143
  94.4 0.1 broadcast_in_dim.8
  94.5 8.6 %all_to_all.35 = bf16[4,16,24,128]{3,2,1,0:T(8,128)(2,1)S(1)} all-to-all(bf16[4,16,24,128]{3,2,1,0:T(8,128)(2,1)S(1)} %broadcast_in_dim.8), channel_id=1, replica_groups=mesh['z'=16,'x'=4,'c'=2,'t'=4] {'x'}, dimensions={0} | all-to-all | bytes 786432 | tf_op jit(solution)/shard_map/all_to_all | solution.py:143
  103.1 6.8 %all-gather = bf16[8,16,24,128]{3,2,1,0:T(8,128)(2,1)S(1)} all-gather(bf16[4,16,24,128]{3,2,1,0:T(8,128)(2,1)S(1)} %all_to_all.35), channel_id=2, replica_groups=mesh['z'=16,'x'=4,'c'=2,'t'=4] {'c'}, dimensions={0}, use_global_device_ids=true | all-gather | bytes 1179648 | tf_op jit(solution)/shard_map/all_gather | solution.py:179
  109.8 0.9 place.1
  (7 shorter events, 0.1 us)
Async XLA Ops:
  0.6 78.6 %copy-start = (f32[12,256]{1,0:T(8,128)S(1)}, f32[12,256]{1,0:T(8,128)}, u32[]{:S(2)}) copy-start(f32[12,256]{1,0:T(8,128)} %refs_2_.1) | copy-start | bytes 36868
  0.6 78.6 %copy-start.1 = (f32[12,256]{1,0:T(8,128)S(1)}, f32[12,256]{1,0:T(8,128)}, u32[]{:S(2)}) copy-start(f32[12,256]{1,0:T(8,128)} %refs_3_.1) | copy-start | bytes 36868
  0.7 78.6 %copy-start.2 = (f32[12,256]{1,0:T(8,128)S(1)}, f32[12,256]{1,0:T(8,128)}, u32[]{:S(2)}) copy-start(f32[12,256]{1,0:T(8,128)} %refs_4_.1) | copy-start | bytes 36868
  0.7 78.6 %copy-start.3 = (f32[12,256]{1,0:T(8,128)S(1)}, f32[12,256]{1,0:T(8,128)}, u32[]{:S(2)}) copy-start(f32[12,256]{1,0:T(8,128)} %refs_5_.1) | copy-start | bytes 36868
  2.8 10.7 %collective-permute-start = (f32[4,16,24,128]{3,2,1,0:T(8,128)S(1)}, f32[4,16,24,128]{3,2,1,0:T(8,128)S(1)}, u32[]{:S(2)}, u32[]{:S(2)}) collective-permute-start(f32[4,16,24,128]{3,2,1,0:T(8,128)S(1)} %get-tuple-element.13), channel_id=1, source_target_pairs={{0,4},{4,0},{1,5},{5,1},{2,6},{6,2},{3,7},{7,3},{8,12},{12,8},{9,1... | collective-permute-start | bytes 2359304 | tf_op jit(solution)/shard_map/ppermute | solution.py:159

commit v17 on v16

--- a/solution.py
+++ b/solution.py
@@ -18,7 +18,7 @@
 GROUP = C * ROWS
 STEPS = 2
 NZ = Z // STEPS
-SUM_Z = 8
+SUM_Z = 16
 
 F32 = jnp.float32
 BF16 = jnp.bfloat16

time: 111 us -> 111 us (level)
  no operation moved by 1% of the time
where the time goes in v17:
time: 111 us
  blocking collectives  95.2 us (86%)
  starting transfers between devices  8.79 us (8%)
  Pallas kernels  3.99 us (4%)
  waiting for transfers between devices  1.89 us (2%)
    all_to_all x6, blocking collectives, exchange(): return lax.all_to_all(v, axes, split_axis=0, concat_axis=0, tiled=True)  88.4 us
    ppermute x1, starting transfers between devices, shards(): part = part + lax.ppermute(other, 'c', [(0, 1), (1, 0)])  8.79 us
    all_gather x1, blocking collectives, shards(): w = lax.all_gather(w, 'c', axis=0, tiled=False)  6.77 us
    pallas_call x1, Pallas kernels, micro_sum(): pl.pallas_call(sum_kernel, out_shape=(pltpu.VMEM((X, Z, PR, PC), F32),) *...  2.3 us
  transfers between devices with their start and end apart: 1, of which 1 were waited for; matrix products, arithmetic and copies ran while one was open for 0% of the time, Pallas kernels for 0%

profile of v17, /device:TPU:1, one launch (start us, length us, event | category | flops | bytes accessed | tf_op | source)
XLA Modules:
  0.0 110.9 jit_solution(13142514207197232585)
XLA Ops:
  0.6 0.0 copy-start
  0.6 0.0 copy-start.1
  0.7 0.0 copy-start.2
  0.7 0.0 copy-start.3
  0.7 2.3 %micro_sum.1 = (f32[4,16,24,128]{3,2,1,0:T(8,128)S(1)}, f32[4,16,24,128]{3,2,1,0:T(8,128)S(1)}) custom-call(bf16[4,1536,256]{2,1,0:T(8,128)(2,1)} %bitcast.4), custom_call_target="tpu_custom_call" | custom-call | tf_op jit(solution)/shard_map/micro_sum/pallas_call | solution.py:78
  3.0 8.8 %collective-permute-start = (f32[4,16,24,128]{3,2,1,0:T(8,128)S(1)}, f32[4,16,24,128]{3,2,1,0:T(8,128)S(1)}, u32[]{:S(2)}, u32[]{:S(2)}) collective-permute-start(f32[4,16,24,128]{3,2,1,0:T(8,128)S(1)} %get-tuple-element.13), channel_id=1, source_target_pairs={{0,4},{4,0},{1,5},{5,1},{2,6},{6,2},{3,7},{7,3},{8,12},{12,8},{9,1... | collective-permute-start | bytes 2359304 | tf_op jit(solution)/shard_map/ppermute | solution.py:159
  11.8 1.9 %collective-permute-done = f32[4,16,24,128]{3,2,1,0:T(8,128)S(1)} collective-permute-done((f32[4,16,24,128]{3,2,1,0:T(8,128)S(1)}, f32[4,16,24,128]{3,2,1,0:T(8,128)S(1)}, u32[]{:S(2)}, u32[]{:S(2)}) %collective-permute-start) | collective-permute-done | bytes 786464 | tf_op jit(solution)/shard_map/ppermute | solution.py:159
  13.7 0.1 multiply_convert_fusion
  13.8 10.2 %all_to_all.30 = f16[4,16,24,128]{3,2,1,0:T(8,128)(2,1)S(1)} all-to-all(f16[4,16,24,128]{3,2,1,0:T(8,128)(2,1)S(1)} %multiply_convert_fusion), channel_id=1, replica_groups=mesh['z'=16,'x'=4,'c'=2,'t'=4] {'x'}, dimensions={0} | all-to-all | bytes 786432 | tf_op jit(solution)/shard_map/all_to_all | solution.py:143
  24.1 22.5 %all_to_all.31 = f32[16,24,128]{2,1,0:T(8,128)S(1)} all-to-all(f32[16,24,128]{2,1,0:T(8,128)S(1)} %broadcast_multiply_fusion), channel_id=1, replica_groups=mesh['z'=16,'x'=4,'c'=2,'t'=4] {'z'}, dimensions={0} | all-to-all | bytes 393216 | tf_op jit(solution)/shard_map/all_to_all | solution.py:143
  46.6 17.3 %all_to_all.32 = f32[32,1,128]{2,1,0:T(1,128)S(1)} all-to-all(f32[32,1,128]{2,1,0:T(1,128)S(1)} %broadcast_in_dim.6), channel_id=1, replica_groups=mesh['z'=16,'x'=4,'c'=2,'t'=4] {'x','c','t'}, dimensions={0} | all-to-all | bytes 32768 | tf_op jit(solution)/shard_map/all_to_all | solution.py:143
  63.9 15.4 %all_to_all.33.refs_0_ = f32[16,1,128]{2,1,0:T(1,128)S(1)} all-to-all(f32[16,1,128]{2,1,0:T(1,128)S(1)} %broadcast_in_dim.7), channel_id=1, replica_groups=mesh['z'=16,'x'=4,'c'=2,'t'=4] {'z'}, dimensions={0} | all-to-all | bytes 16384 | tf_op jit(solution)/shard_map/all_to_all | solution.py:143
  79.4 0.0 copy-done
  79.4 0.0 copy-done.1
  79.4 0.0 copy-done.2
  79.4 0.0 copy-done.3
  79.4 0.8 update.1
  80.2 14.4 %all_to_all.34 = bf16[16,24,128]{2,1,0:T(8,128)(2,1)S(1)} all-to-all(bf16[16,24,128]{2,1,0:T(8,128)(2,1)S(1)} %get-tuple-element.18), channel_id=1, replica_groups=mesh['z'=16,'x'=4,'c'=2,'t'=4] {'z'}, dimensions={0} | all-to-all | bytes 196608 | tf_op jit(solution)/shard_map/all_to_all | solution.py:143
  94.6 0.1 broadcast_in_dim.8
  94.6 8.6 %all_to_all.35 = bf16[4,16,24,128]{3,2,1,0:T(8,128)(2,1)S(1)} all-to-all(bf16[4,16,24,128]{3,2,1,0:T(8,128)(2,1)S(1)} %broadcast_in_dim.8), channel_id=1, replica_groups=mesh['z'=16,'x'=4,'c'=2,'t'=4] {'x'}, dimensions={0} | all-to-all | bytes 786432 | tf_op jit(solution)/shard_map/all_to_all | solution.py:143
  103.2 6.8 %all-gather = bf16[8,16,24,128]{3,2,1,0:T(8,128)(2,1)S(1)} all-gather(bf16[4,16,24,128]{3,2,1,0:T(8,128)(2,1)S(1)} %all_to_all.35), channel_id=2, replica_groups=mesh['z'=16,'x'=4,'c'=2,'t'=4] {'c'}, dimensions={0}, use_global_device_ids=true | all-gather | bytes 1179648 | tf_op jit(solution)/shard_map/all_gather | solution.py:179
  110.0 0.9 place.1
  (7 shorter events, 0.1 us)
Async XLA Ops:
  0.6 78.7 %copy-start = (f32[12,256]{1,0:T(8,128)S(1)}, f32[12,256]{1,0:T(8,128)}, u32[]{:S(2)}) copy-start(f32[12,256]{1,0:T(8,128)} %refs_2_.1) | copy-start | bytes 36868
  0.6 78.7 %copy-start.1 = (f32[12,256]{1,0:T(8,128)S(1)}, f32[12,256]{1,0:T(8,128)}, u32[]{:S(2)}) copy-start(f32[12,256]{1,0:T(8,128)} %refs_3_.1) | copy-start | bytes 36868
  0.7 78.7 %copy-start.2 = (f32[12,256]{1,0:T(8,128)S(1)}, f32[12,256]{1,0:T(8,128)}, u32[]{:S(2)}) copy-start(f32[12,256]{1,0:T(8,128)} %refs_4_.1) | copy-start | bytes 36868
  0.7 78.7 %copy-start.3 = (f32[12,256]{1,0:T(8,128)S(1)}, f32[12,256]{1,0:T(8,128)}, u32[]{:S(2)}) copy-start(f32[12,256]{1,0:T(8,128)} %refs_5_.1) | copy-start | bytes 36868
  3.0 10.7 %collective-permute-start = (f32[4,16,24,128]{3,2,1,0:T(8,128)S(1)}, f32[4,16,24,128]{3,2,1,0:T(8,128)S(1)}, u32[]{:S(2)}, u32[]{:S(2)}) collective-permute-start(f32[4,16,24,128]{3,2,1,0:T(8,128)S(1)} %get-tuple-element.13), channel_id=1, source_target_pairs={{0,4},{4,0},{1,5},{5,1},{2,6},{6,2},{3,7},{7,3},{8,12},{12,8},{9,1... | collective-permute-start | bytes 2359304 | tf_op jit(solution)/shard_map/ppermute | solution.py:159
